TPU v7x, 32 devices: a whole 2x2x4 slice. The times are simulated.
32 devices in a mesh: ctx: 8 (over y, x, core), fsdp: 4 (over z).
Axes of the slice: x: 2, y: 2, z: 4, core: 2. Of those that a mesh axis runs over, the one named last changes fastest.
Arguments:
- block_input: bfloat16 [2, 4, 512, 1536], P(None, 'fsdp', 'ctx'), may hold values from -6 to 6
- positions: int32 [2, 4, 512], P(None, 'fsdp', 'ctx'), may hold values from 0 to 511, as said below
- segments: int32 [2, 4, 512], P(None, 'fsdp', 'ctx'), may hold values from 0 to 2, as said below
- out_cotangent: bfloat16 [2, 4, 512, 1536], P(None, 'fsdp', 'ctx'), may hold values from -6 to 6
- attn_gain: bfloat16 [1536], P(('ctx', 'fsdp')), may hold values from 0.5 to 1.5
- w_query: bfloat16 [1536, 1536], P(('ctx', 'fsdp')), may hold values from -0.15625 to 0.15625
- w_key: bfloat16 [1536, 768], P(('ctx', 'fsdp')), may hold values from -0.15625 to 0.15625
- w_value: bfloat16 [1536, 768], P(('ctx', 'fsdp')), may hold values from -0.15625 to 0.15625
- w_out: bfloat16 [1536, 1536], P(('ctx', 'fsdp')), may hold values from -0.625 to 0.625
- mlp_gain: bfloat16 [1536], P(('ctx', 'fsdp')), may hold values from 0.5 to 1.5
- w_gate: bfloat16 [1536, 4096], P(('ctx', 'fsdp')), may hold values from -0.15625 to 0.15625
- w_up: bfloat16 [1536, 4096], P(('ctx', 'fsdp')), may hold values from -0.15625 to 0.15625
- w_down: bfloat16 [4096, 1536], P(('ctx', 'fsdp')), may hold values from -0.09375 to 0.09375
Outputs:
- block_output: bfloat16 [2, 4, 512, 1536], P(None, 'fsdp', 'ctx')
- input_grad: bfloat16 [2, 4, 512, 1536], P(None, 'fsdp', 'ctx')
- grad_attn_gain: float32 [1536], P(('ctx', 'fsdp'))
- grad_query: float32 [1536, 1536], P(('ctx', 'fsdp'))
- grad_key: float32 [1536, 768], P(('ctx', 'fsdp'))
- grad_value: float32 [1536, 768], P(('ctx', 'fsdp'))
- grad_out: float32 [1536, 1536], P(('ctx', 'fsdp'))
- grad_mlp_gain: float32 [1536], P(('ctx', 'fsdp'))
- grad_gate: float32 [1536, 4096], P(('ctx', 'fsdp'))
- grad_up: float32 [1536, 4096], P(('ctx', 'fsdp'))
- grad_down: float32 [4096, 1536], P(('ctx', 'fsdp'))
Inputs may be any that keep to these rules, and one draw needn't show every extreme that they name: In each sequence every position appears once; the 64 tokens of one index of ctx are 32 consecutive positions starting at c * 32 followed by 32 starting at (15 - c) * 32, for some c below 8. `segments`: ordered by position, segment ids start at 0 and rise by one at each new document, except that the last document of each sequence has the id 512 // 200; every document has 200 to 2000 positions except that the last of a sequence may have fewer.
All inputs are finite; a program needn't handle non-finite values.
Results may differ from a plain program's by a relative error of at most 0.02.
Values may be sent and summed in bfloat16 or wider, within the bound.
No kernel may reach another device: no remote copies, remote signals or barrier semaphores. Data moves between devices by JAX's collectives and lax.ppermute only.
A program may use at most 192 MiB of HBM per device.

v0:
```python
import math

import jax
import jax.numpy as jnp
from jax import lax
from jax.sharding import Mesh, PartitionSpec as P

HEADS = 16
KV_HEADS = 8
HEAD = 96
EPS = 1e-05
THETA = 100000.0
f32 = jnp.float32
bf16 = jnp.bfloat16


def rope_tables(position_ids):
    half = HEAD // 2
    ladder = jnp.arange(half).astype(f32) * (2.0 / HEAD)
    inverse = jnp.exp(-math.log(THETA) * ladder)
    angles = position_ids.astype(f32)[:, None] * inverse[None, :]
    return jnp.cos(angles)[:, None, :], jnp.sin(angles)[:, None, :]


def rotate(vectors, cosine, sine):
    half = HEAD // 2
    a, b = vectors[..., :half], vectors[..., half:]
    return jnp.concatenate([a * cosine - b * sine, b * cosine + a * sine], axis=-1)


def unrotate(grads, cosine, sine):
    half = HEAD // 2
    a, b = grads[..., :half], grads[..., half:]
    return jnp.concatenate([a * cosine + b * sine, b * cosine - a * sine], axis=-1)


def rms_scale(values):
    return lax.rsqrt(jnp.mean(values * values, axis=-1, keepdims=True) + EPS)


def norm_back(grad, normed, scale):
    return scale * (grad - normed * jnp.mean(grad * normed, axis=-1, keepdims=True))


def mm(a, b):
    return jnp.dot(a, b, preferred_element_type=f32)


def mm_tn(a, b):
    return jnp.einsum("td,te->de", a, b, preferred_element_type=f32)


def mm_nt(a, b):
    return jnp.einsum("te,de->td", a, b, preferred_element_type=f32)


def on_device(
    block_input,
    positions,
    segments,
    out_cotangent,
    attn_gain,
    w_query,
    w_key,
    w_value,
    w_out,
    mlp_gain,
    w_gate,
    w_up,
    w_down,
):
    chips = lax.axis_size("chip")
    rows_z = lax.axis_size("fsdp")
    chip = lax.axis_index("chip")
    core = lax.axis_index("core")
    place = lax.axis_index("fsdp")
    tok = block_input.shape[2]
    width = block_input.shape[3]
    d_rows = w_query.shape[0]
    q_cols = w_query.shape[1] // chips
    kv_cols = w_key.shape[1] // chips
    ff_cols = w_gate.shape[1] // (2 * chips)
    kv_heads = KV_HEADS // chips
    factor = HEAD ** (-0.5)

    def core_swap(a):
        return lax.ppermute(a, "core", [(0, 1), (1, 0)])

    def chip_xor(a, j):
        return lax.ppermute(a, "chip", [(i, i ^ j) for i in range(chips)])

    def pick(a, index, axis=0):
        return lax.dynamic_index_in_dim(a, index, axis, keepdims=False)

    def gather_chips(a, axis=0):
        return jnp.concatenate([a] + [chip_xor(a, j) for j in range(1, chips)], axis=axis)

    def scatter_chips(a):
        step = a.shape[0] // chips
        total = a[:step]
        for j in range(1, chips):
            total = total + chip_xor(a[j * step : (j + 1) * step].astype(bf16), j).astype(f32)
        return total

    def by_chip(pieces):
        stacked = jnp.stack(pieces)
        bit = 1
        while bit < chips:
            view = stacked.reshape((chips // (2 * bit), 2, bit) + stacked.shape[1:])
            flipped = jnp.flip(view, axis=1)
            stacked = jnp.where((chip & bit) != 0, flipped, view).reshape(stacked.shape)
            bit *= 2
        return stacked

    def exchange_chips(pack):
        pieces = [pick(pack, chip)]
        for j in range(1, chips):
            pieces.append(chip_xor(pick(pack, chip ^ j), j))
        return by_chip(pieces)

    def core_pair(mine, other, axis):
        first = core == 0
        return jnp.stack([jnp.where(first, mine, other), jnp.where(first, other, mine)], axis)

    def both_cores(a):
        return core_pair(a, core_swap(a), 0)

    def chip_slices(weights, cols):
        return jnp.stack(
            [
                jnp.concatenate([w[:, k * n : (k + 1) * n] for w, n in zip(weights, cols)], axis=1)
                for k in range(chips)
            ]
        )

    def tie(*values):
        return lax.optimization_barrier(values)

    def along_z(a, step):
        return lax.ppermute(a, "fsdp", [(i, (i + step) % rows_z) for i in range(rows_z)])

    def ring_first(a):
        return along_z(a, 1), along_z(a, -1)

    def ring_rest(a, right, left):
        found = [(a, 0, 0), (right, -1, 0), (left, 1, 0)]
        for step in range(2, rows_z // 2 + 1):
            if 2 * step == rows_z:
                half = a.shape[-1] // 2
                found.append((along_z(right[..., :half], 1), -step, 0))
                found.append((along_z(left[..., half:], -1), step, half))
            else:
                right, left = along_z(right, 1), along_z(left, -1)
                found += [(right, -step, 0), (left, step, 0)]
        return found

    def assemble(found, groups):
        rows, cols = found[0][0].shape
        whole = jnp.zeros((groups, rows_z, rows // groups, cols), bf16)
        for piece, offset, column in found:
            piece = piece.reshape(groups, 1, rows // groups, piece.shape[-1])
            index = lax.rem(place + offset + rows_z, rows_z)
            whole = lax.dynamic_update_slice(whole, piece, (0, index, 0, column))
        return whole

    def again(found, pieces):
        return [(piece,) + f[1:] for piece, f in zip(pieces, found)]

    def pieces_of(found):
        return [f[0] for f in found]

    def scaled(gain, *weights):
        return [(w.astype(f32) * gain.astype(f32)[:, None]).astype(bf16) for w in weights]

    pack_qkv = chip_slices(
        scaled(attn_gain, w_query, w_key, w_value), (q_cols, kv_cols, kv_cols)
    )
    piece_qkv = exchange_chips(pack_qkv).reshape(-1, pack_qkv.shape[-1])
    marks = jnp.stack([positions[:, 0] // 32, positions[:, 0] % 32, segments[:, 0]], axis=-1)
    marks = jnp.pad(marks.astype(bf16), ((0, 0), (0, 0), (0, 125)))
    pair = jnp.concatenate([out_cotangent[:, 0], block_input[:, 0], marks], axis=-1)
    pair = jnp.concatenate([pick(pair, core), core_swap(pick(pair, 1 - core))])
    lower, upper = w_down[: w_down.shape[0] // 2], w_down[w_down.shape[0] // 2 :]
    rows = jnp.concatenate([w_out, lower])
    gate_up = scaled(mlp_gain, w_gate, w_up)
    pack_gu = jnp.stack(
        [
            jnp.concatenate([w[:, n * ff_cols : (n + 1) * ff_cols] for w in gate_up], axis=1)
            for n in range(2 * chips)
        ]
    ).reshape(chips, 2, d_rows, 2 * ff_cols)
    pair, piece_qkv, pack_gu = tie(pair, piece_qkv, pack_gu)
    dy_low, x_low = pair[:, :width], pair[:, width:]

    qkv_right, qkv_left = ring_first(piece_qkv)
    piece_gu = exchange_chips(pack_gu)
    qkv_right, qkv_left, piece_gu, x_low, rows = tie(qkv_right, qkv_left, piece_gu, x_low, rows)
    rows = lax.all_gather(rows, "fsdp", axis=0)

    near = [j for j in range(1, chips) if j & (j - 1) == 0]
    far = [j for j in range(1, chips) if j & (j - 1) != 0]
    x_parts = {0: x_low, **{j: chip_xor(x_low, j) for j in near}}
    found_qkv = ring_rest(piece_qkv, qkv_right, qkv_left)
    piece_gu = core_pair(pick(piece_gu, core, 1), core_swap(pick(piece_gu, 1 - core, 1)), 1)
    piece_gu = piece_gu.reshape(2 * chips * d_rows, 2 * ff_cols)
    order = sorted(x_parts)
    piece_gu, *late = tie(piece_gu, *[x_parts[j] for j in order], *pieces_of(found_qkv))
    x_parts = dict(zip(order, late))
    x_parts.update({j: chip_xor(x_low, j) for j in far})
    x_all = jnp.concatenate([x_parts[j] for j in range(chips)])
    found_qkv = again(found_qkv, late[len(order) :])
    marks = x_all[:, width : width + 3].astype(f32).T
    pos_all, seg_all = marks[0] * 32.0 + marks[1], marks[2]
    x_all, x_low = x_all[:, :width], x_low[:, :width]
    allowed = (seg_all[:, None] == seg_all[None, :]) & (pos_all[None, :] <= pos_all[:, None])
    cosine, sine = rope_tables(pos_all)
    w_qkv = assemble(found_qkv, chips)
    w_qkv = core_pair(w_qkv, core_swap(w_qkv), 1).reshape(width, -1)
    w_qkv, x_all, dy_low, cosine, sine, allowed = tie(w_qkv, x_all, dy_low, cosine, sine, allowed)
    own = x_low.shape[0]
    seq = x_all.shape[0]

    dy_all = gather_chips(dy_low)
    x_full = x_all.astype(f32)
    h_one = (x_full * rms_scale(x_full)).astype(bf16)
    qkv = mm(h_one, w_qkv)
    q_rot = rotate(qkv[:, :q_cols].reshape(seq, kv_heads * 2, HEAD), cosine, sine)
    q_rot = q_rot.astype(bf16).reshape(seq, kv_heads, 2, HEAD)
    k_rot = rotate(
        qkv[:, q_cols : q_cols + kv_cols].reshape(seq, kv_heads, HEAD), cosine, sine
    ).astype(bf16)
    value = qkv[:, q_cols + kv_cols :].astype(bf16).reshape(seq, kv_heads, HEAD)
    q_rot, rows = tie(q_rot, rows)
    along_out = rows[:, : w_out.shape[0]].reshape(-1, width)
    out_w = both_cores(along_out).reshape(-1, width)
    scores = jnp.einsum("sgrh,tgh->grst", q_rot, k_rot, preferred_element_type=f32) * factor
    scores = jnp.where(allowed, scores, -1e30)
    raised = jnp.exp(scores - jnp.max(scores, axis=-1, keepdims=True))
    soft = raised / jnp.sum(raised, axis=-1, keepdims=True)
    soft_low = soft.astype(bf16)
    mixed = jnp.einsum("grst,tgh->sgrh", soft_low, value, preferred_element_type=f32)
    mixed = mixed.astype(bf16).reshape(seq, q_cols)
    mixed, dy_all, out_w = tie(mixed, dy_all, out_w)
    x_own = x_low.astype(f32)
    middle = x_own + scatter_chips(mm(mixed, out_w))

    dy_both = jnp.concatenate([dy_all, core_swap(dy_all)])
    along_gu = lax.all_gather(piece_gu, "fsdp", axis=0, tiled=True)
    middle, dy_both = tie(middle, dy_both)
    scale_two = rms_scale(middle)
    n_two = middle * scale_two
    h_two = gather_chips(n_two.astype(bf16))
    h_two, upper = tie(h_two, upper)
    upper_right, upper_left = ring_first(upper)
    h_both, along_gu, upper_right, upper_left = tie(
        jnp.concatenate([h_two, core_swap(h_two)]), along_gu, upper_right, upper_left
    )
    along_upper = assemble(ring_rest(upper, upper_right, upper_left), 1)[0]
    along_down = jnp.concatenate([rows[:, w_out.shape[0] :], along_upper], axis=1)
    along_down = along_down.reshape(-1, width)
    w_gu = along_gu.reshape(rows_z, 2 * chips, d_rows, 2 * ff_cols)
    w_gu = jnp.transpose(w_gu, (1, 0, 2, 3)).reshape(width, 2 * ff_cols)
    gu = mm(h_both, w_gu)
    gate, up = gu[:, :ff_cols], gu[:, ff_cols:]
    sigma = jax.nn.sigmoid(gate)
    act = (gate * sigma * up).astype(bf16)
    d_act = mm_nt(dy_both, along_down)
    d_gate = (d_act * up * sigma * (1.0 + gate * (1.0 - sigma))).astype(bf16)
    d_up = (d_act * gate * sigma).astype(bf16)
    d_gu = jnp.concatenate([d_gate, d_up], axis=1)
    g_down = mm_tn(act, dy_both).astype(bf16)
    g_down, d_gu = tie(g_down, d_gu)
    g_down = lax.psum_scatter(g_down, "fsdp", scatter_dimension=0, tiled=True)

    def give_partial(rows, weights, product):
        other = core_swap(product(rows[seq:], weights).astype(bf16)).astype(f32)
        return product(rows[:seq], weights) + other

    d_h_two, act = tie(give_partial(d_gu, w_gu, mm_nt), act)
    g_gu = mm_tn(h_both, d_gu).astype(bf16).reshape(2 * chips, rows_z, d_rows, 2 * ff_cols)
    g_gu = jnp.transpose(g_gu, (1, 0, 2, 3)).reshape(width, 2 * ff_cols)
    d_h_two, g_gu = tie(scatter_chips(d_h_two), g_gu)
    g_gu = lax.psum_scatter(g_gu, "fsdp", scatter_dimension=0, tiled=True)

    dy_own = dy_low.astype(f32)
    d_middle = dy_own + norm_back(d_h_two, n_two, scale_two)
    branch = gather_chips(d_middle.astype(bf16))
    partial = give_partial(act, along_down, mm)
    kept, given = partial[:own], partial[own:].astype(bf16)
    branch, kept, given, g_down = tie(branch, kept, given, g_down)

    g_out = mm_tn(mixed, branch).astype(bf16)
    g_out = g_out.reshape(2, g_out.shape[0] // 2, g_out.shape[1])
    g_out = pick(g_out, core) + core_swap(pick(g_out, 1 - core))
    d_mixed = mm_nt(branch, out_w).astype(bf16).reshape(seq, kv_heads, 2, HEAD)
    d_soft = jnp.einsum("sgrh,tgh->grst", d_mixed, value, preferred_element_type=f32)
    d_value = jnp.einsum("grst,sgrh->tgh", soft_low, d_mixed, preferred_element_type=f32)
    inner = jnp.sum(soft * d_soft, axis=-1, keepdims=True)
    d_scores = (soft * (d_soft - inner)).astype(bf16)
    d_q = jnp.einsum("grst,tgh->sgrh", d_scores, k_rot, preferred_element_type=f32) * factor
    d_k = jnp.einsum("grst,sgrh->tgh", d_scores, q_rot, preferred_element_type=f32) * factor
    d_q = unrotate(d_q.reshape(seq, kv_heads * 2, HEAD), cosine, sine)
    d_k = unrotate(d_k, cosine, sine)
    d_qkv = jnp.concatenate(
        [
            d_q.reshape(seq, q_cols).astype(bf16),
            d_k.reshape(seq, kv_cols).astype(bf16),
            d_value.reshape(seq, kv_cols).astype(bf16),
        ],
        axis=1,
    )
    d_qkv, g_out = tie(d_qkv, g_out)
    cols_qkv = d_qkv.shape[1]
    g_qkv = mm_tn(h_one, d_qkv).astype(bf16).reshape(chips, 2, rows_z, d_rows, cols_qkv)
    g_qkv = pick(g_qkv, core, 1) + core_swap(pick(g_qkv, 1 - core, 1))
    g_qkv = jnp.transpose(g_qkv, (1, 0, 2, 3)).reshape(1, rows_z, chips * d_rows, cols_qkv)
    folds = width // cols_qkv
    g_out = g_out.reshape(1, rows_z, d_rows, width)
    g_rest = [g_out[..., k * cols_qkv : (k + 1) * cols_qkv] for k in range(folds)]
    g_rest = jnp.concatenate([g_qkv] + g_rest, axis=2)
    d_h_one = mm_nt(d_qkv, w_qkv)
    g_rest, d_h_one = tie(g_rest.reshape(-1, cols_qkv), d_h_one)
    g_rest = lax.psum_scatter(g_rest, "fsdp", scatter_dimension=0, tiled=True)
    d_h_one, given, g_gu = tie(scatter_chips(d_h_one), given, g_gu)
    result = middle + kept
    for j in range(1, chips):
        result = result + chip_xor(given[(j - 1) * own : j * own], j).astype(f32)
    g_gu = g_gu.reshape(chips, 2, d_rows, 2 * ff_cols)
    g_gu = core_pair(pick(g_gu, core, 1), core_swap(pick(g_gu, 1 - core, 1)), 1)
    g_gu = exchange_chips(g_gu)
    def spread_ff(grad):
        grad = jnp.transpose(grad.astype(f32), (2, 0, 1, 3))
        return grad.reshape(d_rows, 2 * chips * ff_cols)

    g_gate, g_up = spread_ff(g_gu[..., :ff_cols]), spread_ff(g_gu[..., ff_cols:])

    def of_gain(grads, weights):
        return sum(jnp.sum(g * w.astype(f32), axis=1) for g, w in zip(grads, weights))

    def by_gain(gain, grads):
        return [g * gain.astype(f32)[:, None] for g in grads]

    g_mlp_gain = of_gain((g_gate, g_up), (w_gate, w_up))
    g_gate, g_up = by_gain(mlp_gain, (g_gate, g_up))
    result, g_rest, g_gate, g_up, g_mlp_gain = tie(
        result.astype(bf16), g_rest, g_gate, g_up, g_mlp_gain
    )
    scale_one = rms_scale(x_own)
    n_one = x_own * scale_one
    d_input = (d_middle + norm_back(d_h_one, n_one, scale_one)).astype(bf16)

    def give_back(a):
        mine, theirs = a[:tok], core_swap(a[tok:])
        first = core == 0
        return jnp.stack([jnp.where(first, mine, theirs), jnp.where(first, theirs, mine)])[:, None]

    def spread(grad, start, cols):
        part = grad[:, :, start : start + cols].astype(f32)
        return jnp.transpose(part, (1, 0, 2)).reshape(d_rows, chips * cols)

    g_down = g_down.astype(f32)
    result, d_input = give_back(result), give_back(d_input)
    g_rest, g_gate, g_up, g_down, g_mlp_gain, result, d_input = tie(
        g_rest, g_gate, g_up, g_down, g_mlp_gain, result, d_input
    )
    g_qkv = exchange_chips(g_rest[: chips * d_rows].reshape(chips, d_rows, cols_qkv))
    g_out = g_rest[chips * d_rows :].reshape(folds, d_rows, cols_qkv)
    g_out = jnp.transpose(g_out, (1, 0, 2)).reshape(d_rows, width).astype(f32)
    g_query = spread(g_qkv, 0, q_cols)
    g_key = spread(g_qkv, q_cols, kv_cols)
    g_value = spread(g_qkv, q_cols + kv_cols, kv_cols)
    g_attn_gain = of_gain((g_query, g_key, g_value), (w_query, w_key, w_value))
    g_query, g_key, g_value = by_gain(attn_gain, (g_query, g_key, g_value))
    return (
        result,
        d_input,
        g_attn_gain,
        g_query,
        g_key,
        g_value,
        g_out,
        g_mlp_gain,
        g_gate,
        g_up,
        g_down,
    )


def solution(mesh):
    ctx, fsdp = mesh.shape["ctx"], mesh.shape["fsdp"]
    split = Mesh(mesh.devices.reshape(ctx // 2, 2, fsdp), ("chip", "core", "fsdp"))
    ctx_axes = ("chip", "core")
    all_axes = ("chip", "core", "fsdp")
    tokens = P(None, "fsdp", ctx_axes, None)
    marks = P(None, "fsdp", ctx_axes)
    vector, matrix = P(all_axes), P(all_axes, None)
    return jax.shard_map(
        on_device,
        mesh=split,
        in_specs=(
            tokens, marks, marks, tokens, vector, matrix, matrix, matrix, matrix,
            vector, matrix, matrix, matrix,
        ),
        out_specs=(
            tokens, tokens, vector, matrix, matrix, matrix, matrix, vector,
            matrix, matrix, matrix,
        ),
        check_vma=False,
    )
```

profile of v0, /device:TPU:0, one launch (start us, length us, event | category | flops | bytes accessed | tf_op | source)
XLA Modules:
  0.0 353.3 jit_solution(17350886094072629340)
XLA Ops:
  10.6 4.0 %collective-permute-start.3 = (bf16[48,768]{1,0:T(8,128)(2,1)S(1)}, bf16[48,768]{1,0:T(8,128)(2,1)S(1)}, u32[]{:S(2)}, u32[]{:S(2)}) collective-permute-start(bf16[48,768]{1,0:T(8,128)(2,1)S(1)} %get-tuple-element.262), channel_id=1, source_target_pairs={{0,24},{8,16},{16,8},{24,0},{1,25},{9,17},{17,9},{25,1},{2,26},{10... | collective-permute-start | bytes 221192 | tf_op jit(solution)/shard_map/ppermute | solution.py:90
  17.0 2.0 collective-permute-done.2
  25.7 3.6 %collective-permute-start.5 = (bf16[192,768]{1,0:T(8,128)(2,1)S(1)}, bf16[192,768]{1,0:T(8,128)(2,1)S(1)}, u32[]{:S(2)}, u32[]{:S(2)}) collective-permute-start(bf16[192,768]{1,0:T(8,128)(2,1)S(1)} %bitcast.379), channel_id=1, source_target_pairs={{0,3},{1,0},{2,1},{3,2},{4,7},{5,4},{6,5},{7,6},{8,11},{9,8},{10,9... | collective-permute-start | bytes 884744 | tf_op jit(solution)/shard_map/ppermute | solution.py:140
  30.3 2.1 collective-permute-done.7
  33.0 3.7 %collective-permute-done.5 = bf16[192,768]{1,0:T(8,128)(2,1)S(1)} collective-permute-done((bf16[192,768]{1,0:T(8,128)(2,1)S(1)}, bf16[192,768]{1,0:T(8,128)(2,1)S(1)}, u32[]{:S(2)}, u32[]{:S(2)}) %collective-permute-start.5) | collective-permute-done | bytes 294944 | tf_op jit(solution)/shard_map/ppermute | solution.py:140
  36.7 4.2 %collective-permute-done.4 = bf16[192,768]{1,0:T(8,128)(2,1)S(1)} collective-permute-done((bf16[192,768]{1,0:T(8,128)(2,1)S(1)}, bf16[192,768]{1,0:T(8,128)(2,1)S(1)}, u32[]{:S(2)}, u32[]{:S(2)}) %collective-permute-start.4) | collective-permute-done | bytes 294944 | tf_op jit(solution)/shard_map/ppermute | solution.py:140
  45.5 1.8 collective-permute-start.13
  49.7 4.5 %collective-permute-done.13 = bf16[192,384]{1,0:T(8,128)(2,1)S(1)} collective-permute-done((bf16[192,384]{1,0:T(8,128)(2,1)S(1)}, bf16[192,384]{1,0:T(8,128)(2,1)S(1)}, u32[]{:S(2)}, u32[]{:S(2)}) %collective-permute-start.13) | collective-permute-done | bytes 147488 | tf_op jit(solution)/shard_map/ppermute | solution.py:140
  54.2 5.0 %collective-permute-done.12 = bf16[192,384]{1,0:T(8,128)(2,1)S(1)} collective-permute-done((bf16[192,384]{1,0:T(8,128)(2,1)S(1)}, bf16[192,384]{1,0:T(8,128)(2,1)S(1)}, u32[]{:S(2)}, u32[]{:S(2)}) %collective-permute-start.12) | collective-permute-done | bytes 147488 | tf_op jit(solution)/shard_map/ppermute | solution.py:140
  83.8 3.6 %collective-permute-done.18 = bf16[128,1536]{1,0:T(8,128)(2,1)S(1)} collective-permute-done((bf16[128,1536]{1,0:T(8,128)(2,1)S(1)}, bf16[128,1536]{1,0:T(8,128)(2,1)S(1)}, u32[]{:S(2)}, u32[]{:S(2)}) %collective-permute-start.18) | collective-permute-done | bytes 393248 | tf_op jit(solution)/shard_map/ppermute | solution.py:90
  87.4 7.9 %collective-permute-done.17 = bf16[128,1536]{1,0:T(8,128)(2,1)} collective-permute-done((bf16[128,1536]{1,0:T(8,128)(2,1)S(1)}, bf16[128,1536]{1,0:T(8,128)(2,1)}, u32[]{:S(2)}, u32[]{:S(2)}) %collective-permute-start.17) | collective-permute-done | bytes 393248 | tf_op jit(solution)/shard_map/ppermute | solution.py:90
  95.3 2.4 pad_maximum_fusion.5
  98.9 3.7 %fusion.98 = (f32[2,2,512]{2,1,0:T(2,128)S(1)}, f32[2,2,512,512]{2,3,1,0:T(8,128)}) fusion(pred[512,512]{0,1:T(8,128)(4,1)S(1)} %copy-done.48, bf16[512,2,2,96]{0,3,2,1:T(8,128)(2,1)S(1)} %pad_maximum_fusion.15, bf16[512,2,48]{0,2,1:T(8,128)(2,1)S(1)} %get-tuple-element.232, bf16[512,2,48]{0,2,1:T(8,128)(2,1)S(1)} %get-tuple-element.231), kind=kOutput, calls=%fused_computation.284 | convolution fusion | flops 205914624 | bytes 5054464 | tf_op jit(solution)/shard_map/sub | solution.py:238
  102.6 2.7 convolution_convert_fusion.6
  110.7 8.5 %collective-permute-done.20 = bf16[128,1536]{1,0:T(8,128)(2,1)S(1)} collective-permute-done((bf16[128,1536]{1,0:T(8,128)(2,1)S(1)}, bf16[128,1536]{1,0:T(8,128)(2,1)S(1)}, u32[]{:S(2)}, u32[]{:S(2)}) %collective-permute-start.20) | collective-permute-done | bytes 393248 | tf_op jit(solution)/shard_map/ppermute | solution.py:90
  119.2 8.7 %collective-permute-done.22 = bf16[128,1536]{1,0:T(8,128)(2,1)S(1)} collective-permute-done((bf16[128,1536]{1,0:T(8,128)(2,1)S(1)}, bf16[128,1536]{1,0:T(8,128)(2,1)S(1)}, u32[]{:S(2)}, u32[]{:S(2)}) %collective-permute-start.22) | collective-permute-done | bytes 393248 | tf_op jit(solution)/shard_map/ppermute | solution.py:90
  129.7 3.3 pad_maximum_fusion
  136.8 9.4 %collective-permute-done.26 = bf16[128,1536]{1,0:T(8,128)(2,1)S(1)} collective-permute-done((bf16[128,1536]{1,0:T(8,128)(2,1)S(1)}, bf16[128,1536]{1,0:T(8,128)(2,1)S(1)}, u32[]{:S(2)}, u32[]{:S(2)}) %collective-permute-start.26) | collective-permute-done | bytes 393248 | tf_op jit(solution)/shard_map/ppermute | solution.py:90
  146.2 6.5 %collective-permute-done.25 = bf16[128,1536]{1,0:T(8,128)(2,1)S(1)} collective-permute-done((bf16[128,1536]{1,0:T(8,128)(2,1)S(1)}, bf16[128,1536]{1,0:T(8,128)(2,1)S(1)}, u32[]{:S(2)}, u32[]{:S(2)}) %collective-permute-start.25) | collective-permute-done | bytes 393248 | tf_op jit(solution)/shard_map/ppermute | solution.py:90
  153.0 3.2 collective-permute-start.29
  156.3 1.8 pad_maximum_fusion.1
  158.2 3.4 collective-permute-done.29
  162.2 6.3 %collective-permute-done.28 = bf16[64,1536]{1,0:T(8,128)(2,1)} collective-permute-done((bf16[64,1536]{1,0:T(8,128)(2,1)S(1)}, bf16[64,1536]{1,0:T(8,128)(2,1)}, u32[]{:S(2)}, u32[]{:S(2)}) %collective-permute-start.28) | collective-permute-done | bytes 196640 | tf_op jit(solution)/shard_map/ppermute | solution.py:140
  170.5 2.4 copy.75
  175.4 3.6 %fusion.100 = f32[1024,1024]{0,1:T(8,128)S(1)} fusion(bf16[1024,1536]{1,0:T(8,128)(2,1)S(1)} %copy-done.8, bf16[1536,1024]{1,0:T(8,128)(2,1)S(1)} %bitcast.337), kind=kOutput, calls=%fused_computation.286 | convolution fusion | flops 3221225472 | bytes 10485760 | tf_op jit(solution)/shard_map/dot_general | solution.py:46
  179.0 1.8 collective-permute-done.30
  181.0 3.6 %multiply_convert_fusion.1 = (bf16[1024,512]{0,1:T(8,128)(2,1)S(1)}, bf16[1024,512]{0,1:T(8,128)(2,1)}, bf16[1024,512]{0,1:T(8,128)(2,1)S(1)}) fusion(f32[1024,1024]{0,1:T(8,128)S(1)} %fusion.100, bf16[1024,1536]{1,0:T(8,128)(2,1)S(1)} %copy-done.7, bf16[512,1536]{1,0:T(8,128)(2,1)S(1)} %bitcast.330), kind=kOutput, calls=%fused_computation.27 | convolution fusion | flops 1619001344 | bytes 12058624 | tf_op jit(solution)/shard_map/te,de->td/dot_general | solution.py:54
  185.6 3.0 convolution_convert_fusion.4
  190.8 3.0 convolution_convert_fusion.3
  193.8 3.5 %collective-permute-done.32 = bf16[512,1536]{1,0:T(8,128)(2,1)S(1)} collective-permute-done((bf16[512,1536]{1,0:T(8,128)(2,1)}, bf16[512,1536]{1,0:T(8,128)(2,1)S(1)}, u32[]{:S(2)}, u32[]{:S(2)}) %collective-permute-start.32) | collective-permute-done | bytes 1572896 | tf_op jit(solution)/shard_map/ppermute | solution.py:87
  197.4 4.1 %convert_add_fusion.1 = f32[512,1536]{1,0:T(8,128)S(1)} fusion(bf16[512,1536]{1,0:T(8,128)(2,1)S(1)} %collective-permute-done.32, bf16[1536,1024]{1,0:T(8,128)(2,1)} %bitcast.338, bf16[1024,1024]{0,1:T(8,128)(2,1)} %copy-done.17), kind=kOutput, calls=%fused_computation.18 | convolution fusion | flops 1612185600 | bytes 8912896 | tf_op jit(solution)/shard_map/te,de->td/dot_general | solution.py:54
  205.3 3.8 %convolution_convert_fusion = bf16[1536,1024]{1,0:T(8,128)(2,1)S(1)} fusion(bf16[1024,1536]{1,0:T(8,128)(2,1)S(1)} %copy-done.9, bf16[1024,1024]{0,1:T(8,128)(2,1)S(1)} %copy-done.18), kind=kOutput, calls=%fused_computation.10 | convolution fusion | flops 3222798336 | bytes 8388608 | tf_op jit(solution)/shard_map/td,te->de/dot_general | solution.py:50
  209.1 2.0 copy.76
  211.8 2.2 convolution_convert_fusion.2
  214.0 7.5 %collective-permute-done.35 = bf16[128,1536]{1,0:T(8,128)(2,1)S(1)} collective-permute-done((bf16[128,1536]{1,0:T(8,128)(2,1)S(1)}, bf16[128,1536]{1,0:T(8,128)(2,1)S(1)}, u32[]{:S(2)}, u32[]{:S(2)}) %collective-permute-start.35) | collective-permute-done | bytes 393248 | tf_op jit(solution)/shard_map/ppermute | solution.py:90
  227.4 9.1 %collective-permute-done.38 = bf16[128,1536]{1,0:T(8,128)(2,1)S(1)} collective-permute-done((bf16[128,1536]{1,0:T(8,128)(2,1)S(1)}, bf16[128,1536]{1,0:T(8,128)(2,1)S(1)}, u32[]{:S(2)}, u32[]{:S(2)}) %collective-permute-start.38) | collective-permute-done | bytes 393248 | tf_op jit(solution)/shard_map/ppermute | solution.py:90
  236.5 5.4 %collective-permute-done.37 = bf16[128,1536]{1,0:T(8,128)(2,1)} collective-permute-done((bf16[128,1536]{1,0:T(8,128)(2,1)S(1)}, bf16[128,1536]{1,0:T(8,128)(2,1)}, u32[]{:S(2)}, u32[]{:S(2)}) %collective-permute-start.37) | collective-permute-done | bytes 393248 | tf_op jit(solution)/shard_map/ppermute | solution.py:90
  241.9 2.4 pad_maximum_fusion.8
  244.3 2.5 convert_add_fusion
  248.9 2.7 convolution_convert_fusion.7
  263.1 3.1 fusion.101
  267.7 2.1 convert.86
  275.1 7.8 %collective-permute-done.42 = bf16[128,1536]{1,0:T(8,128)(2,1)} collective-permute-done((bf16[128,1536]{1,0:T(8,128)(2,1)}, bf16[128,1536]{1,0:T(8,128)(2,1)}, u32[]{:S(2)}, u32[]{:S(2)}) %collective-permute-start.42) | collective-permute-done | bytes 393248 | tf_op jit(solution)/shard_map/ppermute | solution.py:90
  282.9 8.4 %collective-permute-done.44 = bf16[128,1536]{1,0:T(8,128)(2,1)} collective-permute-done((bf16[128,1536]{1,0:T(8,128)(2,1)S(1)}, bf16[128,1536]{1,0:T(8,128)(2,1)}, u32[]{:S(2)}, u32[]{:S(2)}) %collective-permute-start.44) | collective-permute-done | bytes 393248 | tf_op jit(solution)/shard_map/ppermute | solution.py:90
  302.9 5.8 %collective-permute-done.45 = bf16[128,1536]{1,0:T(8,128)(2,1)S(1)} collective-permute-done((bf16[128,1536]{1,0:T(8,128)(2,1)S(1)}, bf16[128,1536]{1,0:T(8,128)(2,1)S(1)}, u32[]{:S(2)}, u32[]{:S(2)}) %collective-permute-start.45) | collective-permute-done | bytes 393248 | tf_op jit(solution)/shard_map/ppermute | solution.py:90
  310.3 6.9 %collective-permute-done.47 = bf16[128,1536]{1,0:T(8,128)(2,1)S(1)} collective-permute-done((bf16[128,1536]{1,0:T(8,128)(2,1)S(1)}, bf16[128,1536]{1,0:T(8,128)(2,1)S(1)}, u32[]{:S(2)}, u32[]{:S(2)}) %collective-permute-start.47) | collective-permute-done | bytes 393248 | tf_op jit(solution)/shard_map/ppermute | solution.py:90
  317.2 2.0 collective-permute-done.46
  321.4 5.2 %collective-permute-done.50 = bf16[2,48,1024]{2,1,0:T(8,128)(2,1)S(1)} collective-permute-done((bf16[2,48,1024]{2,1,0:T(8,128)(2,1)S(1)}, bf16[2,48,1024]{2,1,0:T(8,128)(2,1)S(1)}, u32[]{:S(2)}, u32[]{:S(2)}) %collective-permute-start.50) | collective-permute-done | bytes 196640 | tf_op jit(solution)/shard_map/ppermute | solution.py:90
  (390 shorter events, 131.5 us)
Async XLA Ops:
  7.2 90.4 %all-gather.6.cloned.1.call-start = ((), (), s32[]{:S(2)}) async-start(), calls=%async_computation.7 | async-start | bytes 1720320 | tf_op jit(solution)/shard_map/all_gather | solution.py:198
  21.5 8.8 %collective-permute-start.8 = (bf16[2,48,1024]{2,1,0:T(8,128)(2,1)}, bf16[2,48,1024]{2,1,0:T(8,128)(2,1)S(1)}, u32[]{:S(2)}, u32[]{:S(2)}) collective-permute-start(bf16[2,48,1024]{2,1,0:T(8,128)(2,1)} %get-tuple-element.220), channel_id=1, source_target_pairs={{0,24},{8,16},{16,8},{24,0},{1,25},{9,17},{17,9},{25,1},{2,26},{10... | collective-permute-start | bytes 589832 | tf_op jit(solution)/shard_map/ppermute | solution.py:90
  23.0 9.4 %collective-permute-start.7 = (bf16[2,48,1024]{2,1,0:T(8,128)(2,1)S(1)}, bf16[2,48,1024]{2,1,0:T(8,128)(2,1)S(1)}, u32[]{:S(2)}, u32[]{:S(2)}) collective-permute-start(bf16[2,48,1024]{2,1,0:T(8,128)(2,1)S(1)} %get-tuple-element.221), channel_id=1, source_target_pairs={{0,16},{8,24},{16,0},{24,8},{1,17},{9,25},{17,1},{25,9},{2,18},{10... | collective-permute-start | bytes 589832 | tf_op jit(solution)/shard_map/ppermute | solution.py:90
  23.7 8.8 %collective-permute-start.6 = (bf16[2,48,1024]{2,1,0:T(8,128)(2,1)S(1)}, bf16[2,48,1024]{2,1,0:T(8,128)(2,1)S(1)}, u32[]{:S(2)}, u32[]{:S(2)}) collective-permute-start(bf16[2,48,1024]{2,1,0:T(8,128)(2,1)S(1)} %get-tuple-element.222), channel_id=1, source_target_pairs={{0,8},{8,0},{16,24},{24,16},{1,9},{9,1},{17,25},{25,17},{2,10},{10... | collective-permute-start | bytes 589832 | tf_op jit(solution)/shard_map/ppermute | solution.py:90
  25.7 11.0 %collective-permute-start.5 = (bf16[192,768]{1,0:T(8,128)(2,1)S(1)}, bf16[192,768]{1,0:T(8,128)(2,1)S(1)}, u32[]{:S(2)}, u32[]{:S(2)}) collective-permute-start(bf16[192,768]{1,0:T(8,128)(2,1)S(1)} %bitcast.379), channel_id=1, source_target_pairs={{0,3},{1,0},{2,1},{3,2},{4,7},{5,4},{6,5},{7,6},{8,11},{9,8},{10,9... | collective-permute-start | bytes 884744 | tf_op jit(solution)/shard_map/ppermute | solution.py:140
  29.3 11.6 %collective-permute-start.4 = (bf16[192,768]{1,0:T(8,128)(2,1)S(1)}, bf16[192,768]{1,0:T(8,128)(2,1)S(1)}, u32[]{:S(2)}, u32[]{:S(2)}) collective-permute-start(bf16[192,768]{1,0:T(8,128)(2,1)S(1)} %bitcast.380), channel_id=1, source_target_pairs={{0,1},{1,2},{2,3},{3,0},{4,5},{5,6},{6,7},{7,4},{8,9},{9,10},{10,1... | collective-permute-start | bytes 884744 | tf_op jit(solution)/shard_map/ppermute | solution.py:140
  41.7 126.8 %all-gather.4.cloned.1.call-start = ((), (), s32[]{:S(2)}) async-start(), calls=%async_computation.3 | async-start | bytes 3932160 | tf_op jit(solution)/shard_map/all_gather | solution.py:248
  41.8 17.4 %collective-permute-start.11 = (bf16[128,1664]{1,0:T(8,128)(2,1)S(1)}, bf16[128,1664]{1,0:T(8,128)(2,1)}, u32[]{:S(2)}, u32[]{:S(2)}) collective-permute-start(bf16[128,1664]{1,0:T(8,128)(2,1)S(1)} %slice.312), channel_id=1, source_target_pairs={{0,16},{8,24},{16,0},{24,8},{1,17},{9,25},{17,1},{25,9},{2,18},{10... | collective-permute-start | bytes 1277960 | tf_op jit(solution)/shard_map/ppermute | solution.py:90
  43.3 15.9 %collective-permute-start.10 = (bf16[128,1664]{1,0:T(8,128)(2,1)S(1)}, bf16[128,1664]{1,0:T(8,128)(2,1)}, u32[]{:S(2)}, u32[]{:S(2)}) collective-permute-start(bf16[128,1664]{1,0:T(8,128)(2,1)S(1)} %slice.312), channel_id=1, source_target_pairs={{0,8},{8,0},{16,24},{24,16},{1,9},{9,1},{17,25},{25,17},{2,10},{10... | collective-permute-start | bytes 1277960 | tf_op jit(solution)/shard_map/ppermute | solution.py:90
  44.3 22.5 %collective-permute-start.15 = (bf16[128,1664]{1,0:T(8,128)(2,1)S(1)}, bf16[128,1664]{1,0:T(8,128)(2,1)}, u32[]{:S(2)}, u32[]{:S(2)}) collective-permute-start(bf16[128,1664]{1,0:T(8,128)(2,1)S(1)} %slice.312), channel_id=1, source_target_pairs={{0,24},{8,16},{16,8},{24,0},{1,25},{9,17},{17,9},{25,1},{2,26},{10... | collective-permute-start | bytes 1277960 | tf_op jit(solution)/shard_map/ppermute | solution.py:90
  45.5 8.7 %collective-permute-start.13 = (bf16[192,384]{1,0:T(8,128)(2,1)S(1)}, bf16[192,384]{1,0:T(8,128)(2,1)S(1)}, u32[]{:S(2)}, u32[]{:S(2)}) collective-permute-start(bf16[192,384]{1,0:T(8,128)(2,1)S(1)} %slice.316), channel_id=1, source_target_pairs={{0,3},{1,0},{2,1},{3,2},{4,7},{5,4},{6,5},{7,6},{8,11},{9,8},{10,9... | collective-permute-start | bytes 442376 | tf_op jit(solution)/shard_map/ppermute | solution.py:140
  47.3 11.9 %collective-permute-start.12 = (bf16[192,384]{1,0:T(8,128)(2,1)S(1)}, bf16[192,384]{1,0:T(8,128)(2,1)S(1)}, u32[]{:S(2)}, u32[]{:S(2)}) collective-permute-start(bf16[192,384]{1,0:T(8,128)(2,1)S(1)} %slice.315), channel_id=1, source_target_pairs={{0,1},{1,2},{2,3},{3,0},{4,5},{5,6},{6,7},{7,4},{8,9},{9,10},{10,1... | collective-permute-start | bytes 442376 | tf_op jit(solution)/shard_map/ppermute | solution.py:140
  64.6 7.7 %collective-permute-start.14 = (bf16[4,4,48,768]{3,2,1,0:T(8,128)(2,1)}, bf16[4,4,48,768]{3,2,1,0:T(8,128)(2,1)}, u32[]{:S(2)}, u32[]{:S(2)}) collective-permute-start(bf16[4,4,48,768]{3,2,1,0:T(8,128)(2,1)} %constant_dynamic-update-slice_fusion.4), channel_id=1, source_target_pairs={{0,4},{4,0},{1,5},{5,1},{2,6},{6,2},{3,7},{7,3},{8,12},{12,8},{9,1... | collective-permute-start | bytes 3538952 | tf_op jit(solution)/shard_map/ppermute | solution.py:87
  69.2 179.7 %reduce-scatter.4.cloned.1.call-start = ((), (), s32[]{:S(2)}) async-start(), calls=%async_computation.4 | async-start | bytes 1966080 | tf_op jit(solution)/shard_map/reduce_scatter | solution.py:273
  74.4 13.0 %collective-permute-start.18 = (bf16[128,1536]{1,0:T(8,128)(2,1)S(1)}, bf16[128,1536]{1,0:T(8,128)(2,1)S(1)}, u32[]{:S(2)}, u32[]{:S(2)}) collective-permute-start(bf16[128,1536]{1,0:T(8,128)(2,1)S(1)} %slice.318), channel_id=1, source_target_pairs={{0,24},{8,16},{16,8},{24,0},{1,25},{9,17},{17,9},{25,1},{2,26},{10... | collective-permute-start | bytes 1179656 | tf_op jit(solution)/shard_map/ppermute | solution.py:90
  75.4 19.8 %collective-permute-start.17 = (bf16[128,1536]{1,0:T(8,128)(2,1)S(1)}, bf16[128,1536]{1,0:T(8,128)(2,1)}, u32[]{:S(2)}, u32[]{:S(2)}) collective-permute-start(bf16[128,1536]{1,0:T(8,128)(2,1)S(1)} %slice.318), channel_id=1, source_target_pairs={{0,16},{8,24},{16,0},{24,8},{1,17},{9,25},{17,1},{25,9},{2,18},{10... | collective-permute-start | bytes 1179656 | tf_op jit(solution)/shard_map/ppermute | solution.py:90
  77.2 18.0 %collective-permute-start.16 = (bf16[128,1536]{1,0:T(8,128)(2,1)S(1)}, bf16[128,1536]{1,0:T(8,128)(2,1)}, u32[]{:S(2)}, u32[]{:S(2)}) collective-permute-start(bf16[128,1536]{1,0:T(8,128)(2,1)S(1)} %slice.318), channel_id=1, source_target_pairs={{0,8},{8,0},{16,24},{24,16},{1,9},{9,1},{17,25},{25,17},{2,10},{10... | collective-permute-start | bytes 1179656 | tf_op jit(solution)/shard_map/ppermute | solution.py:90
  98.7 6.5 %collective-permute-start.19 = (bf16[192,1536]{1,0:T(8,128)(2,1)S(1)}, bf16[192,1536]{1,0:T(8,128)(2,1)S(1)}, u32[]{:S(2)}, u32[]{:S(2)}) collective-permute-start(bf16[192,1536]{1,0:T(8,128)(2,1)S(1)} %bitcast.360), channel_id=1, source_target_pairs={{0,4},{4,0},{1,5},{5,1},{2,6},{6,2},{3,7},{7,3},{8,12},{12,8},{9,1... | collective-permute-start | bytes 1769480 | tf_op jit(solution)/shard_map/ppermute | solution.py:87
  105.5 24.1 %collective-permute-start.23 = (bf16[512,1536]{1,0:T(8,128)(2,1)}, bf16[512,1536]{1,0:T(8,128)(2,1)S(1)}, u32[]{:S(2)}, u32[]{:S(2)}) collective-permute-start(bf16[512,1536]{1,0:T(8,128)(2,1)} %pad_maximum_fusion.5), channel_id=1, source_target_pairs={{0,4},{4,0},{1,5},{5,1},{2,6},{6,2},{3,7},{7,3},{8,12},{12,8},{9,1... | collective-permute-start | bytes 4718600 | tf_op jit(solution)/shard_map/ppermute | solution.py:87
  107.2 12.1 %collective-permute-start.20 = (bf16[128,1536]{1,0:T(8,128)(2,1)S(1)}, bf16[128,1536]{1,0:T(8,128)(2,1)S(1)}, u32[]{:S(2)}, u32[]{:S(2)}) collective-permute-start(bf16[128,1536]{1,0:T(8,128)(2,1)S(1)} %get-tuple-element.189), channel_id=1, source_target_pairs={{0,8},{8,0},{16,24},{24,16},{1,9},{9,1},{17,25},{25,17},{2,10},{10... | collective-permute-start | bytes 1179656 | tf_op jit(solution)/shard_map/ppermute | solution.py:90
  108.7 19.2 %collective-permute-start.22 = (bf16[128,1536]{1,0:T(8,128)(2,1)S(1)}, bf16[128,1536]{1,0:T(8,128)(2,1)S(1)}, u32[]{:S(2)}, u32[]{:S(2)}) collective-permute-start(bf16[128,1536]{1,0:T(8,128)(2,1)S(1)} %get-tuple-element.190), channel_id=1, source_target_pairs={{0,24},{8,16},{16,8},{24,0},{1,25},{9,17},{17,9},{25,1},{2,26},{10... | collective-permute-start | bytes 1179656 | tf_op jit(solution)/shard_map/ppermute | solution.py:90
  110.0 19.3 %collective-permute-start.21 = (bf16[128,1536]{1,0:T(8,128)(2,1)S(1)}, bf16[128,1536]{1,0:T(8,128)(2,1)S(1)}, u32[]{:S(2)}, u32[]{:S(2)}) collective-permute-start(bf16[128,1536]{1,0:T(8,128)(2,1)S(1)} %get-tuple-element.191), channel_id=1, source_target_pairs={{0,16},{8,24},{16,0},{24,8},{1,17},{9,25},{17,1},{25,9},{2,18},{10... | collective-permute-start | bytes 1179656 | tf_op jit(solution)/shard_map/ppermute | solution.py:90
  133.2 13.0 %collective-permute-start.26 = (bf16[128,1536]{1,0:T(8,128)(2,1)S(1)}, bf16[128,1536]{1,0:T(8,128)(2,1)S(1)}, u32[]{:S(2)}, u32[]{:S(2)}) collective-permute-start(bf16[128,1536]{1,0:T(8,128)(2,1)S(1)} %multiply_convert_fusion.3), channel_id=1, source_target_pairs={{0,24},{8,16},{16,8},{24,0},{1,25},{9,17},{17,9},{25,1},{2,26},{10... | collective-permute-start | bytes 1179656 | tf_op jit(solution)/shard_map/ppermute | solution.py:90
  134.9 17.8 %collective-permute-start.25 = (bf16[128,1536]{1,0:T(8,128)(2,1)S(1)}, bf16[128,1536]{1,0:T(8,128)(2,1)S(1)}, u32[]{:S(2)}, u32[]{:S(2)}) collective-permute-start(bf16[128,1536]{1,0:T(8,128)(2,1)S(1)} %multiply_convert_fusion.3), channel_id=1, source_target_pairs={{0,16},{8,24},{16,0},{24,8},{1,17},{9,25},{17,1},{25,9},{2,18},{10... | collective-permute-start | bytes 1179656 | tf_op jit(solution)/shard_map/ppermute | solution.py:90
  135.5 17.2 %collective-permute-start.24 = (bf16[128,1536]{1,0:T(8,128)(2,1)S(1)}, bf16[128,1536]{1,0:T(8,128)(2,1)S(1)}, u32[]{:S(2)}, u32[]{:S(2)}) collective-permute-start(bf16[128,1536]{1,0:T(8,128)(2,1)S(1)} %multiply_convert_fusion.3), channel_id=1, source_target_pairs={{0,8},{8,0},{16,24},{24,16},{1,9},{9,1},{17,25},{25,17},{2,10},{10... | collective-permute-start | bytes 1179656 | tf_op jit(solution)/shard_map/ppermute | solution.py:90
  153.0 8.6 %collective-permute-start.29 = (bf16[64,1536]{1,0:T(8,128)(2,1)S(1)}, bf16[64,1536]{1,0:T(8,128)(2,1)S(1)}, u32[]{:S(2)}, u32[]{:S(2)}) collective-permute-start(bf16[64,1536]{1,0:T(8,128)(2,1)S(1)} %copy-done.30), channel_id=1, source_target_pairs={{0,3},{1,0},{2,1},{3,2},{4,7},{5,4},{6,5},{7,6},{8,11},{9,8},{10,9... | collective-permute-start | bytes 589832 | tf_op jit(solution)/shard_map/ppermute | solution.py:140
  156.2 12.4 %collective-permute-start.28 = (bf16[64,1536]{1,0:T(8,128)(2,1)S(1)}, bf16[64,1536]{1,0:T(8,128)(2,1)}, u32[]{:S(2)}, u32[]{:S(2)}) collective-permute-start(bf16[64,1536]{1,0:T(8,128)(2,1)S(1)} %copy-done.30), channel_id=1, source_target_pairs={{0,1},{1,2},{2,3},{3,0},{4,5},{5,6},{6,7},{7,4},{8,9},{9,10},{10,1... | collective-permute-start | bytes 589832 | tf_op jit(solution)/shard_map/ppermute | solution.py:140
  172.9 8.0 %collective-permute-start.31 = (bf16[64,768]{1,0:T(8,128)(2,1)S(1)}, bf16[64,768]{1,0:T(8,128)(2,1)S(1)}, u32[]{:S(2)}, u32[]{:S(2)}) collective-permute-start(bf16[64,768]{1,0:T(8,128)(2,1)S(1)} %slice.340), channel_id=1, source_target_pairs={{0,3},{1,0},{2,1},{3,2},{4,7},{5,4},{6,5},{7,6},{8,11},{9,8},{10,9... | collective-permute-start | bytes 294920 | tf_op jit(solution)/shard_map/ppermute | solution.py:140
  174.0 6.9 %collective-permute-start.30 = (bf16[64,768]{1,0:T(8,128)(2,1)S(1)}, bf16[64,768]{1,0:T(8,128)(2,1)S(1)}, u32[]{:S(2)}, u32[]{:S(2)}) collective-permute-start(bf16[64,768]{1,0:T(8,128)(2,1)S(1)} %slice.339), channel_id=1, source_target_pairs={{0,1},{1,2},{2,3},{3,0},{4,5},{5,6},{6,7},{7,4},{8,9},{9,10},{10,1... | collective-permute-start | bytes 294920 | tf_op jit(solution)/shard_map/ppermute | solution.py:140
  193.8 100.3 %reduce-scatter.6.cloned.1.call-start = ((), (), s32[]{:S(2)}) async-start(), calls=%async_computation.5 | async-start | bytes 3932160 | tf_op jit(solution)/shard_map/reduce_scatter | solution.py:283
  201.7 12.3 %collective-permute-start.33 = (bf16[128,1536]{1,0:T(8,128)(2,1)S(1)}, bf16[128,1536]{1,0:T(8,128)(2,1)S(1)}, u32[]{:S(2)}, u32[]{:S(2)}) collective-permute-start(bf16[128,1536]{1,0:T(8,128)(2,1)S(1)} %get-tuple-element.186), channel_id=1, source_target_pairs={{0,8},{8,0},{16,24},{24,16},{1,9},{9,1},{17,25},{25,17},{2,10},{10... | collective-permute-start | bytes 1179656 | tf_op jit(solution)/shard_map/ppermute | solution.py:90
  202.6 18.9 %collective-permute-start.35 = (bf16[128,1536]{1,0:T(8,128)(2,1)S(1)}, bf16[128,1536]{1,0:T(8,128)(2,1)S(1)}, u32[]{:S(2)}, u32[]{:S(2)}) collective-permute-start(bf16[128,1536]{1,0:T(8,128)(2,1)S(1)} %get-tuple-element.187), channel_id=1, source_target_pairs={{0,24},{8,16},{16,8},{24,0},{1,25},{9,17},{17,9},{25,1},{2,26},{10... | collective-permute-start | bytes 1179656 | tf_op jit(solution)/shard_map/ppermute | solution.py:90
  203.9 19.0 %collective-permute-start.34 = (bf16[128,1536]{1,0:T(8,128)(2,1)S(1)}, bf16[128,1536]{1,0:T(8,128)(2,1)S(1)}, u32[]{:S(2)}, u32[]{:S(2)}) collective-permute-start(bf16[128,1536]{1,0:T(8,128)(2,1)S(1)} %get-tuple-element.188), channel_id=1, source_target_pairs={{0,16},{8,24},{16,0},{24,8},{1,17},{9,25},{17,1},{25,9},{2,18},{10... | collective-permute-start | bytes 1179656 | tf_op jit(solution)/shard_map/ppermute | solution.py:90
  214.0 30.3 %collective-permute-start.39 = (bf16[512,1536]{1,0:T(8,128)(2,1)}, bf16[512,1536]{1,0:T(8,128)(2,1)}, u32[]{:S(2)}, u32[]{:S(2)}) collective-permute-start(bf16[512,1536]{1,0:T(8,128)(2,1)} %convolution_convert_fusion.2), channel_id=1, source_target_pairs={{0,4},{4,0},{1,5},{5,1},{2,6},{6,2},{3,7},{7,3},{8,12},{12,8},{9,1... | collective-permute-start | bytes 4718600 | tf_op jit(solution)/shard_map/ppermute | solution.py:87
  223.5 13.0 %collective-permute-start.38 = (bf16[128,1536]{1,0:T(8,128)(2,1)S(1)}, bf16[128,1536]{1,0:T(8,128)(2,1)S(1)}, u32[]{:S(2)}, u32[]{:S(2)}) collective-permute-start(bf16[128,1536]{1,0:T(8,128)(2,1)S(1)} %fusion.86), channel_id=1, source_target_pairs={{0,24},{8,16},{16,8},{24,0},{1,25},{9,17},{17,9},{25,1},{2,26},{10... | collective-permute-start | bytes 1179656 | tf_op jit(solution)/shard_map/ppermute | solution.py:90
  225.3 16.7 %collective-permute-start.37 = (bf16[128,1536]{1,0:T(8,128)(2,1)S(1)}, bf16[128,1536]{1,0:T(8,128)(2,1)}, u32[]{:S(2)}, u32[]{:S(2)}) collective-permute-start(bf16[128,1536]{1,0:T(8,128)(2,1)S(1)} %fusion.86), channel_id=1, source_target_pairs={{0,16},{8,24},{16,0},{24,8},{1,17},{9,25},{17,1},{25,9},{2,18},{10... | collective-permute-start | bytes 1179656 | tf_op jit(solution)/shard_map/ppermute | solution.py:90
  226.7 15.3 %collective-permute-start.36 = (bf16[128,1536]{1,0:T(8,128)(2,1)S(1)}, bf16[128,1536]{1,0:T(8,128)(2,1)}, u32[]{:S(2)}, u32[]{:S(2)}) collective-permute-start(bf16[128,1536]{1,0:T(8,128)(2,1)S(1)} %fusion.86), channel_id=1, source_target_pairs={{0,8},{8,0},{16,24},{24,16},{1,9},{9,1},{17,25},{25,17},{2,10},{10... | collective-permute-start | bytes 1179656 | tf_op jit(solution)/shard_map/ppermute | solution.py:90
  227.1 105.8 %reduce-scatter.8.cloned.1.call-start = ((), (), s32[]{:S(2)}) async-start(), calls=%async_computation.6 | async-start | bytes 2211840 | tf_op jit(solution)/shard_map/reduce_scatter | solution.py:323
  270.6 12.3 %collective-permute-start.42 = (bf16[128,1536]{1,0:T(8,128)(2,1)}, bf16[128,1536]{1,0:T(8,128)(2,1)}, u32[]{:S(2)}, u32[]{:S(2)}) collective-permute-start(bf16[128,1536]{1,0:T(8,128)(2,1)} %get-tuple-element.183), channel_id=1, source_target_pairs={{0,8},{8,0},{16,24},{24,16},{1,9},{9,1},{17,25},{25,17},{2,10},{10... | collective-permute-start | bytes 1179656 | tf_op jit(solution)/shard_map/ppermute | solution.py:90
  272.2 19.1 %collective-permute-start.44 = (bf16[128,1536]{1,0:T(8,128)(2,1)S(1)}, bf16[128,1536]{1,0:T(8,128)(2,1)}, u32[]{:S(2)}, u32[]{:S(2)}) collective-permute-start(bf16[128,1536]{1,0:T(8,128)(2,1)S(1)} %get-tuple-element.184), channel_id=1, source_target_pairs={{0,24},{8,16},{16,8},{24,0},{1,25},{9,17},{17,9},{25,1},{2,26},{10... | collective-permute-start | bytes 1179656 | tf_op jit(solution)/shard_map/ppermute | solution.py:90
  273.5 19.0 %collective-permute-start.43 = (bf16[128,1536]{1,0:T(8,128)(2,1)S(1)}, bf16[128,1536]{1,0:T(8,128)(2,1)}, u32[]{:S(2)}, u32[]{:S(2)}) collective-permute-start(bf16[128,1536]{1,0:T(8,128)(2,1)S(1)} %get-tuple-element.185), channel_id=1, source_target_pairs={{0,16},{8,24},{16,0},{24,8},{1,17},{9,25},{17,1},{25,9},{2,18},{10... | collective-permute-start | bytes 1179656 | tf_op jit(solution)/shard_map/ppermute | solution.py:90
  296.7 12.1 %collective-permute-start.45 = (bf16[128,1536]{1,0:T(8,128)(2,1)S(1)}, bf16[128,1536]{1,0:T(8,128)(2,1)S(1)}, u32[]{:S(2)}, u32[]{:S(2)}) collective-permute-start(bf16[128,1536]{1,0:T(8,128)(2,1)S(1)} %get-tuple-element.194), channel_id=1, source_target_pairs={{0,8},{8,0},{16,24},{24,16},{1,9},{9,1},{17,25},{25,17},{2,10},{10... | collective-permute-start | bytes 1179656 | tf_op jit(solution)/shard_map/ppermute | solution.py:90
  297.6 19.6 %collective-permute-start.47 = (bf16[128,1536]{1,0:T(8,128)(2,1)S(1)}, bf16[128,1536]{1,0:T(8,128)(2,1)S(1)}, u32[]{:S(2)}, u32[]{:S(2)}) collective-permute-start(bf16[128,1536]{1,0:T(8,128)(2,1)S(1)} %get-tuple-element.195), channel_id=1, source_target_pairs={{0,24},{8,16},{16,8},{24,0},{1,25},{9,17},{17,9},{25,1},{2,26},{10... | collective-permute-start | bytes 1179656 | tf_op jit(solution)/shard_map/ppermute | solution.py:90
  298.8 20.4 %collective-permute-start.46 = (bf16[128,1536]{1,0:T(8,128)(2,1)S(1)}, bf16[128,1536]{1,0:T(8,128)(2,1)S(1)}, u32[]{:S(2)}, u32[]{:S(2)}) collective-permute-start(bf16[128,1536]{1,0:T(8,128)(2,1)S(1)} %get-tuple-element.196), channel_id=1, source_target_pairs={{0,16},{8,24},{16,0},{24,8},{1,17},{9,25},{17,1},{25,9},{2,18},{10... | collective-permute-start | bytes 1179656 | tf_op jit(solution)/shard_map/ppermute | solution.py:90
  300.7 20.7 %collective-permute-start.49 = (bf16[2,48,1024]{2,1,0:T(8,128)(2,1)S(1)}, bf16[2,48,1024]{2,1,0:T(8,128)(2,1)S(1)}, u32[]{:S(2)}, u32[]{:S(2)}) collective-permute-start(bf16[2,48,1024]{2,1,0:T(8,128)(2,1)S(1)} %get-tuple-element.216), channel_id=1, source_target_pairs={{0,8},{8,0},{16,24},{24,16},{1,9},{9,1},{17,25},{25,17},{2,10},{10... | collective-permute-start | bytes 589832 | tf_op jit(solution)/shard_map/ppermute | solution.py:90
  301.6 25.0 %collective-permute-start.50 = (bf16[2,48,1024]{2,1,0:T(8,128)(2,1)S(1)}, bf16[2,48,1024]{2,1,0:T(8,128)(2,1)S(1)}, u32[]{:S(2)}, u32[]{:S(2)}) collective-permute-start(bf16[2,48,1024]{2,1,0:T(8,128)(2,1)S(1)} %get-tuple-element.217), channel_id=1, source_target_pairs={{0,16},{8,24},{16,0},{24,8},{1,17},{9,25},{17,1},{25,9},{2,18},{10... | collective-permute-start | bytes 589832 | tf_op jit(solution)/shard_map/ppermute | solution.py:90
  308.7 17.9 %collective-permute-start.51 = (bf16[2,48,1024]{2,1,0:T(8,128)(2,1)S(1)}, bf16[2,48,1024]{2,1,0:T(8,128)(2,1)S(1)}, u32[]{:S(2)}, u32[]{:S(2)}) collective-permute-start(bf16[2,48,1024]{2,1,0:T(8,128)(2,1)S(1)} %get-tuple-element.218), channel_id=1, source_target_pairs={{0,24},{8,16},{16,8},{24,0},{1,25},{9,17},{17,9},{25,1},{2,26},{10... | collective-permute-start | bytes 589832 | tf_op jit(solution)/shard_map/ppermute | solution.py:90
  321.1 11.9 %collective-permute-start.53 = (bf16[64,1536]{1,0:T(8,128)(2,1)}, bf16[64,1536]{1,0:T(8,128)(2,1)}, u32[]{:S(2)}, u32[]{:S(2)}) collective-permute-start(bf16[64,1536]{1,0:T(8,128)(2,1)} %slice.438), channel_id=1, source_target_pairs={{0,4},{4,0},{1,5},{5,1},{2,6},{6,2},{3,7},{7,3},{8,12},{12,8},{9,1... | collective-permute-start | bytes 589832 | tf_op jit(solution)/shard_map/ppermute | solution.py:87
  (74 other events, 389.0 us)
Sparse Core Ops, SparseCore 0:
  41.9 35.7 all-gather.5
  79.8 62.9 all-gather.3
  193.9 35.6 reduce-scatter.3
  231.8 59.2 reduce-scatter.5
  293.2 38.3 reduce-scatter.7
where the time goes:
time: 358 us; the launch traced here: 353 us
  waiting for transfers between devices  149 us (42%)
  starting transfers between devices  57 us (16%)
  matrix products  45.5 us (13%)
  other arithmetic  43.8 us (12%)
  local copies, waits for them, and re-layouts  42.6 us (12%)
  between operations  15.7 us (4%)
    ppermute x36, waiting for transfers between devices, chip_xor(): return lax.ppermute(a, 'chip', [(i, i ^ j) for i in range(chips)])  116 us
    ppermute x36, starting transfers between devices, chip_xor(): return lax.ppermute(a, 'chip', [(i, i ^ j) for i in range(chips)])  44 us
    ppermute x8, waiting for transfers between devices, along_z(): lax.ppermute(a, 'fsdp', [(i, (i + step) % rows_z) for i in range(rows_z)])  29.1 us
    dot_general x5, matrix products, mm_nt(): return jnp.einsum('te,de->td', a, b, preferred_element_type=f32)  16.4 us
    unnamed x125, local copies, waits for them, and re-layouts  14.2 us
    ppermute x8, starting transfers between devices, along_z(): lax.ppermute(a, 'fsdp', [(i, (i + step) % rows_z) for i in range(rows_z)])  11.4 us
    dot_general x5, matrix products, mm(): return jnp.dot(a, b, preferred_element_type=f32)  10.7 us
    dot_general x4, matrix products, mm_tn(): return jnp.einsum('td,te->de', a, b, preferred_element_type=f32)  9.16 us
  transfers between devices with their start and end apart: 62, of which 35 were waited for; matrix products, arithmetic and copies ran while one was open for 28% of the time, Pallas kernels for 0%

commit v1 on v0

--- a/solution.py
+++ b/solution.py
@@ -220,7 +220,6 @@
     own = x_low.shape[0]
     seq = x_all.shape[0]
 
-    dy_all = gather_chips(dy_low)
     x_full = x_all.astype(f32)
     h_one = (x_full * rms_scale(x_full)).astype(bf16)
     qkv = mm(h_one, w_qkv)
@@ -230,7 +229,8 @@
         qkv[:, q_cols : q_cols + kv_cols].reshape(seq, kv_heads, HEAD), cosine, sine
     ).astype(bf16)
     value = qkv[:, q_cols + kv_cols :].astype(bf16).reshape(seq, kv_heads, HEAD)
-    q_rot, rows = tie(q_rot, rows)
+    q_rot, rows, dy_low = tie(q_rot, rows, dy_low)
+    dy_all = gather_chips(dy_low)
     along_out = rows[:, : w_out.shape[0]].reshape(-1, width)
     out_w = both_cores(along_out).reshape(-1, width)
     scores = jnp.einsum("sgrh,tgh->grst", q_rot, k_rot, preferred_element_type=f32) * factor

time: 358 us -> 352 us (0.983)
    unnamed x125 -> x121, local copies, waits for them, and re-layouts: 14.2 us -> 13 us
  transfers between devices with their start and end apart: 62 -> 62, of which waited for: 35 -> 36; matrix products, arithmetic and copies ran while one was open for 28% -> 27% of each run, Pallas kernels for 0% -> 0%
where the time goes in v1:
time: 352 us; the launch traced here: 347 us
  waiting for transfers between devices  146 us (41%)
  starting transfers between devices  56.6 us (16%)
  matrix products  46.6 us (13%)
  other arithmetic  41.9 us (12%)
  local copies, waits for them, and re-layouts  40.5 us (12%)
  between operations  15.7 us (4%)
    ppermute x36, waiting for transfers between devices, chip_xor(): return lax.ppermute(a, 'chip', [(i, i ^ j) for i in range(chips)])  113 us
    ppermute x36, starting transfers between devices, chip_xor(): return lax.ppermute(a, 'chip', [(i, i ^ j) for i in range(chips)])  44 us
    ppermute x8, waiting for transfers between devices, along_z(): lax.ppermute(a, 'fsdp', [(i, (i + step) % rows_z) for i in range(rows_z)])  29 us
    dot_general x5, matrix products, mm_nt(): return jnp.einsum('te,de->td', a, b, preferred_element_type=f32)  16.5 us
    unnamed x121, local copies, waits for them, and re-layouts  13 us
    ppermute x8, starting transfers between devices, along_z(): lax.ppermute(a, 'fsdp', [(i, (i + step) % rows_z) for i in range(rows_z)])  11.4 us
    dot_general x5, matrix products, mm(): return jnp.dot(a, b, preferred_element_type=f32)  10.7 us
    dot_general x4, matrix products, mm_tn(): return jnp.einsum('td,te->de', a, b, preferred_element_type=f32)  9.16 us
  transfers between devices with their start and end apart: 62, of which 36 were waited for; matrix products, arithmetic and copies ran while one was open for 27% of the time, Pallas kernels for 0%

profile of v1, /device:TPU:0, one launch (start us, length us, event | category | flops | bytes accessed | tf_op | source)
XLA Modules:
  0.0 347.2 jit_solution(13593567603323745407)
XLA Ops:
  10.6 4.0 %collective-permute-start.3 = (bf16[48,768]{1,0:T(8,128)(2,1)S(1)}, bf16[48,768]{1,0:T(8,128)(2,1)S(1)}, u32[]{:S(2)}, u32[]{:S(2)}) collective-permute-start(bf16[48,768]{1,0:T(8,128)(2,1)S(1)} %get-tuple-element.264), channel_id=1, source_target_pairs={{0,24},{8,16},{16,8},{24,0},{1,25},{9,17},{17,9},{25,1},{2,26},{10... | collective-permute-start | bytes 221192 | tf_op jit(solution)/shard_map/ppermute | solution.py:90
  17.0 2.0 collective-permute-done.2
  25.7 3.6 %collective-permute-start.5 = (bf16[192,768]{1,0:T(8,128)(2,1)S(1)}, bf16[192,768]{1,0:T(8,128)(2,1)S(1)}, u32[]{:S(2)}, u32[]{:S(2)}) collective-permute-start(bf16[192,768]{1,0:T(8,128)(2,1)S(1)} %bitcast.379), channel_id=1, source_target_pairs={{0,3},{1,0},{2,1},{3,2},{4,7},{5,4},{6,5},{7,6},{8,11},{9,8},{10,9... | collective-permute-start | bytes 884744 | tf_op jit(solution)/shard_map/ppermute | solution.py:140
  30.3 2.1 collective-permute-done.7
  33.0 3.7 %collective-permute-done.5 = bf16[192,768]{1,0:T(8,128)(2,1)S(1)} collective-permute-done((bf16[192,768]{1,0:T(8,128)(2,1)S(1)}, bf16[192,768]{1,0:T(8,128)(2,1)S(1)}, u32[]{:S(2)}, u32[]{:S(2)}) %collective-permute-start.5) | collective-permute-done | bytes 294944 | tf_op jit(solution)/shard_map/ppermute | solution.py:140
  36.7 4.2 %collective-permute-done.4 = bf16[192,768]{1,0:T(8,128)(2,1)S(1)} collective-permute-done((bf16[192,768]{1,0:T(8,128)(2,1)S(1)}, bf16[192,768]{1,0:T(8,128)(2,1)S(1)}, u32[]{:S(2)}, u32[]{:S(2)}) %collective-permute-start.4) | collective-permute-done | bytes 294944 | tf_op jit(solution)/shard_map/ppermute | solution.py:140
  45.5 1.8 collective-permute-start.13
  49.7 4.5 %collective-permute-done.13 = bf16[192,384]{1,0:T(8,128)(2,1)S(1)} collective-permute-done((bf16[192,384]{1,0:T(8,128)(2,1)S(1)}, bf16[192,384]{1,0:T(8,128)(2,1)S(1)}, u32[]{:S(2)}, u32[]{:S(2)}) %collective-permute-start.13) | collective-permute-done | bytes 147488 | tf_op jit(solution)/shard_map/ppermute | solution.py:140
  54.2 5.0 %collective-permute-done.12 = bf16[192,384]{1,0:T(8,128)(2,1)S(1)} collective-permute-done((bf16[192,384]{1,0:T(8,128)(2,1)S(1)}, bf16[192,384]{1,0:T(8,128)(2,1)S(1)}, u32[]{:S(2)}, u32[]{:S(2)}) %collective-permute-start.12) | collective-permute-done | bytes 147488 | tf_op jit(solution)/shard_map/ppermute | solution.py:140
  72.4 1.8 select_bitcast_fusion.1
  79.8 1.8 collective-permute-start.17
  83.5 4.7 %fusion.98 = (f32[2,2,512]{2,1,0:T(2,128)S(1)}, f32[2,2,512,512]{2,3,1,0:T(8,128)}) fusion(pred[512,512]{0,1:T(8,128)(4,1)} %compare_and_fusion, bf16[512,2,2,96]{0,3,2,1:T(8,128)(2,1)S(1)} %pad_maximum_fusion.15, bf16[512,2,48]{0,2,1:T(8,128)(2,1)S(1)} %copy-done.37, bf16[512,2,48]{0,2,1:T(8,128)(2,1)S(1)} %get-tuple-element.233), kind=kOutput, calls=%fused_computation.284 | convolution fusion | flops 205914624 | bytes 5054464 | tf_op jit(solution)/shard_map/sub | solution.py:238
  88.2 2.8 convolution_convert_fusion.6
  91.7 7.9 %collective-permute-done.17 = bf16[128,1536]{1,0:T(8,128)(2,1)} collective-permute-done((bf16[128,1536]{1,0:T(8,128)(2,1)S(1)}, bf16[128,1536]{1,0:T(8,128)(2,1)}, u32[]{:S(2)}, u32[]{:S(2)}) %collective-permute-start.17) | collective-permute-done | bytes 393248 | tf_op jit(solution)/shard_map/ppermute | solution.py:90
  105.8 8.5 %collective-permute-done.20 = bf16[128,1536]{1,0:T(8,128)(2,1)S(1)} collective-permute-done((bf16[128,1536]{1,0:T(8,128)(2,1)S(1)}, bf16[128,1536]{1,0:T(8,128)(2,1)S(1)}, u32[]{:S(2)}, u32[]{:S(2)}) %collective-permute-start.20) | collective-permute-done | bytes 393248 | tf_op jit(solution)/shard_map/ppermute | solution.py:90
  114.3 8.8 %collective-permute-done.22 = bf16[128,1536]{1,0:T(8,128)(2,1)S(1)} collective-permute-done((bf16[128,1536]{1,0:T(8,128)(2,1)S(1)}, bf16[128,1536]{1,0:T(8,128)(2,1)S(1)}, u32[]{:S(2)}, u32[]{:S(2)}) %collective-permute-start.22) | collective-permute-done | bytes 393248 | tf_op jit(solution)/shard_map/ppermute | solution.py:90
  124.9 1.9 pad_maximum_fusion
  130.6 9.4 %collective-permute-done.26 = bf16[128,1536]{1,0:T(8,128)(2,1)S(1)} collective-permute-done((bf16[128,1536]{1,0:T(8,128)(2,1)S(1)}, bf16[128,1536]{1,0:T(8,128)(2,1)S(1)}, u32[]{:S(2)}, u32[]{:S(2)}) %collective-permute-start.26) | collective-permute-done | bytes 393248 | tf_op jit(solution)/shard_map/ppermute | solution.py:90
  140.0 6.6 %collective-permute-done.25 = bf16[128,1536]{1,0:T(8,128)(2,1)S(1)} collective-permute-done((bf16[128,1536]{1,0:T(8,128)(2,1)S(1)}, bf16[128,1536]{1,0:T(8,128)(2,1)S(1)}, u32[]{:S(2)}, u32[]{:S(2)}) %collective-permute-start.25) | collective-permute-done | bytes 393248 | tf_op jit(solution)/shard_map/ppermute | solution.py:90
  146.9 3.2 collective-permute-start.29
  150.2 1.8 pad_maximum_fusion.1
  152.0 3.4 collective-permute-done.29
  156.0 6.4 %collective-permute-done.28 = bf16[64,1536]{1,0:T(8,128)(2,1)} collective-permute-done((bf16[64,1536]{1,0:T(8,128)(2,1)S(1)}, bf16[64,1536]{1,0:T(8,128)(2,1)}, u32[]{:S(2)}, u32[]{:S(2)}) %collective-permute-start.28) | collective-permute-done | bytes 196640 | tf_op jit(solution)/shard_map/ppermute | solution.py:140
  164.3 2.4 copy.75
  169.3 3.6 %fusion.100 = f32[1024,1024]{0,1:T(8,128)S(1)} fusion(bf16[1024,1536]{1,0:T(8,128)(2,1)S(1)} %copy-done.8, bf16[1536,1024]{1,0:T(8,128)(2,1)S(1)} %bitcast.337), kind=kOutput, calls=%fused_computation.286 | convolution fusion | flops 3221225472 | bytes 10485760 | tf_op jit(solution)/shard_map/dot_general | solution.py:46
  174.8 3.6 %multiply_convert_fusion.1 = (bf16[1024,512]{0,1:T(8,128)(2,1)S(1)}, bf16[1024,512]{0,1:T(8,128)(2,1)}, bf16[1024,512]{0,1:T(8,128)(2,1)S(1)}) fusion(f32[1024,1024]{0,1:T(8,128)S(1)} %fusion.100, bf16[1024,1536]{1,0:T(8,128)(2,1)S(1)} %copy-done.7, bf16[512,1536]{1,0:T(8,128)(2,1)S(1)} %bitcast.330), kind=kOutput, calls=%fused_computation.27 | convolution fusion | flops 1619001344 | bytes 12058624 | tf_op jit(solution)/shard_map/te,de->td/dot_general | solution.py:54
  179.4 3.0 convolution_convert_fusion.4
  184.6 3.0 convolution_convert_fusion.3
  187.7 3.5 %collective-permute-done.32 = bf16[512,1536]{1,0:T(8,128)(2,1)S(1)} collective-permute-done((bf16[512,1536]{1,0:T(8,128)(2,1)}, bf16[512,1536]{1,0:T(8,128)(2,1)S(1)}, u32[]{:S(2)}, u32[]{:S(2)}) %collective-permute-start.32) | collective-permute-done | bytes 1572896 | tf_op jit(solution)/shard_map/ppermute | solution.py:87
  191.2 4.1 %convert_add_fusion.1 = f32[512,1536]{1,0:T(8,128)S(1)} fusion(bf16[512,1536]{1,0:T(8,128)(2,1)S(1)} %collective-permute-done.32, bf16[1536,1024]{1,0:T(8,128)(2,1)} %bitcast.338, bf16[1024,1024]{0,1:T(8,128)(2,1)} %copy-done.16), kind=kOutput, calls=%fused_computation.18 | convolution fusion | flops 1612185600 | bytes 8912896 | tf_op jit(solution)/shard_map/te,de->td/dot_general | solution.py:54
  199.1 3.8 %convolution_convert_fusion = bf16[1536,1024]{1,0:T(8,128)(2,1)S(1)} fusion(bf16[1024,1536]{1,0:T(8,128)(2,1)S(1)} %copy-done.9, bf16[1024,1024]{0,1:T(8,128)(2,1)S(1)} %copy-done.17), kind=kOutput, calls=%fused_computation.10 | convolution fusion | flops 3222798336 | bytes 8388608 | tf_op jit(solution)/shard_map/td,te->de/dot_general | solution.py:50
  202.9 2.0 copy.76
  205.6 2.2 convolution_convert_fusion.2
  207.9 7.5 %collective-permute-done.35 = bf16[128,1536]{1,0:T(8,128)(2,1)S(1)} collective-permute-done((bf16[128,1536]{1,0:T(8,128)(2,1)S(1)}, bf16[128,1536]{1,0:T(8,128)(2,1)S(1)}, u32[]{:S(2)}, u32[]{:S(2)}) %collective-permute-start.35) | collective-permute-done | bytes 393248 | tf_op jit(solution)/shard_map/ppermute | solution.py:90
  221.2 9.1 %collective-permute-done.38 = bf16[128,1536]{1,0:T(8,128)(2,1)S(1)} collective-permute-done((bf16[128,1536]{1,0:T(8,128)(2,1)S(1)}, bf16[128,1536]{1,0:T(8,128)(2,1)S(1)}, u32[]{:S(2)}, u32[]{:S(2)}) %collective-permute-start.38) | collective-permute-done | bytes 393248 | tf_op jit(solution)/shard_map/ppermute | solution.py:90
  230.3 5.4 %collective-permute-done.37 = bf16[128,1536]{1,0:T(8,128)(2,1)} collective-permute-done((bf16[128,1536]{1,0:T(8,128)(2,1)S(1)}, bf16[128,1536]{1,0:T(8,128)(2,1)}, u32[]{:S(2)}, u32[]{:S(2)}) %collective-permute-start.37) | collective-permute-done | bytes 393248 | tf_op jit(solution)/shard_map/ppermute | solution.py:90
  235.8 2.4 pad_maximum_fusion.8
  238.2 2.5 convert_add_fusion
  242.7 2.7 convolution_convert_fusion.7
  256.9 3.1 fusion.101
  261.5 2.1 convert.86
  268.9 7.8 %collective-permute-done.42 = bf16[128,1536]{1,0:T(8,128)(2,1)} collective-permute-done((bf16[128,1536]{1,0:T(8,128)(2,1)}, bf16[128,1536]{1,0:T(8,128)(2,1)}, u32[]{:S(2)}, u32[]{:S(2)}) %collective-permute-start.42) | collective-permute-done | bytes 393248 | tf_op jit(solution)/shard_map/ppermute | solution.py:90
  276.7 8.4 %collective-permute-done.44 = bf16[128,1536]{1,0:T(8,128)(2,1)} collective-permute-done((bf16[128,1536]{1,0:T(8,128)(2,1)S(1)}, bf16[128,1536]{1,0:T(8,128)(2,1)}, u32[]{:S(2)}, u32[]{:S(2)}) %collective-permute-start.44) | collective-permute-done | bytes 393248 | tf_op jit(solution)/shard_map/ppermute | solution.py:90
  296.8 5.8 %collective-permute-done.45 = bf16[128,1536]{1,0:T(8,128)(2,1)S(1)} collective-permute-done((bf16[128,1536]{1,0:T(8,128)(2,1)S(1)}, bf16[128,1536]{1,0:T(8,128)(2,1)S(1)}, u32[]{:S(2)}, u32[]{:S(2)}) %collective-permute-start.45) | collective-permute-done | bytes 393248 | tf_op jit(solution)/shard_map/ppermute | solution.py:90
  304.2 6.9 %collective-permute-done.47 = bf16[128,1536]{1,0:T(8,128)(2,1)S(1)} collective-permute-done((bf16[128,1536]{1,0:T(8,128)(2,1)S(1)}, bf16[128,1536]{1,0:T(8,128)(2,1)S(1)}, u32[]{:S(2)}, u32[]{:S(2)}) %collective-permute-start.47) | collective-permute-done | bytes 393248 | tf_op jit(solution)/shard_map/ppermute | solution.py:90
  311.1 2.0 collective-permute-done.46
  315.2 5.2 %collective-permute-done.50 = bf16[2,48,1024]{2,1,0:T(8,128)(2,1)S(1)} collective-permute-done((bf16[2,48,1024]{2,1,0:T(8,128)(2,1)S(1)}, bf16[2,48,1024]{2,1,0:T(8,128)(2,1)S(1)}, u32[]{:S(2)}, u32[]{:S(2)}) %collective-permute-start.50) | collective-permute-done | bytes 196640 | tf_op jit(solution)/shard_map/ppermute | solution.py:90
  329.6 1.8 collective-permute-start.56
  (385 shorter events, 128.0 us)
Async XLA Ops:
  7.2 71.5 %all-gather.6.cloned.1.call-start = ((), (), s32[]{:S(2)}) async-start(), calls=%async_computation.7 | async-start | bytes 1720320 | tf_op jit(solution)/shard_map/all_gather | solution.py:198
  21.5 8.8 %collective-permute-start.8 = (bf16[2,48,1024]{2,1,0:T(8,128)(2,1)}, bf16[2,48,1024]{2,1,0:T(8,128)(2,1)S(1)}, u32[]{:S(2)}, u32[]{:S(2)}) collective-permute-start(bf16[2,48,1024]{2,1,0:T(8,128)(2,1)} %get-tuple-element.222), channel_id=1, source_target_pairs={{0,24},{8,16},{16,8},{24,0},{1,25},{9,17},{17,9},{25,1},{2,26},{10... | collective-permute-start | bytes 589832 | tf_op jit(solution)/shard_map/ppermute | solution.py:90
  23.0 9.4 %collective-permute-start.7 = (bf16[2,48,1024]{2,1,0:T(8,128)(2,1)S(1)}, bf16[2,48,1024]{2,1,0:T(8,128)(2,1)S(1)}, u32[]{:S(2)}, u32[]{:S(2)}) collective-permute-start(bf16[2,48,1024]{2,1,0:T(8,128)(2,1)S(1)} %get-tuple-element.223), channel_id=1, source_target_pairs={{0,16},{8,24},{16,0},{24,8},{1,17},{9,25},{17,1},{25,9},{2,18},{10... | collective-permute-start | bytes 589832 | tf_op jit(solution)/shard_map/ppermute | solution.py:90
  23.7 8.8 %collective-permute-start.6 = (bf16[2,48,1024]{2,1,0:T(8,128)(2,1)S(1)}, bf16[2,48,1024]{2,1,0:T(8,128)(2,1)S(1)}, u32[]{:S(2)}, u32[]{:S(2)}) collective-permute-start(bf16[2,48,1024]{2,1,0:T(8,128)(2,1)S(1)} %get-tuple-element.224), channel_id=1, source_target_pairs={{0,8},{8,0},{16,24},{24,16},{1,9},{9,1},{17,25},{25,17},{2,10},{10... | collective-permute-start | bytes 589832 | tf_op jit(solution)/shard_map/ppermute | solution.py:90
  25.7 11.0 %collective-permute-start.5 = (bf16[192,768]{1,0:T(8,128)(2,1)S(1)}, bf16[192,768]{1,0:T(8,128)(2,1)S(1)}, u32[]{:S(2)}, u32[]{:S(2)}) collective-permute-start(bf16[192,768]{1,0:T(8,128)(2,1)S(1)} %bitcast.379), channel_id=1, source_target_pairs={{0,3},{1,0},{2,1},{3,2},{4,7},{5,4},{6,5},{7,6},{8,11},{9,8},{10,9... | collective-permute-start | bytes 884744 | tf_op jit(solution)/shard_map/ppermute | solution.py:140
  29.3 11.6 %collective-permute-start.4 = (bf16[192,768]{1,0:T(8,128)(2,1)S(1)}, bf16[192,768]{1,0:T(8,128)(2,1)S(1)}, u32[]{:S(2)}, u32[]{:S(2)}) collective-permute-start(bf16[192,768]{1,0:T(8,128)(2,1)S(1)} %bitcast.380), channel_id=1, source_target_pairs={{0,1},{1,2},{2,3},{3,0},{4,5},{5,6},{6,7},{7,4},{8,9},{9,10},{10,1... | collective-permute-start | bytes 884744 | tf_op jit(solution)/shard_map/ppermute | solution.py:140
  41.7 120.7 %all-gather.4.cloned.1.call-start = ((), (), s32[]{:S(2)}) async-start(), calls=%async_computation.3 | async-start | bytes 3932160 | tf_op jit(solution)/shard_map/all_gather | solution.py:248
  41.8 17.4 %collective-permute-start.11 = (bf16[128,1664]{1,0:T(8,128)(2,1)S(1)}, bf16[128,1664]{1,0:T(8,128)(2,1)}, u32[]{:S(2)}, u32[]{:S(2)}) collective-permute-start(bf16[128,1664]{1,0:T(8,128)(2,1)S(1)} %slice.312), channel_id=1, source_target_pairs={{0,16},{8,24},{16,0},{24,8},{1,17},{9,25},{17,1},{25,9},{2,18},{10... | collective-permute-start | bytes 1277960 | tf_op jit(solution)/shard_map/ppermute | solution.py:90
  43.3 15.9 %collective-permute-start.10 = (bf16[128,1664]{1,0:T(8,128)(2,1)S(1)}, bf16[128,1664]{1,0:T(8,128)(2,1)}, u32[]{:S(2)}, u32[]{:S(2)}) collective-permute-start(bf16[128,1664]{1,0:T(8,128)(2,1)S(1)} %slice.312), channel_id=1, source_target_pairs={{0,8},{8,0},{16,24},{24,16},{1,9},{9,1},{17,25},{25,17},{2,10},{10... | collective-permute-start | bytes 1277960 | tf_op jit(solution)/shard_map/ppermute | solution.py:90
  44.3 22.5 %collective-permute-start.15 = (bf16[128,1664]{1,0:T(8,128)(2,1)S(1)}, bf16[128,1664]{1,0:T(8,128)(2,1)}, u32[]{:S(2)}, u32[]{:S(2)}) collective-permute-start(bf16[128,1664]{1,0:T(8,128)(2,1)S(1)} %slice.312), channel_id=1, source_target_pairs={{0,24},{8,16},{16,8},{24,0},{1,25},{9,17},{17,9},{25,1},{2,26},{10... | collective-permute-start | bytes 1277960 | tf_op jit(solution)/shard_map/ppermute | solution.py:90
  45.5 8.7 %collective-permute-start.13 = (bf16[192,384]{1,0:T(8,128)(2,1)S(1)}, bf16[192,384]{1,0:T(8,128)(2,1)S(1)}, u32[]{:S(2)}, u32[]{:S(2)}) collective-permute-start(bf16[192,384]{1,0:T(8,128)(2,1)S(1)} %slice.316), channel_id=1, source_target_pairs={{0,3},{1,0},{2,1},{3,2},{4,7},{5,4},{6,5},{7,6},{8,11},{9,8},{10,9... | collective-permute-start | bytes 442376 | tf_op jit(solution)/shard_map/ppermute | solution.py:140
  47.3 11.9 %collective-permute-start.12 = (bf16[192,384]{1,0:T(8,128)(2,1)S(1)}, bf16[192,384]{1,0:T(8,128)(2,1)S(1)}, u32[]{:S(2)}, u32[]{:S(2)}) collective-permute-start(bf16[192,384]{1,0:T(8,128)(2,1)S(1)} %slice.315), channel_id=1, source_target_pairs={{0,1},{1,2},{2,3},{3,0},{4,5},{5,6},{6,7},{7,4},{8,9},{9,10},{10,1... | collective-permute-start | bytes 442376 | tf_op jit(solution)/shard_map/ppermute | solution.py:140
  64.7 7.7 %collective-permute-start.14 = (bf16[4,4,48,768]{3,2,1,0:T(8,128)(2,1)}, bf16[4,4,48,768]{3,2,1,0:T(8,128)(2,1)}, u32[]{:S(2)}, u32[]{:S(2)}) collective-permute-start(bf16[4,4,48,768]{3,2,1,0:T(8,128)(2,1)} %constant_dynamic-update-slice_fusion.4), channel_id=1, source_target_pairs={{0,4},{4,0},{1,5},{5,1},{2,6},{6,2},{3,7},{7,3},{8,12},{12,8},{9,1... | collective-permute-start | bytes 3538952 | tf_op jit(solution)/shard_map/ppermute | solution.py:87
  69.2 173.5 %reduce-scatter.4.cloned.1.call-start = ((), (), s32[]{:S(2)}) async-start(), calls=%async_computation.4 | async-start | bytes 1966080 | tf_op jit(solution)/shard_map/reduce_scatter | solution.py:273
  78.7 13.0 %collective-permute-start.18 = (bf16[128,1536]{1,0:T(8,128)(2,1)S(1)}, bf16[128,1536]{1,0:T(8,128)(2,1)S(1)}, u32[]{:S(2)}, u32[]{:S(2)}) collective-permute-start(bf16[128,1536]{1,0:T(8,128)(2,1)S(1)} %slice.318), channel_id=1, source_target_pairs={{0,24},{8,16},{16,8},{24,0},{1,25},{9,17},{17,9},{25,1},{2,26},{10... | collective-permute-start | bytes 1179656 | tf_op jit(solution)/shard_map/ppermute | solution.py:90
  79.8 19.8 %collective-permute-start.17 = (bf16[128,1536]{1,0:T(8,128)(2,1)S(1)}, bf16[128,1536]{1,0:T(8,128)(2,1)}, u32[]{:S(2)}, u32[]{:S(2)}) collective-permute-start(bf16[128,1536]{1,0:T(8,128)(2,1)S(1)} %slice.318), channel_id=1, source_target_pairs={{0,16},{8,24},{16,0},{24,8},{1,17},{9,25},{17,1},{25,9},{2,18},{10... | collective-permute-start | bytes 1179656 | tf_op jit(solution)/shard_map/ppermute | solution.py:90
  81.6 18.0 %collective-permute-start.16 = (bf16[128,1536]{1,0:T(8,128)(2,1)S(1)}, bf16[128,1536]{1,0:T(8,128)(2,1)}, u32[]{:S(2)}, u32[]{:S(2)}) collective-permute-start(bf16[128,1536]{1,0:T(8,128)(2,1)S(1)} %slice.318), channel_id=1, source_target_pairs={{0,8},{8,0},{16,24},{24,16},{1,9},{9,1},{17,25},{25,17},{2,10},{10... | collective-permute-start | bytes 1179656 | tf_op jit(solution)/shard_map/ppermute | solution.py:90
  83.4 17.5 %collective-permute-start.19 = (bf16[192,1536]{1,0:T(8,128)(2,1)S(1)}, bf16[192,1536]{1,0:T(8,128)(2,1)S(1)}, u32[]{:S(2)}, u32[]{:S(2)}) collective-permute-start(bf16[192,1536]{1,0:T(8,128)(2,1)S(1)} %bitcast.360), channel_id=1, source_target_pairs={{0,4},{4,0},{1,5},{5,1},{2,6},{6,2},{3,7},{7,3},{8,12},{12,8},{9,1... | collective-permute-start | bytes 1769480 | tf_op jit(solution)/shard_map/ppermute | solution.py:87
  101.1 23.8 %collective-permute-start.23 = (bf16[512,1536]{1,0:T(8,128)(2,1)S(1)}, bf16[512,1536]{1,0:T(8,128)(2,1)S(1)}, u32[]{:S(2)}, u32[]{:S(2)}) collective-permute-start(bf16[512,1536]{1,0:T(8,128)(2,1)S(1)} %pad_maximum_fusion.5), channel_id=1, source_target_pairs={{0,4},{4,0},{1,5},{5,1},{2,6},{6,2},{3,7},{7,3},{8,12},{12,8},{9,1... | collective-permute-start | bytes 4718600 | tf_op jit(solution)/shard_map/ppermute | solution.py:87
  102.3 12.1 %collective-permute-start.20 = (bf16[128,1536]{1,0:T(8,128)(2,1)S(1)}, bf16[128,1536]{1,0:T(8,128)(2,1)S(1)}, u32[]{:S(2)}, u32[]{:S(2)}) collective-permute-start(bf16[128,1536]{1,0:T(8,128)(2,1)S(1)} %get-tuple-element.191), channel_id=1, source_target_pairs={{0,8},{8,0},{16,24},{24,16},{1,9},{9,1},{17,25},{25,17},{2,10},{10... | collective-permute-start | bytes 1179656 | tf_op jit(solution)/shard_map/ppermute | solution.py:90
  103.8 19.3 %collective-permute-start.22 = (bf16[128,1536]{1,0:T(8,128)(2,1)S(1)}, bf16[128,1536]{1,0:T(8,128)(2,1)S(1)}, u32[]{:S(2)}, u32[]{:S(2)}) collective-permute-start(bf16[128,1536]{1,0:T(8,128)(2,1)S(1)} %get-tuple-element.192), channel_id=1, source_target_pairs={{0,24},{8,16},{16,8},{24,0},{1,25},{9,17},{17,9},{25,1},{2,26},{10... | collective-permute-start | bytes 1179656 | tf_op jit(solution)/shard_map/ppermute | solution.py:90
  105.1 19.4 %collective-permute-start.21 = (bf16[128,1536]{1,0:T(8,128)(2,1)S(1)}, bf16[128,1536]{1,0:T(8,128)(2,1)S(1)}, u32[]{:S(2)}, u32[]{:S(2)}) collective-permute-start(bf16[128,1536]{1,0:T(8,128)(2,1)S(1)} %get-tuple-element.193), channel_id=1, source_target_pairs={{0,16},{8,24},{16,0},{24,8},{1,17},{9,25},{17,1},{25,9},{2,18},{10... | collective-permute-start | bytes 1179656 | tf_op jit(solution)/shard_map/ppermute | solution.py:90
  127.0 13.0 %collective-permute-start.26 = (bf16[128,1536]{1,0:T(8,128)(2,1)S(1)}, bf16[128,1536]{1,0:T(8,128)(2,1)S(1)}, u32[]{:S(2)}, u32[]{:S(2)}) collective-permute-start(bf16[128,1536]{1,0:T(8,128)(2,1)S(1)} %multiply_convert_fusion.3), channel_id=1, source_target_pairs={{0,24},{8,16},{16,8},{24,0},{1,25},{9,17},{17,9},{25,1},{2,26},{10... | collective-permute-start | bytes 1179656 | tf_op jit(solution)/shard_map/ppermute | solution.py:90
  128.7 17.9 %collective-permute-start.25 = (bf16[128,1536]{1,0:T(8,128)(2,1)S(1)}, bf16[128,1536]{1,0:T(8,128)(2,1)S(1)}, u32[]{:S(2)}, u32[]{:S(2)}) collective-permute-start(bf16[128,1536]{1,0:T(8,128)(2,1)S(1)} %multiply_convert_fusion.3), channel_id=1, source_target_pairs={{0,16},{8,24},{16,0},{24,8},{1,17},{9,25},{17,1},{25,9},{2,18},{10... | collective-permute-start | bytes 1179656 | tf_op jit(solution)/shard_map/ppermute | solution.py:90
  129.3 17.3 %collective-permute-start.24 = (bf16[128,1536]{1,0:T(8,128)(2,1)S(1)}, bf16[128,1536]{1,0:T(8,128)(2,1)S(1)}, u32[]{:S(2)}, u32[]{:S(2)}) collective-permute-start(bf16[128,1536]{1,0:T(8,128)(2,1)S(1)} %multiply_convert_fusion.3), channel_id=1, source_target_pairs={{0,8},{8,0},{16,24},{24,16},{1,9},{9,1},{17,25},{25,17},{2,10},{10... | collective-permute-start | bytes 1179656 | tf_op jit(solution)/shard_map/ppermute | solution.py:90
  146.9 8.5 %collective-permute-start.29 = (bf16[64,1536]{1,0:T(8,128)(2,1)S(1)}, bf16[64,1536]{1,0:T(8,128)(2,1)S(1)}, u32[]{:S(2)}, u32[]{:S(2)}) collective-permute-start(bf16[64,1536]{1,0:T(8,128)(2,1)S(1)} %copy-done.29), channel_id=1, source_target_pairs={{0,3},{1,0},{2,1},{3,2},{4,7},{5,4},{6,5},{7,6},{8,11},{9,8},{10,9... | collective-permute-start | bytes 589832 | tf_op jit(solution)/shard_map/ppermute | solution.py:140
  150.0 12.4 %collective-permute-start.28 = (bf16[64,1536]{1,0:T(8,128)(2,1)S(1)}, bf16[64,1536]{1,0:T(8,128)(2,1)}, u32[]{:S(2)}, u32[]{:S(2)}) collective-permute-start(bf16[64,1536]{1,0:T(8,128)(2,1)S(1)} %copy-done.29), channel_id=1, source_target_pairs={{0,1},{1,2},{2,3},{3,0},{4,5},{5,6},{6,7},{7,4},{8,9},{9,10},{10,1... | collective-permute-start | bytes 589832 | tf_op jit(solution)/shard_map/ppermute | solution.py:140
  166.7 7.9 %collective-permute-start.31 = (bf16[64,768]{1,0:T(8,128)(2,1)S(1)}, bf16[64,768]{1,0:T(8,128)(2,1)S(1)}, u32[]{:S(2)}, u32[]{:S(2)}) collective-permute-start(bf16[64,768]{1,0:T(8,128)(2,1)S(1)} %slice.340), channel_id=1, source_target_pairs={{0,3},{1,0},{2,1},{3,2},{4,7},{5,4},{6,5},{7,6},{8,11},{9,8},{10,9... | collective-permute-start | bytes 294920 | tf_op jit(solution)/shard_map/ppermute | solution.py:140
  167.8 6.9 %collective-permute-start.30 = (bf16[64,768]{1,0:T(8,128)(2,1)S(1)}, bf16[64,768]{1,0:T(8,128)(2,1)S(1)}, u32[]{:S(2)}, u32[]{:S(2)}) collective-permute-start(bf16[64,768]{1,0:T(8,128)(2,1)S(1)} %slice.339), channel_id=1, source_target_pairs={{0,1},{1,2},{2,3},{3,0},{4,5},{5,6},{6,7},{7,4},{8,9},{9,10},{10,1... | collective-permute-start | bytes 294920 | tf_op jit(solution)/shard_map/ppermute | solution.py:140
  187.6 100.4 %reduce-scatter.6.cloned.1.call-start = ((), (), s32[]{:S(2)}) async-start(), calls=%async_computation.5 | async-start | bytes 3932160 | tf_op jit(solution)/shard_map/reduce_scatter | solution.py:283
  195.6 12.3 %collective-permute-start.33 = (bf16[128,1536]{1,0:T(8,128)(2,1)S(1)}, bf16[128,1536]{1,0:T(8,128)(2,1)S(1)}, u32[]{:S(2)}, u32[]{:S(2)}) collective-permute-start(bf16[128,1536]{1,0:T(8,128)(2,1)S(1)} %get-tuple-element.188), channel_id=1, source_target_pairs={{0,8},{8,0},{16,24},{24,16},{1,9},{9,1},{17,25},{25,17},{2,10},{10... | collective-permute-start | bytes 1179656 | tf_op jit(solution)/shard_map/ppermute | solution.py:90
  196.5 18.9 %collective-permute-start.35 = (bf16[128,1536]{1,0:T(8,128)(2,1)S(1)}, bf16[128,1536]{1,0:T(8,128)(2,1)S(1)}, u32[]{:S(2)}, u32[]{:S(2)}) collective-permute-start(bf16[128,1536]{1,0:T(8,128)(2,1)S(1)} %get-tuple-element.189), channel_id=1, source_target_pairs={{0,24},{8,16},{16,8},{24,0},{1,25},{9,17},{17,9},{25,1},{2,26},{10... | collective-permute-start | bytes 1179656 | tf_op jit(solution)/shard_map/ppermute | solution.py:90
  197.7 19.0 %collective-permute-start.34 = (bf16[128,1536]{1,0:T(8,128)(2,1)S(1)}, bf16[128,1536]{1,0:T(8,128)(2,1)S(1)}, u32[]{:S(2)}, u32[]{:S(2)}) collective-permute-start(bf16[128,1536]{1,0:T(8,128)(2,1)S(1)} %get-tuple-element.190), channel_id=1, source_target_pairs={{0,16},{8,24},{16,0},{24,8},{1,17},{9,25},{17,1},{25,9},{2,18},{10... | collective-permute-start | bytes 1179656 | tf_op jit(solution)/shard_map/ppermute | solution.py:90
  207.9 30.3 %collective-permute-start.39 = (bf16[512,1536]{1,0:T(8,128)(2,1)}, bf16[512,1536]{1,0:T(8,128)(2,1)}, u32[]{:S(2)}, u32[]{:S(2)}) collective-permute-start(bf16[512,1536]{1,0:T(8,128)(2,1)} %convolution_convert_fusion.2), channel_id=1, source_target_pairs={{0,4},{4,0},{1,5},{5,1},{2,6},{6,2},{3,7},{7,3},{8,12},{12,8},{9,1... | collective-permute-start | bytes 4718600 | tf_op jit(solution)/shard_map/ppermute | solution.py:87
  217.4 13.0 %collective-permute-start.38 = (bf16[128,1536]{1,0:T(8,128)(2,1)S(1)}, bf16[128,1536]{1,0:T(8,128)(2,1)S(1)}, u32[]{:S(2)}, u32[]{:S(2)}) collective-permute-start(bf16[128,1536]{1,0:T(8,128)(2,1)S(1)} %fusion.86), channel_id=1, source_target_pairs={{0,24},{8,16},{16,8},{24,0},{1,25},{9,17},{17,9},{25,1},{2,26},{10... | collective-permute-start | bytes 1179656 | tf_op jit(solution)/shard_map/ppermute | solution.py:90
  219.1 16.6 %collective-permute-start.37 = (bf16[128,1536]{1,0:T(8,128)(2,1)S(1)}, bf16[128,1536]{1,0:T(8,128)(2,1)}, u32[]{:S(2)}, u32[]{:S(2)}) collective-permute-start(bf16[128,1536]{1,0:T(8,128)(2,1)S(1)} %fusion.86), channel_id=1, source_target_pairs={{0,16},{8,24},{16,0},{24,8},{1,17},{9,25},{17,1},{25,9},{2,18},{10... | collective-permute-start | bytes 1179656 | tf_op jit(solution)/shard_map/ppermute | solution.py:90
  220.5 15.2 %collective-permute-start.36 = (bf16[128,1536]{1,0:T(8,128)(2,1)S(1)}, bf16[128,1536]{1,0:T(8,128)(2,1)}, u32[]{:S(2)}, u32[]{:S(2)}) collective-permute-start(bf16[128,1536]{1,0:T(8,128)(2,1)S(1)} %fusion.86), channel_id=1, source_target_pairs={{0,8},{8,0},{16,24},{24,16},{1,9},{9,1},{17,25},{25,17},{2,10},{10... | collective-permute-start | bytes 1179656 | tf_op jit(solution)/shard_map/ppermute | solution.py:90
  221.0 105.8 %reduce-scatter.8.cloned.1.call-start = ((), (), s32[]{:S(2)}) async-start(), calls=%async_computation.6 | async-start | bytes 2211840 | tf_op jit(solution)/shard_map/reduce_scatter | solution.py:323
  264.4 12.3 %collective-permute-start.42 = (bf16[128,1536]{1,0:T(8,128)(2,1)}, bf16[128,1536]{1,0:T(8,128)(2,1)}, u32[]{:S(2)}, u32[]{:S(2)}) collective-permute-start(bf16[128,1536]{1,0:T(8,128)(2,1)} %get-tuple-element.185), channel_id=1, source_target_pairs={{0,8},{8,0},{16,24},{24,16},{1,9},{9,1},{17,25},{25,17},{2,10},{10... | collective-permute-start | bytes 1179656 | tf_op jit(solution)/shard_map/ppermute | solution.py:90
  266.1 19.1 %collective-permute-start.44 = (bf16[128,1536]{1,0:T(8,128)(2,1)S(1)}, bf16[128,1536]{1,0:T(8,128)(2,1)}, u32[]{:S(2)}, u32[]{:S(2)}) collective-permute-start(bf16[128,1536]{1,0:T(8,128)(2,1)S(1)} %get-tuple-element.186), channel_id=1, source_target_pairs={{0,24},{8,16},{16,8},{24,0},{1,25},{9,17},{17,9},{25,1},{2,26},{10... | collective-permute-start | bytes 1179656 | tf_op jit(solution)/shard_map/ppermute | solution.py:90
  267.3 19.0 %collective-permute-start.43 = (bf16[128,1536]{1,0:T(8,128)(2,1)S(1)}, bf16[128,1536]{1,0:T(8,128)(2,1)}, u32[]{:S(2)}, u32[]{:S(2)}) collective-permute-start(bf16[128,1536]{1,0:T(8,128)(2,1)S(1)} %get-tuple-element.187), channel_id=1, source_target_pairs={{0,16},{8,24},{16,0},{24,8},{1,17},{9,25},{17,1},{25,9},{2,18},{10... | collective-permute-start | bytes 1179656 | tf_op jit(solution)/shard_map/ppermute | solution.py:90
  290.5 12.1 %collective-permute-start.45 = (bf16[128,1536]{1,0:T(8,128)(2,1)S(1)}, bf16[128,1536]{1,0:T(8,128)(2,1)S(1)}, u32[]{:S(2)}, u32[]{:S(2)}) collective-permute-start(bf16[128,1536]{1,0:T(8,128)(2,1)S(1)} %get-tuple-element.196), channel_id=1, source_target_pairs={{0,8},{8,0},{16,24},{24,16},{1,9},{9,1},{17,25},{25,17},{2,10},{10... | collective-permute-start | bytes 1179656 | tf_op jit(solution)/shard_map/ppermute | solution.py:90
  291.4 19.6 %collective-permute-start.47 = (bf16[128,1536]{1,0:T(8,128)(2,1)S(1)}, bf16[128,1536]{1,0:T(8,128)(2,1)S(1)}, u32[]{:S(2)}, u32[]{:S(2)}) collective-permute-start(bf16[128,1536]{1,0:T(8,128)(2,1)S(1)} %get-tuple-element.197), channel_id=1, source_target_pairs={{0,24},{8,16},{16,8},{24,0},{1,25},{9,17},{17,9},{25,1},{2,26},{10... | collective-permute-start | bytes 1179656 | tf_op jit(solution)/shard_map/ppermute | solution.py:90
  292.6 20.4 %collective-permute-start.46 = (bf16[128,1536]{1,0:T(8,128)(2,1)S(1)}, bf16[128,1536]{1,0:T(8,128)(2,1)S(1)}, u32[]{:S(2)}, u32[]{:S(2)}) collective-permute-start(bf16[128,1536]{1,0:T(8,128)(2,1)S(1)} %get-tuple-element.198), channel_id=1, source_target_pairs={{0,16},{8,24},{16,0},{24,8},{1,17},{9,25},{17,1},{25,9},{2,18},{10... | collective-permute-start | bytes 1179656 | tf_op jit(solution)/shard_map/ppermute | solution.py:90
  294.5 20.7 %collective-permute-start.49 = (bf16[2,48,1024]{2,1,0:T(8,128)(2,1)S(1)}, bf16[2,48,1024]{2,1,0:T(8,128)(2,1)S(1)}, u32[]{:S(2)}, u32[]{:S(2)}) collective-permute-start(bf16[2,48,1024]{2,1,0:T(8,128)(2,1)S(1)} %get-tuple-element.218), channel_id=1, source_target_pairs={{0,8},{8,0},{16,24},{24,16},{1,9},{9,1},{17,25},{25,17},{2,10},{10... | collective-permute-start | bytes 589832 | tf_op jit(solution)/shard_map/ppermute | solution.py:90
  295.4 25.0 %collective-permute-start.50 = (bf16[2,48,1024]{2,1,0:T(8,128)(2,1)S(1)}, bf16[2,48,1024]{2,1,0:T(8,128)(2,1)S(1)}, u32[]{:S(2)}, u32[]{:S(2)}) collective-permute-start(bf16[2,48,1024]{2,1,0:T(8,128)(2,1)S(1)} %get-tuple-element.219), channel_id=1, source_target_pairs={{0,16},{8,24},{16,0},{24,8},{1,17},{9,25},{17,1},{25,9},{2,18},{10... | collective-permute-start | bytes 589832 | tf_op jit(solution)/shard_map/ppermute | solution.py:90
  302.5 17.9 %collective-permute-start.51 = (bf16[2,48,1024]{2,1,0:T(8,128)(2,1)S(1)}, bf16[2,48,1024]{2,1,0:T(8,128)(2,1)S(1)}, u32[]{:S(2)}, u32[]{:S(2)}) collective-permute-start(bf16[2,48,1024]{2,1,0:T(8,128)(2,1)S(1)} %get-tuple-element.220), channel_id=1, source_target_pairs={{0,24},{8,16},{16,8},{24,0},{1,25},{9,17},{17,9},{25,1},{2,26},{10... | collective-permute-start | bytes 589832 | tf_op jit(solution)/shard_map/ppermute | solution.py:90
  315.0 11.9 %collective-permute-start.53 = (bf16[64,1536]{1,0:T(8,128)(2,1)}, bf16[64,1536]{1,0:T(8,128)(2,1)}, u32[]{:S(2)}, u32[]{:S(2)}) collective-permute-start(bf16[64,1536]{1,0:T(8,128)(2,1)} %slice.438), channel_id=1, source_target_pairs={{0,4},{4,0},{1,5},{5,1},{2,6},{6,2},{3,7},{7,3},{8,12},{12,8},{9,1... | collective-permute-start | bytes 589832 | tf_op jit(solution)/shard_map/ppermute | solution.py:87
  (71 other events, 357.7 us)
Sparse Core Ops, SparseCore 0:
  41.9 35.7 all-gather.5
  79.8 62.9 all-gather.3
  187.7 35.7 reduce-scatter.3
  225.7 59.2 reduce-scatter.5
  287.1 38.4 reduce-scatter.7

commit v2 on v1

--- a/solution.py
+++ b/solution.py
@@ -240,21 +240,19 @@
     soft_low = soft.astype(bf16)
     mixed = jnp.einsum("grst,tgh->sgrh", soft_low, value, preferred_element_type=f32)
     mixed = mixed.astype(bf16).reshape(seq, q_cols)
-    mixed, dy_all, out_w = tie(mixed, dy_all, out_w)
+    mixed, out_w = tie(mixed, out_w)
     x_own = x_low.astype(f32)
     middle = x_own + scatter_chips(mm(mixed, out_w))
 
     dy_both = jnp.concatenate([dy_all, core_swap(dy_all)])
     along_gu = lax.all_gather(piece_gu, "fsdp", axis=0, tiled=True)
-    middle, dy_both = tie(middle, dy_both)
+    middle, dy_both, upper = tie(middle, dy_both, upper)
+    upper_right, upper_left = ring_first(upper)
     scale_two = rms_scale(middle)
     n_two = middle * scale_two
     h_two = gather_chips(n_two.astype(bf16))
-    h_two, upper = tie(h_two, upper)
-    upper_right, upper_left = ring_first(upper)
-    h_both, along_gu, upper_right, upper_left = tie(
-        jnp.concatenate([h_two, core_swap(h_two)]), along_gu, upper_right, upper_left
-    )
+    h_two, upper_right, upper_left = tie(h_two, upper_right, upper_left)
+    h_both, along_gu = tie(jnp.concatenate([h_two, core_swap(h_two)]), along_gu)
     along_upper = assemble(ring_rest(upper, upper_right, upper_left), 1)[0]
     along_down = jnp.concatenate([rows[:, w_out.shape[0] :], along_upper], axis=1)
     along_down = along_down.reshape(-1, width)

time: 352 us -> 347 us (0.986)
  waiting for transfers between devices: 146 us -> 138 us
    ppermute x8, waiting for transfers between devices: 29 us -> 22 us  [along_z(): lax.ppermute(a, 'fsdp', [(i, (i + step) % rows_z) for i in range(rows_z)])]
    unnamed x121 -> x117, local copies, waits for them, and re-layouts: 13 us -> 14.8 us
  transfers between devices with their start and end apart: 62 -> 62, of which waited for: 36 -> 35; matrix products, arithmetic and copies ran while one was open for 27% -> 27% of each run, Pallas kernels for 0% -> 0%
where the time goes in v2:
time: 347 us; the launch traced here: 342 us
  waiting for transfers between devices  138 us (40%)
  starting transfers between devices  58.7 us (17%)
  matrix products  47.6 us (14%)
  other arithmetic  42.4 us (12%)
  local copies, waits for them, and re-layouts  39.8 us (11%)
  between operations  15.6 us (4%)
    ppermute x36, waiting for transfers between devices, chip_xor(): return lax.ppermute(a, 'chip', [(i, i ^ j) for i in range(chips)])  113 us
    ppermute x36, starting transfers between devices, chip_xor(): return lax.ppermute(a, 'chip', [(i, i ^ j) for i in range(chips)])  44.1 us
    ppermute x8, waiting for transfers between devices, along_z(): lax.ppermute(a, 'fsdp', [(i, (i + step) % rows_z) for i in range(rows_z)])  22 us
    dot_general x5, matrix products, mm_nt(): return jnp.einsum('te,de->td', a, b, preferred_element_type=f32)  17.3 us
    unnamed x117, local copies, waits for them, and re-layouts  14.8 us
    ppermute x8, starting transfers between devices, along_z(): lax.ppermute(a, 'fsdp', [(i, (i + step) % rows_z) for i in range(rows_z)])  13 us
    dot_general x5, matrix products, mm(): return jnp.dot(a, b, preferred_element_type=f32)  10.7 us
    dot_general x4, matrix products, mm_tn(): return jnp.einsum('td,te->de', a, b, preferred_element_type=f32)  9.17 us
  transfers between devices with their start and end apart: 62, of which 35 were waited for; matrix products, arithmetic and copies ran while one was open for 27% of the time, Pallas kernels for 0%

profile of v2, /device:TPU:0, one launch (start us, length us, event | category | flops | bytes accessed | tf_op | source)
XLA Modules:
  0.0 342.4 jit_solution(7077514456010231613)
XLA Ops:
  10.6 4.0 %collective-permute-start.3 = (bf16[48,768]{1,0:T(8,128)(2,1)S(1)}, bf16[48,768]{1,0:T(8,128)(2,1)S(1)}, u32[]{:S(2)}, u32[]{:S(2)}) collective-permute-start(bf16[48,768]{1,0:T(8,128)(2,1)S(1)} %get-tuple-element.262), channel_id=1, source_target_pairs={{0,24},{8,16},{16,8},{24,0},{1,25},{9,17},{17,9},{25,1},{2,26},{10... | collective-permute-start | bytes 221192 | tf_op jit(solution)/shard_map/ppermute | solution.py:90
  17.0 2.0 collective-permute-done.2
  25.7 3.6 %collective-permute-start.5 = (bf16[192,768]{1,0:T(8,128)(2,1)S(1)}, bf16[192,768]{1,0:T(8,128)(2,1)S(1)}, u32[]{:S(2)}, u32[]{:S(2)}) collective-permute-start(bf16[192,768]{1,0:T(8,128)(2,1)S(1)} %bitcast.379), channel_id=1, source_target_pairs={{0,3},{1,0},{2,1},{3,2},{4,7},{5,4},{6,5},{7,6},{8,11},{9,8},{10,9... | collective-permute-start | bytes 884744 | tf_op jit(solution)/shard_map/ppermute | solution.py:140
  30.3 2.1 collective-permute-done.7
  33.0 3.7 %collective-permute-done.5 = bf16[192,768]{1,0:T(8,128)(2,1)S(1)} collective-permute-done((bf16[192,768]{1,0:T(8,128)(2,1)S(1)}, bf16[192,768]{1,0:T(8,128)(2,1)S(1)}, u32[]{:S(2)}, u32[]{:S(2)}) %collective-permute-start.5) | collective-permute-done | bytes 294944 | tf_op jit(solution)/shard_map/ppermute | solution.py:140
  36.7 4.2 %collective-permute-done.4 = bf16[192,768]{1,0:T(8,128)(2,1)S(1)} collective-permute-done((bf16[192,768]{1,0:T(8,128)(2,1)S(1)}, bf16[192,768]{1,0:T(8,128)(2,1)S(1)}, u32[]{:S(2)}, u32[]{:S(2)}) %collective-permute-start.4) | collective-permute-done | bytes 294944 | tf_op jit(solution)/shard_map/ppermute | solution.py:140
  45.5 1.8 collective-permute-start.13
  49.7 4.5 %collective-permute-done.13 = bf16[192,384]{1,0:T(8,128)(2,1)S(1)} collective-permute-done((bf16[192,384]{1,0:T(8,128)(2,1)S(1)}, bf16[192,384]{1,0:T(8,128)(2,1)S(1)}, u32[]{:S(2)}, u32[]{:S(2)}) %collective-permute-start.13) | collective-permute-done | bytes 147488 | tf_op jit(solution)/shard_map/ppermute | solution.py:140
  54.2 5.0 %collective-permute-done.12 = bf16[192,384]{1,0:T(8,128)(2,1)S(1)} collective-permute-done((bf16[192,384]{1,0:T(8,128)(2,1)S(1)}, bf16[192,384]{1,0:T(8,128)(2,1)S(1)}, u32[]{:S(2)}, u32[]{:S(2)}) %collective-permute-start.12) | collective-permute-done | bytes 147488 | tf_op jit(solution)/shard_map/ppermute | solution.py:140
  79.6 1.8 collective-permute-start.21
  83.3 4.8 %fusion.98 = (f32[2,2,512]{2,1,0:T(2,128)S(1)}, f32[2,2,512,512]{2,3,1,0:T(8,128)}) fusion(pred[512,512]{0,1:T(8,128)(4,1)} %compare_and_fusion, bf16[512,2,2,96]{0,3,2,1:T(8,128)(2,1)S(1)} %pad_maximum_fusion.14, bf16[512,2,48]{0,2,1:T(8,128)(2,1)} %get-tuple-element.232, bf16[512,2,48]{0,2,1:T(8,128)(2,1)S(1)} %get-tuple-element.231), kind=kOutput, calls=%fused_computation.288 | convolution fusion | flops 205914624 | bytes 5054464 | tf_op jit(solution)/shard_map/sub | solution.py:238
  88.1 2.9 convolution_convert_fusion.6
  91.6 7.8 %collective-permute-done.21 = bf16[128,1536]{1,0:T(8,128)(2,1)S(1)} collective-permute-done((bf16[128,1536]{1,0:T(8,128)(2,1)S(1)}, bf16[128,1536]{1,0:T(8,128)(2,1)S(1)}, u32[]{:S(2)}, u32[]{:S(2)}) %collective-permute-start.21) | collective-permute-done | bytes 393248 | tf_op jit(solution)/shard_map/ppermute | solution.py:90
  105.6 8.4 %collective-permute-done.17 = bf16[128,1536]{1,0:T(8,128)(2,1)S(1)} collective-permute-done((bf16[128,1536]{1,0:T(8,128)(2,1)S(1)}, bf16[128,1536]{1,0:T(8,128)(2,1)S(1)}, u32[]{:S(2)}, u32[]{:S(2)}) %collective-permute-start.17) | collective-permute-done | bytes 393248 | tf_op jit(solution)/shard_map/ppermute | solution.py:90
  114.1 8.8 %collective-permute-done.19 = bf16[128,1536]{1,0:T(8,128)(2,1)S(1)} collective-permute-done((bf16[128,1536]{1,0:T(8,128)(2,1)S(1)}, bf16[128,1536]{1,0:T(8,128)(2,1)S(1)}, u32[]{:S(2)}, u32[]{:S(2)}) %collective-permute-start.19) | collective-permute-done | bytes 393248 | tf_op jit(solution)/shard_map/ppermute | solution.py:90
  125.5 3.1 collective-permute-start.28
  132.6 9.3 %collective-permute-done.26 = bf16[128,1536]{1,0:T(8,128)(2,1)S(1)} collective-permute-done((bf16[128,1536]{1,0:T(8,128)(2,1)S(1)}, bf16[128,1536]{1,0:T(8,128)(2,1)S(1)}, u32[]{:S(2)}, u32[]{:S(2)}) %collective-permute-start.26) | collective-permute-done | bytes 393248 | tf_op jit(solution)/shard_map/ppermute | solution.py:90
  141.9 6.2 %collective-permute-done.25 = bf16[128,1536]{1,0:T(8,128)(2,1)S(1)} collective-permute-done((bf16[128,1536]{1,0:T(8,128)(2,1)S(1)}, bf16[128,1536]{1,0:T(8,128)(2,1)S(1)}, u32[]{:S(2)}, u32[]{:S(2)}) %collective-permute-start.25) | collective-permute-done | bytes 393248 | tf_op jit(solution)/shard_map/ppermute | solution.py:90
  150.4 3.2 collective-permute-start.31
  153.6 2.7 collective-permute-done.30
  158.3 1.9 pad_maximum_fusion
  160.2 2.4 copy.75
  163.1 3.6 %fusion.100 = f32[1024,1024]{0,1:T(8,128)S(1)} fusion(bf16[1024,1536]{1,0:T(8,128)(2,1)S(1)} %copy-done.7, bf16[1536,1024]{1,0:T(8,128)(2,1)S(1)} %bitcast.337), kind=kOutput, calls=%fused_computation.290 | convolution fusion | flops 3221225472 | bytes 10485760 | tf_op jit(solution)/shard_map/dot_general | solution.py:46
  166.7 3.9 %multiply_convert_fusion.1 = (bf16[1024,512]{0,1:T(8,128)(2,1)}, bf16[1024,512]{0,1:T(8,128)(2,1)}, bf16[1024,512]{0,1:T(8,128)(2,1)S(1)}) fusion(f32[1024,1024]{0,1:T(8,128)S(1)} %fusion.100, bf16[1024,1536]{1,0:T(8,128)(2,1)S(1)} %copy-done.47, bf16[512,1536]{1,0:T(8,128)(2,1)S(1)} %bitcast.330), kind=kOutput, calls=%fused_computation.26 | convolution fusion | flops 1619001344 | bytes 12058624 | tf_op jit(solution)/shard_map/te,de->td/dot_general | solution.py:54
  171.6 3.0 convolution_convert_fusion.4
  174.6 1.9 pad_maximum_fusion.2
  177.1 3.1 convolution_convert_fusion.3
  180.7 3.2 collective-permute-done.32
  183.9 4.5 %convert_add_fusion.1 = f32[512,1536]{1,0:T(8,128)S(1)} fusion(bf16[512,1536]{1,0:T(8,128)(2,1)} %collective-permute-done.32, bf16[1536,1024]{1,0:T(8,128)(2,1)} %bitcast.338, bf16[1024,1024]{0,1:T(8,128)(2,1)} %copy-done.15), kind=kOutput, calls=%fused_computation.17 | convolution fusion | flops 1612185600 | bytes 8912896 | tf_op jit(solution)/shard_map/te,de->td/dot_general | solution.py:54
  192.3 3.8 %convolution_convert_fusion = bf16[1536,1024]{1,0:T(8,128)(2,1)S(1)} fusion(bf16[1024,1536]{1,0:T(8,128)(2,1)S(1)} %copy-done.8, bf16[1024,1024]{0,1:T(8,128)(2,1)S(1)} %copy-done.16), kind=kOutput, calls=%fused_computation.10 | convolution fusion | flops 3222798336 | bytes 8388608 | tf_op jit(solution)/shard_map/td,te->de/dot_general | solution.py:50
  196.1 2.0 copy.76
  198.8 2.3 convolution_convert_fusion.2
  201.1 7.5 %collective-permute-done.35 = bf16[128,1536]{1,0:T(8,128)(2,1)S(1)} collective-permute-done((bf16[128,1536]{1,0:T(8,128)(2,1)S(1)}, bf16[128,1536]{1,0:T(8,128)(2,1)S(1)}, u32[]{:S(2)}, u32[]{:S(2)}) %collective-permute-start.35) | collective-permute-done | bytes 393248 | tf_op jit(solution)/shard_map/ppermute | solution.py:90
  210.6 1.8 collective-permute-start.38
  214.4 9.2 %collective-permute-done.38 = bf16[128,1536]{1,0:T(8,128)(2,1)} collective-permute-done((bf16[128,1536]{1,0:T(8,128)(2,1)S(1)}, bf16[128,1536]{1,0:T(8,128)(2,1)}, u32[]{:S(2)}, u32[]{:S(2)}) %collective-permute-start.38) | collective-permute-done | bytes 393248 | tf_op jit(solution)/shard_map/ppermute | solution.py:90
  223.6 5.3 %collective-permute-done.37 = bf16[128,1536]{1,0:T(8,128)(2,1)} collective-permute-done((bf16[128,1536]{1,0:T(8,128)(2,1)S(1)}, bf16[128,1536]{1,0:T(8,128)(2,1)}, u32[]{:S(2)}, u32[]{:S(2)}) %collective-permute-start.37) | collective-permute-done | bytes 393248 | tf_op jit(solution)/shard_map/ppermute | solution.py:90
  229.0 2.5 pad_maximum_fusion.7
  231.4 2.4 convert_add_fusion
  236.0 2.7 convolution_convert_fusion.7
  250.2 3.1 fusion.101
  254.8 2.1 convert.86
  262.2 7.8 %collective-permute-done.42 = bf16[128,1536]{1,0:T(8,128)(2,1)} collective-permute-done((bf16[128,1536]{1,0:T(8,128)(2,1)}, bf16[128,1536]{1,0:T(8,128)(2,1)}, u32[]{:S(2)}, u32[]{:S(2)}) %collective-permute-start.42) | collective-permute-done | bytes 393248 | tf_op jit(solution)/shard_map/ppermute | solution.py:90
  270.0 8.4 %collective-permute-done.44 = bf16[128,1536]{1,0:T(8,128)(2,1)} collective-permute-done((bf16[128,1536]{1,0:T(8,128)(2,1)S(1)}, bf16[128,1536]{1,0:T(8,128)(2,1)}, u32[]{:S(2)}, u32[]{:S(2)}) %collective-permute-start.44) | collective-permute-done | bytes 393248 | tf_op jit(solution)/shard_map/ppermute | solution.py:90
  290.0 5.8 %collective-permute-done.45 = bf16[128,1536]{1,0:T(8,128)(2,1)S(1)} collective-permute-done((bf16[128,1536]{1,0:T(8,128)(2,1)S(1)}, bf16[128,1536]{1,0:T(8,128)(2,1)S(1)}, u32[]{:S(2)}, u32[]{:S(2)}) %collective-permute-start.45) | collective-permute-done | bytes 393248 | tf_op jit(solution)/shard_map/ppermute | solution.py:90
  297.4 6.9 %collective-permute-done.47 = bf16[128,1536]{1,0:T(8,128)(2,1)S(1)} collective-permute-done((bf16[128,1536]{1,0:T(8,128)(2,1)S(1)}, bf16[128,1536]{1,0:T(8,128)(2,1)S(1)}, u32[]{:S(2)}, u32[]{:S(2)}) %collective-permute-start.47) | collective-permute-done | bytes 393248 | tf_op jit(solution)/shard_map/ppermute | solution.py:90
  304.3 2.0 collective-permute-done.46
  308.5 5.2 %collective-permute-done.50 = bf16[2,48,1024]{2,1,0:T(8,128)(2,1)S(1)} collective-permute-done((bf16[2,48,1024]{2,1,0:T(8,128)(2,1)S(1)}, bf16[2,48,1024]{2,1,0:T(8,128)(2,1)S(1)}, u32[]{:S(2)}, u32[]{:S(2)}) %collective-permute-start.50) | collective-permute-done | bytes 196640 | tf_op jit(solution)/shard_map/ppermute | solution.py:90
  324.8 1.8 collective-permute-start.56
  (381 shorter events, 126.9 us)
Async XLA Ops:
  7.2 71.3 %all-gather.6.cloned.1.call-start = ((), (), s32[]{:S(2)}) async-start(), calls=%async_computation.7 | async-start | bytes 1720320 | tf_op jit(solution)/shard_map/all_gather | solution.py:198
  21.5 8.8 %collective-permute-start.8 = (bf16[2,48,1024]{2,1,0:T(8,128)(2,1)}, bf16[2,48,1024]{2,1,0:T(8,128)(2,1)S(1)}, u32[]{:S(2)}, u32[]{:S(2)}) collective-permute-start(bf16[2,48,1024]{2,1,0:T(8,128)(2,1)} %get-tuple-element.220), channel_id=1, source_target_pairs={{0,24},{8,16},{16,8},{24,0},{1,25},{9,17},{17,9},{25,1},{2,26},{10... | collective-permute-start | bytes 589832 | tf_op jit(solution)/shard_map/ppermute | solution.py:90
  23.0 9.4 %collective-permute-start.7 = (bf16[2,48,1024]{2,1,0:T(8,128)(2,1)S(1)}, bf16[2,48,1024]{2,1,0:T(8,128)(2,1)S(1)}, u32[]{:S(2)}, u32[]{:S(2)}) collective-permute-start(bf16[2,48,1024]{2,1,0:T(8,128)(2,1)S(1)} %get-tuple-element.221), channel_id=1, source_target_pairs={{0,16},{8,24},{16,0},{24,8},{1,17},{9,25},{17,1},{25,9},{2,18},{10... | collective-permute-start | bytes 589832 | tf_op jit(solution)/shard_map/ppermute | solution.py:90
  23.7 8.8 %collective-permute-start.6 = (bf16[2,48,1024]{2,1,0:T(8,128)(2,1)S(1)}, bf16[2,48,1024]{2,1,0:T(8,128)(2,1)S(1)}, u32[]{:S(2)}, u32[]{:S(2)}) collective-permute-start(bf16[2,48,1024]{2,1,0:T(8,128)(2,1)S(1)} %get-tuple-element.222), channel_id=1, source_target_pairs={{0,8},{8,0},{16,24},{24,16},{1,9},{9,1},{17,25},{25,17},{2,10},{10... | collective-permute-start | bytes 589832 | tf_op jit(solution)/shard_map/ppermute | solution.py:90
  25.7 11.0 %collective-permute-start.5 = (bf16[192,768]{1,0:T(8,128)(2,1)S(1)}, bf16[192,768]{1,0:T(8,128)(2,1)S(1)}, u32[]{:S(2)}, u32[]{:S(2)}) collective-permute-start(bf16[192,768]{1,0:T(8,128)(2,1)S(1)} %bitcast.379), channel_id=1, source_target_pairs={{0,3},{1,0},{2,1},{3,2},{4,7},{5,4},{6,5},{7,6},{8,11},{9,8},{10,9... | collective-permute-start | bytes 884744 | tf_op jit(solution)/shard_map/ppermute | solution.py:140
  29.3 11.6 %collective-permute-start.4 = (bf16[192,768]{1,0:T(8,128)(2,1)S(1)}, bf16[192,768]{1,0:T(8,128)(2,1)S(1)}, u32[]{:S(2)}, u32[]{:S(2)}) collective-permute-start(bf16[192,768]{1,0:T(8,128)(2,1)S(1)} %bitcast.380), channel_id=1, source_target_pairs={{0,1},{1,2},{2,3},{3,0},{4,5},{5,6},{6,7},{7,4},{8,9},{9,10},{10,1... | collective-permute-start | bytes 884744 | tf_op jit(solution)/shard_map/ppermute | solution.py:140
  41.7 118.5 %all-gather.4.cloned.1.call-start = ((), (), s32[]{:S(2)}) async-start(), calls=%async_computation.3 | async-start | bytes 3932160 | tf_op jit(solution)/shard_map/all_gather | solution.py:248
  41.8 17.4 %collective-permute-start.11 = (bf16[128,1664]{1,0:T(8,128)(2,1)S(1)}, bf16[128,1664]{1,0:T(8,128)(2,1)}, u32[]{:S(2)}, u32[]{:S(2)}) collective-permute-start(bf16[128,1664]{1,0:T(8,128)(2,1)S(1)} %slice.312), channel_id=1, source_target_pairs={{0,16},{8,24},{16,0},{24,8},{1,17},{9,25},{17,1},{25,9},{2,18},{10... | collective-permute-start | bytes 1277960 | tf_op jit(solution)/shard_map/ppermute | solution.py:90
  43.3 15.9 %collective-permute-start.10 = (bf16[128,1664]{1,0:T(8,128)(2,1)S(1)}, bf16[128,1664]{1,0:T(8,128)(2,1)}, u32[]{:S(2)}, u32[]{:S(2)}) collective-permute-start(bf16[128,1664]{1,0:T(8,128)(2,1)S(1)} %slice.312), channel_id=1, source_target_pairs={{0,8},{8,0},{16,24},{24,16},{1,9},{9,1},{17,25},{25,17},{2,10},{10... | collective-permute-start | bytes 1277960 | tf_op jit(solution)/shard_map/ppermute | solution.py:90
  44.3 22.4 %collective-permute-start.15 = (bf16[128,1664]{1,0:T(8,128)(2,1)S(1)}, bf16[128,1664]{1,0:T(8,128)(2,1)}, u32[]{:S(2)}, u32[]{:S(2)}) collective-permute-start(bf16[128,1664]{1,0:T(8,128)(2,1)S(1)} %slice.312), channel_id=1, source_target_pairs={{0,24},{8,16},{16,8},{24,0},{1,25},{9,17},{17,9},{25,1},{2,26},{10... | collective-permute-start | bytes 1277960 | tf_op jit(solution)/shard_map/ppermute | solution.py:90
  45.5 8.7 %collective-permute-start.13 = (bf16[192,384]{1,0:T(8,128)(2,1)S(1)}, bf16[192,384]{1,0:T(8,128)(2,1)S(1)}, u32[]{:S(2)}, u32[]{:S(2)}) collective-permute-start(bf16[192,384]{1,0:T(8,128)(2,1)S(1)} %slice.316), channel_id=1, source_target_pairs={{0,3},{1,0},{2,1},{3,2},{4,7},{5,4},{6,5},{7,6},{8,11},{9,8},{10,9... | collective-permute-start | bytes 442376 | tf_op jit(solution)/shard_map/ppermute | solution.py:140
  47.3 11.9 %collective-permute-start.12 = (bf16[192,384]{1,0:T(8,128)(2,1)S(1)}, bf16[192,384]{1,0:T(8,128)(2,1)S(1)}, u32[]{:S(2)}, u32[]{:S(2)}) collective-permute-start(bf16[192,384]{1,0:T(8,128)(2,1)S(1)} %slice.315), channel_id=1, source_target_pairs={{0,1},{1,2},{2,3},{3,0},{4,5},{5,6},{6,7},{7,4},{8,9},{9,10},{10,1... | collective-permute-start | bytes 442376 | tf_op jit(solution)/shard_map/ppermute | solution.py:140
  64.6 7.7 %collective-permute-start.14 = (bf16[4,4,48,768]{3,2,1,0:T(8,128)(2,1)}, bf16[4,4,48,768]{3,2,1,0:T(8,128)(2,1)}, u32[]{:S(2)}, u32[]{:S(2)}) collective-permute-start(bf16[4,4,48,768]{3,2,1,0:T(8,128)(2,1)} %constant_dynamic-update-slice_fusion.9), channel_id=1, source_target_pairs={{0,4},{4,0},{1,5},{5,1},{2,6},{6,2},{3,7},{7,3},{8,12},{12,8},{9,1... | collective-permute-start | bytes 3538952 | tf_op jit(solution)/shard_map/ppermute | solution.py:87
  69.1 166.9 %reduce-scatter.4.cloned.1.call-start = ((), (), s32[]{:S(2)}) async-start(), calls=%async_computation.4 | async-start | bytes 1966080 | tf_op jit(solution)/shard_map/reduce_scatter | solution.py:271
  78.6 13.0 %collective-permute-start.22 = (bf16[128,1536]{1,0:T(8,128)(2,1)S(1)}, bf16[128,1536]{1,0:T(8,128)(2,1)S(1)}, u32[]{:S(2)}, u32[]{:S(2)}) collective-permute-start(bf16[128,1536]{1,0:T(8,128)(2,1)S(1)} %slice.318), channel_id=1, source_target_pairs={{0,24},{8,16},{16,8},{24,0},{1,25},{9,17},{17,9},{25,1},{2,26},{10... | collective-permute-start | bytes 1179656 | tf_op jit(solution)/shard_map/ppermute | solution.py:90
  79.6 19.7 %collective-permute-start.21 = (bf16[128,1536]{1,0:T(8,128)(2,1)S(1)}, bf16[128,1536]{1,0:T(8,128)(2,1)S(1)}, u32[]{:S(2)}, u32[]{:S(2)}) collective-permute-start(bf16[128,1536]{1,0:T(8,128)(2,1)S(1)} %slice.318), channel_id=1, source_target_pairs={{0,16},{8,24},{16,0},{24,8},{1,17},{9,25},{17,1},{25,9},{2,18},{10... | collective-permute-start | bytes 1179656 | tf_op jit(solution)/shard_map/ppermute | solution.py:90
  81.4 18.0 %collective-permute-start.20 = (bf16[128,1536]{1,0:T(8,128)(2,1)S(1)}, bf16[128,1536]{1,0:T(8,128)(2,1)S(1)}, u32[]{:S(2)}, u32[]{:S(2)}) collective-permute-start(bf16[128,1536]{1,0:T(8,128)(2,1)S(1)} %slice.318), channel_id=1, source_target_pairs={{0,8},{8,0},{16,24},{24,16},{1,9},{9,1},{17,25},{25,17},{2,10},{10... | collective-permute-start | bytes 1179656 | tf_op jit(solution)/shard_map/ppermute | solution.py:90
  83.2 16.4 %collective-permute-start.16 = (bf16[192,1536]{1,0:T(8,128)(2,1)S(1)}, bf16[192,1536]{1,0:T(8,128)(2,1)}, u32[]{:S(2)}, u32[]{:S(2)}) collective-permute-start(bf16[192,1536]{1,0:T(8,128)(2,1)S(1)} %bitcast.360), channel_id=1, source_target_pairs={{0,4},{4,0},{1,5},{5,1},{2,6},{6,2},{3,7},{7,3},{8,12},{12,8},{9,1... | collective-permute-start | bytes 1769480 | tf_op jit(solution)/shard_map/ppermute | solution.py:87
  99.5 25.1 %collective-permute-start.23 = (bf16[512,1536]{1,0:T(8,128)(2,1)S(1)}, bf16[512,1536]{1,0:T(8,128)(2,1)S(1)}, u32[]{:S(2)}, u32[]{:S(2)}) collective-permute-start(bf16[512,1536]{1,0:T(8,128)(2,1)S(1)} %pad_maximum_fusion.4), channel_id=1, source_target_pairs={{0,4},{4,0},{1,5},{5,1},{2,6},{6,2},{3,7},{7,3},{8,12},{12,8},{9,1... | collective-permute-start | bytes 4718600 | tf_op jit(solution)/shard_map/ppermute | solution.py:87
  102.0 12.1 %collective-permute-start.17 = (bf16[128,1536]{1,0:T(8,128)(2,1)S(1)}, bf16[128,1536]{1,0:T(8,128)(2,1)S(1)}, u32[]{:S(2)}, u32[]{:S(2)}) collective-permute-start(bf16[128,1536]{1,0:T(8,128)(2,1)S(1)} %get-tuple-element.189), channel_id=1, source_target_pairs={{0,8},{8,0},{16,24},{24,16},{1,9},{9,1},{17,25},{25,17},{2,10},{10... | collective-permute-start | bytes 1179656 | tf_op jit(solution)/shard_map/ppermute | solution.py:90
  103.7 19.2 %collective-permute-start.19 = (bf16[128,1536]{1,0:T(8,128)(2,1)S(1)}, bf16[128,1536]{1,0:T(8,128)(2,1)S(1)}, u32[]{:S(2)}, u32[]{:S(2)}) collective-permute-start(bf16[128,1536]{1,0:T(8,128)(2,1)S(1)} %get-tuple-element.190), channel_id=1, source_target_pairs={{0,24},{8,16},{16,8},{24,0},{1,25},{9,17},{17,9},{25,1},{2,26},{10... | collective-permute-start | bytes 1179656 | tf_op jit(solution)/shard_map/ppermute | solution.py:90
  105.0 19.3 %collective-permute-start.18 = (bf16[128,1536]{1,0:T(8,128)(2,1)S(1)}, bf16[128,1536]{1,0:T(8,128)(2,1)S(1)}, u32[]{:S(2)}, u32[]{:S(2)}) collective-permute-start(bf16[128,1536]{1,0:T(8,128)(2,1)S(1)} %get-tuple-element.191), channel_id=1, source_target_pairs={{0,16},{8,24},{16,0},{24,8},{1,17},{9,25},{17,1},{25,9},{2,18},{10... | collective-permute-start | bytes 1179656 | tf_op jit(solution)/shard_map/ppermute | solution.py:90
  125.5 22.7 %collective-permute-start.28 = (bf16[64,1536]{1,0:T(8,128)(2,1)S(1)}, bf16[64,1536]{1,0:T(8,128)(2,1)S(1)}, u32[]{:S(2)}, u32[]{:S(2)}) collective-permute-start(bf16[64,1536]{1,0:T(8,128)(2,1)S(1)} %copy-done.26), channel_id=1, source_target_pairs={{0,3},{1,0},{2,1},{3,2},{4,7},{5,4},{6,5},{7,6},{8,11},{9,8},{10,9... | collective-permute-start | bytes 589832 | tf_op jit(solution)/shard_map/ppermute | solution.py:140
  128.7 20.7 %collective-permute-start.27 = (bf16[64,1536]{1,0:T(8,128)(2,1)S(1)}, bf16[64,1536]{1,0:T(8,128)(2,1)S(1)}, u32[]{:S(2)}, u32[]{:S(2)}) collective-permute-start(bf16[64,1536]{1,0:T(8,128)(2,1)S(1)} %copy-done.26), channel_id=1, source_target_pairs={{0,1},{1,2},{2,3},{3,0},{4,5},{5,6},{6,7},{7,4},{8,9},{9,10},{10,1... | collective-permute-start | bytes 589832 | tf_op jit(solution)/shard_map/ppermute | solution.py:140
  128.9 13.0 %collective-permute-start.26 = (bf16[128,1536]{1,0:T(8,128)(2,1)S(1)}, bf16[128,1536]{1,0:T(8,128)(2,1)S(1)}, u32[]{:S(2)}, u32[]{:S(2)}) collective-permute-start(bf16[128,1536]{1,0:T(8,128)(2,1)S(1)} %multiply_convert_fusion.3), channel_id=1, source_target_pairs={{0,24},{8,16},{16,8},{24,0},{1,25},{9,17},{17,9},{25,1},{2,26},{10... | collective-permute-start | bytes 1179656 | tf_op jit(solution)/shard_map/ppermute | solution.py:90
  130.7 17.5 %collective-permute-start.25 = (bf16[128,1536]{1,0:T(8,128)(2,1)S(1)}, bf16[128,1536]{1,0:T(8,128)(2,1)S(1)}, u32[]{:S(2)}, u32[]{:S(2)}) collective-permute-start(bf16[128,1536]{1,0:T(8,128)(2,1)S(1)} %multiply_convert_fusion.3), channel_id=1, source_target_pairs={{0,16},{8,24},{16,0},{24,8},{1,17},{9,25},{17,1},{25,9},{2,18},{10... | collective-permute-start | bytes 1179656 | tf_op jit(solution)/shard_map/ppermute | solution.py:90
  131.3 16.9 %collective-permute-start.24 = (bf16[128,1536]{1,0:T(8,128)(2,1)S(1)}, bf16[128,1536]{1,0:T(8,128)(2,1)S(1)}, u32[]{:S(2)}, u32[]{:S(2)}) collective-permute-start(bf16[128,1536]{1,0:T(8,128)(2,1)S(1)} %multiply_convert_fusion.3), channel_id=1, source_target_pairs={{0,8},{8,0},{16,24},{24,16},{1,9},{9,1},{17,25},{25,17},{2,10},{10... | collective-permute-start | bytes 1179656 | tf_op jit(solution)/shard_map/ppermute | solution.py:90
  149.4 7.0 %collective-permute-start.30 = (bf16[64,768]{1,0:T(8,128)(2,1)S(1)}, bf16[64,768]{1,0:T(8,128)(2,1)S(1)}, u32[]{:S(2)}, u32[]{:S(2)}) collective-permute-start(bf16[64,768]{1,0:T(8,128)(2,1)S(1)} %slice.339), channel_id=1, source_target_pairs={{0,1},{1,2},{2,3},{3,0},{4,5},{5,6},{6,7},{7,4},{8,9},{9,10},{10,1... | collective-permute-start | bytes 294920 | tf_op jit(solution)/shard_map/ppermute | solution.py:140
  150.3 8.0 %collective-permute-start.29 = (bf16[512,1536]{1,0:T(8,128)(2,1)S(1)}, bf16[512,1536]{1,0:T(8,128)(2,1)S(1)}, u32[]{:S(2)}, u32[]{:S(2)}) collective-permute-start(bf16[512,1536]{1,0:T(8,128)(2,1)S(1)} %pad_maximum_fusion.5), channel_id=1, source_target_pairs={{0,4},{4,0},{1,5},{5,1},{2,6},{6,2},{3,7},{7,3},{8,12},{12,8},{9,1... | collective-permute-start | bytes 4718600 | tf_op jit(solution)/shard_map/ppermute | solution.py:87
  180.2 101.0 %reduce-scatter.6.cloned.1.call-start = ((), (), s32[]{:S(2)}) async-start(), calls=%async_computation.5 | async-start | bytes 3932160 | tf_op jit(solution)/shard_map/reduce_scatter | solution.py:281
  188.7 12.3 %collective-permute-start.33 = (bf16[128,1536]{1,0:T(8,128)(2,1)S(1)}, bf16[128,1536]{1,0:T(8,128)(2,1)S(1)}, u32[]{:S(2)}, u32[]{:S(2)}) collective-permute-start(bf16[128,1536]{1,0:T(8,128)(2,1)S(1)} %get-tuple-element.186), channel_id=1, source_target_pairs={{0,8},{8,0},{16,24},{24,16},{1,9},{9,1},{17,25},{25,17},{2,10},{10... | collective-permute-start | bytes 1179656 | tf_op jit(solution)/shard_map/ppermute | solution.py:90
  189.7 18.9 %collective-permute-start.35 = (bf16[128,1536]{1,0:T(8,128)(2,1)S(1)}, bf16[128,1536]{1,0:T(8,128)(2,1)S(1)}, u32[]{:S(2)}, u32[]{:S(2)}) collective-permute-start(bf16[128,1536]{1,0:T(8,128)(2,1)S(1)} %get-tuple-element.187), channel_id=1, source_target_pairs={{0,24},{8,16},{16,8},{24,0},{1,25},{9,17},{17,9},{25,1},{2,26},{10... | collective-permute-start | bytes 1179656 | tf_op jit(solution)/shard_map/ppermute | solution.py:90
  190.9 19.0 %collective-permute-start.34 = (bf16[128,1536]{1,0:T(8,128)(2,1)S(1)}, bf16[128,1536]{1,0:T(8,128)(2,1)S(1)}, u32[]{:S(2)}, u32[]{:S(2)}) collective-permute-start(bf16[128,1536]{1,0:T(8,128)(2,1)S(1)} %get-tuple-element.188), channel_id=1, source_target_pairs={{0,16},{8,24},{16,0},{24,8},{1,17},{9,25},{17,1},{25,9},{2,18},{10... | collective-permute-start | bytes 1179656 | tf_op jit(solution)/shard_map/ppermute | solution.py:90
  201.1 30.3 %collective-permute-start.39 = (bf16[512,1536]{1,0:T(8,128)(2,1)}, bf16[512,1536]{1,0:T(8,128)(2,1)}, u32[]{:S(2)}, u32[]{:S(2)}) collective-permute-start(bf16[512,1536]{1,0:T(8,128)(2,1)} %convolution_convert_fusion.2), channel_id=1, source_target_pairs={{0,4},{4,0},{1,5},{5,1},{2,6},{6,2},{3,7},{7,3},{8,12},{12,8},{9,1... | collective-permute-start | bytes 4718600 | tf_op jit(solution)/shard_map/ppermute | solution.py:87
  210.6 13.1 %collective-permute-start.38 = (bf16[128,1536]{1,0:T(8,128)(2,1)S(1)}, bf16[128,1536]{1,0:T(8,128)(2,1)}, u32[]{:S(2)}, u32[]{:S(2)}) collective-permute-start(bf16[128,1536]{1,0:T(8,128)(2,1)S(1)} %fusion.86), channel_id=1, source_target_pairs={{0,24},{8,16},{16,8},{24,0},{1,25},{9,17},{17,9},{25,1},{2,26},{10... | collective-permute-start | bytes 1179656 | tf_op jit(solution)/shard_map/ppermute | solution.py:90
  212.4 16.6 %collective-permute-start.37 = (bf16[128,1536]{1,0:T(8,128)(2,1)S(1)}, bf16[128,1536]{1,0:T(8,128)(2,1)}, u32[]{:S(2)}, u32[]{:S(2)}) collective-permute-start(bf16[128,1536]{1,0:T(8,128)(2,1)S(1)} %fusion.86), channel_id=1, source_target_pairs={{0,16},{8,24},{16,0},{24,8},{1,17},{9,25},{17,1},{25,9},{2,18},{10... | collective-permute-start | bytes 1179656 | tf_op jit(solution)/shard_map/ppermute | solution.py:90
  213.7 15.2 %collective-permute-start.36 = (bf16[128,1536]{1,0:T(8,128)(2,1)S(1)}, bf16[128,1536]{1,0:T(8,128)(2,1)}, u32[]{:S(2)}, u32[]{:S(2)}) collective-permute-start(bf16[128,1536]{1,0:T(8,128)(2,1)S(1)} %fusion.86), channel_id=1, source_target_pairs={{0,8},{8,0},{16,24},{24,16},{1,9},{9,1},{17,25},{25,17},{2,10},{10... | collective-permute-start | bytes 1179656 | tf_op jit(solution)/shard_map/ppermute | solution.py:90
  214.2 107.9 %reduce-scatter.8.cloned.1.call-start = ((), (), s32[]{:S(2)}) async-start(), calls=%async_computation.6 | async-start | bytes 2211840 | tf_op jit(solution)/shard_map/reduce_scatter | solution.py:321
  257.7 12.3 %collective-permute-start.42 = (bf16[128,1536]{1,0:T(8,128)(2,1)}, bf16[128,1536]{1,0:T(8,128)(2,1)}, u32[]{:S(2)}, u32[]{:S(2)}) collective-permute-start(bf16[128,1536]{1,0:T(8,128)(2,1)} %get-tuple-element.183), channel_id=1, source_target_pairs={{0,8},{8,0},{16,24},{24,16},{1,9},{9,1},{17,25},{25,17},{2,10},{10... | collective-permute-start | bytes 1179656 | tf_op jit(solution)/shard_map/ppermute | solution.py:90
  259.3 19.1 %collective-permute-start.44 = (bf16[128,1536]{1,0:T(8,128)(2,1)S(1)}, bf16[128,1536]{1,0:T(8,128)(2,1)}, u32[]{:S(2)}, u32[]{:S(2)}) collective-permute-start(bf16[128,1536]{1,0:T(8,128)(2,1)S(1)} %get-tuple-element.184), channel_id=1, source_target_pairs={{0,24},{8,16},{16,8},{24,0},{1,25},{9,17},{17,9},{25,1},{2,26},{10... | collective-permute-start | bytes 1179656 | tf_op jit(solution)/shard_map/ppermute | solution.py:90
  260.6 19.0 %collective-permute-start.43 = (bf16[128,1536]{1,0:T(8,128)(2,1)S(1)}, bf16[128,1536]{1,0:T(8,128)(2,1)}, u32[]{:S(2)}, u32[]{:S(2)}) collective-permute-start(bf16[128,1536]{1,0:T(8,128)(2,1)S(1)} %get-tuple-element.185), channel_id=1, source_target_pairs={{0,16},{8,24},{16,0},{24,8},{1,17},{9,25},{17,1},{25,9},{2,18},{10... | collective-permute-start | bytes 1179656 | tf_op jit(solution)/shard_map/ppermute | solution.py:90
  283.7 12.1 %collective-permute-start.45 = (bf16[128,1536]{1,0:T(8,128)(2,1)S(1)}, bf16[128,1536]{1,0:T(8,128)(2,1)S(1)}, u32[]{:S(2)}, u32[]{:S(2)}) collective-permute-start(bf16[128,1536]{1,0:T(8,128)(2,1)S(1)} %get-tuple-element.194), channel_id=1, source_target_pairs={{0,8},{8,0},{16,24},{24,16},{1,9},{9,1},{17,25},{25,17},{2,10},{10... | collective-permute-start | bytes 1179656 | tf_op jit(solution)/shard_map/ppermute | solution.py:90
  284.7 19.6 %collective-permute-start.47 = (bf16[128,1536]{1,0:T(8,128)(2,1)S(1)}, bf16[128,1536]{1,0:T(8,128)(2,1)S(1)}, u32[]{:S(2)}, u32[]{:S(2)}) collective-permute-start(bf16[128,1536]{1,0:T(8,128)(2,1)S(1)} %get-tuple-element.195), channel_id=1, source_target_pairs={{0,24},{8,16},{16,8},{24,0},{1,25},{9,17},{17,9},{25,1},{2,26},{10... | collective-permute-start | bytes 1179656 | tf_op jit(solution)/shard_map/ppermute | solution.py:90
  285.9 20.4 %collective-permute-start.46 = (bf16[128,1536]{1,0:T(8,128)(2,1)S(1)}, bf16[128,1536]{1,0:T(8,128)(2,1)S(1)}, u32[]{:S(2)}, u32[]{:S(2)}) collective-permute-start(bf16[128,1536]{1,0:T(8,128)(2,1)S(1)} %get-tuple-element.196), channel_id=1, source_target_pairs={{0,16},{8,24},{16,0},{24,8},{1,17},{9,25},{17,1},{25,9},{2,18},{10... | collective-permute-start | bytes 1179656 | tf_op jit(solution)/shard_map/ppermute | solution.py:90
  287.7 20.7 %collective-permute-start.49 = (bf16[2,48,1024]{2,1,0:T(8,128)(2,1)S(1)}, bf16[2,48,1024]{2,1,0:T(8,128)(2,1)S(1)}, u32[]{:S(2)}, u32[]{:S(2)}) collective-permute-start(bf16[2,48,1024]{2,1,0:T(8,128)(2,1)S(1)} %get-tuple-element.216), channel_id=1, source_target_pairs={{0,8},{8,0},{16,24},{24,16},{1,9},{9,1},{17,25},{25,17},{2,10},{10... | collective-permute-start | bytes 589832 | tf_op jit(solution)/shard_map/ppermute | solution.py:90
  288.7 25.0 %collective-permute-start.50 = (bf16[2,48,1024]{2,1,0:T(8,128)(2,1)S(1)}, bf16[2,48,1024]{2,1,0:T(8,128)(2,1)S(1)}, u32[]{:S(2)}, u32[]{:S(2)}) collective-permute-start(bf16[2,48,1024]{2,1,0:T(8,128)(2,1)S(1)} %get-tuple-element.217), channel_id=1, source_target_pairs={{0,16},{8,24},{16,0},{24,8},{1,17},{9,25},{17,1},{25,9},{2,18},{10... | collective-permute-start | bytes 589832 | tf_op jit(solution)/shard_map/ppermute | solution.py:90
  295.8 17.9 %collective-permute-start.51 = (bf16[2,48,1024]{2,1,0:T(8,128)(2,1)S(1)}, bf16[2,48,1024]{2,1,0:T(8,128)(2,1)S(1)}, u32[]{:S(2)}, u32[]{:S(2)}) collective-permute-start(bf16[2,48,1024]{2,1,0:T(8,128)(2,1)S(1)} %get-tuple-element.218), channel_id=1, source_target_pairs={{0,24},{8,16},{16,8},{24,0},{1,25},{9,17},{17,9},{25,1},{2,26},{10... | collective-permute-start | bytes 589832 | tf_op jit(solution)/shard_map/ppermute | solution.py:90
  307.5 14.6 %collective-permute-start.53 = (bf16[64,1536]{1,0:T(8,128)(2,1)S(1)}, bf16[64,1536]{1,0:T(8,128)(2,1)}, u32[]{:S(2)}, u32[]{:S(2)}) collective-permute-start(bf16[64,1536]{1,0:T(8,128)(2,1)S(1)} %slice.438), channel_id=1, source_target_pairs={{0,4},{4,0},{1,5},{5,1},{2,6},{6,2},{3,7},{7,3},{8,12},{12,8},{9,1... | collective-permute-start | bytes 589832 | tf_op jit(solution)/shard_map/ppermute | solution.py:87
  (67 other events, 328.7 us)
Sparse Core Ops, SparseCore 0:
  41.9 35.7 all-gather.5
  79.8 71.2 all-gather.3
  180.3 35.9 reduce-scatter.3
  218.4 59.2 reduce-scatter.5
  279.9 38.3 reduce-scatter.7

commit v3 on v2

--- a/solution.py
+++ b/solution.py
@@ -320,12 +320,13 @@
     g_rest, d_h_one = tie(g_rest.reshape(-1, cols_qkv), d_h_one)
     g_rest = lax.psum_scatter(g_rest, "fsdp", scatter_dimension=0, tiled=True)
     d_h_one, given, g_gu = tie(scatter_chips(d_h_one), given, g_gu)
+    g_gu = g_gu.reshape(chips, 2, d_rows, 2 * ff_cols)
+    g_gu = core_pair(pick(g_gu, core, 1), core_swap(pick(g_gu, 1 - core, 1)), 1)
+    g_gu = exchange_chips(g_gu)
+    given, g_gu = tie(given, g_gu)
     result = middle + kept
     for j in range(1, chips):
         result = result + chip_xor(given[(j - 1) * own : j * own], j).astype(f32)
-    g_gu = g_gu.reshape(chips, 2, d_rows, 2 * ff_cols)
-    g_gu = core_pair(pick(g_gu, core, 1), core_swap(pick(g_gu, 1 - core, 1)), 1)
-    g_gu = exchange_chips(g_gu)
     def spread_ff(grad):
         grad = jnp.transpose(grad.astype(f32), (2, 0, 1, 3))
         return grad.reshape(d_rows, 2 * chips * ff_cols)

time: 347 us -> 351 us (1.012)
  other arithmetic: 42.4 us -> 47.4 us
  waiting for transfers between devices: 138 us -> 133 us
    ppermute x36, waiting for transfers between devices: 113 us -> 108 us  [chip_xor(): return lax.ppermute(a, 'chip', [(i, i ^ j) for i in range(chips)])]
    reshape x2, local copies, waits for them, and re-layouts: 1.35 us -> 5.41 us  [spread_ff(): return grad.reshape(d_rows, 2 * chips * ff_cols)]
    unnamed x117 -> x113, local copies, waits for them, and re-layouts: 14.8 us -> 13.2 us
  transfers between devices with their start and end apart: 62 -> 62, of which waited for: 35 -> 34; matrix products, arithmetic and copies ran while one was open for 27% -> 29% of each run, Pallas kernels for 0% -> 0%
where the time goes in v3:
time: 351 us; the launch traced here: 345 us
  waiting for transfers between devices  133 us (38%)
  starting transfers between devices  58.7 us (17%)
  matrix products  47.7 us (14%)
  other arithmetic  47.4 us (14%)
  local copies, waits for them, and re-layouts  42.9 us (12%)
  between operations  15.5 us (4%)
    ppermute x36, waiting for transfers between devices, chip_xor(): return lax.ppermute(a, 'chip', [(i, i ^ j) for i in range(chips)])  108 us
    ppermute x36, starting transfers between devices, chip_xor(): return lax.ppermute(a, 'chip', [(i, i ^ j) for i in range(chips)])  43.7 us
    ppermute x8, waiting for transfers between devices, along_z(): lax.ppermute(a, 'fsdp', [(i, (i + step) % rows_z) for i in range(rows_z)])  22 us
    dot_general x5, matrix products, mm_nt(): return jnp.einsum('te,de->td', a, b, preferred_element_type=f32)  17.3 us
    unnamed x113, local copies, waits for them, and re-layouts  13.2 us
    ppermute x8, starting transfers between devices, along_z(): lax.ppermute(a, 'fsdp', [(i, (i + step) % rows_z) for i in range(rows_z)])  13 us
    dot_general x5, matrix products, mm(): return jnp.dot(a, b, preferred_element_type=f32)  10.7 us
    dot_general x4, matrix products, mm_tn(): return jnp.einsum('td,te->de', a, b, preferred_element_type=f32)  9.18 us
  transfers between devices with their start and end apart: 62, of which 34 were waited for; matrix products, arithmetic and copies ran while one was open for 29% of the time, Pallas kernels for 0%

profile of v3, /device:TPU:0, one launch (start us, length us, event | category | flops | bytes accessed | tf_op | source)
XLA Modules:
  0.0 345.5 jit_solution(4197405420021357013)
XLA Ops:
  10.6 4.0 %collective-permute-start.3 = (bf16[48,768]{1,0:T(8,128)(2,1)S(1)}, bf16[48,768]{1,0:T(8,128)(2,1)S(1)}, u32[]{:S(2)}, u32[]{:S(2)}) collective-permute-start(bf16[48,768]{1,0:T(8,128)(2,1)S(1)} %get-tuple-element.266), channel_id=1, source_target_pairs={{0,24},{8,16},{16,8},{24,0},{1,25},{9,17},{17,9},{25,1},{2,26},{10... | collective-permute-start | bytes 221192 | tf_op jit(solution)/shard_map/ppermute | solution.py:90
  17.0 2.0 collective-permute-done.2
  25.7 3.6 %collective-permute-start.5 = (bf16[192,768]{1,0:T(8,128)(2,1)S(1)}, bf16[192,768]{1,0:T(8,128)(2,1)S(1)}, u32[]{:S(2)}, u32[]{:S(2)}) collective-permute-start(bf16[192,768]{1,0:T(8,128)(2,1)S(1)} %bitcast.375), channel_id=1, source_target_pairs={{0,3},{1,0},{2,1},{3,2},{4,7},{5,4},{6,5},{7,6},{8,11},{9,8},{10,9... | collective-permute-start | bytes 884744 | tf_op jit(solution)/shard_map/ppermute | solution.py:140
  30.3 2.1 collective-permute-done.7
  33.0 3.7 %collective-permute-done.5 = bf16[192,768]{1,0:T(8,128)(2,1)S(1)} collective-permute-done((bf16[192,768]{1,0:T(8,128)(2,1)S(1)}, bf16[192,768]{1,0:T(8,128)(2,1)S(1)}, u32[]{:S(2)}, u32[]{:S(2)}) %collective-permute-start.5) | collective-permute-done | bytes 294944 | tf_op jit(solution)/shard_map/ppermute | solution.py:140
  36.7 4.2 %collective-permute-done.4 = bf16[192,768]{1,0:T(8,128)(2,1)S(1)} collective-permute-done((bf16[192,768]{1,0:T(8,128)(2,1)S(1)}, bf16[192,768]{1,0:T(8,128)(2,1)S(1)}, u32[]{:S(2)}, u32[]{:S(2)}) %collective-permute-start.4) | collective-permute-done | bytes 294944 | tf_op jit(solution)/shard_map/ppermute | solution.py:140
  49.7 4.5 %collective-permute-done.13 = bf16[192,384]{1,0:T(8,128)(2,1)S(1)} collective-permute-done((bf16[192,384]{1,0:T(8,128)(2,1)S(1)}, bf16[192,384]{1,0:T(8,128)(2,1)S(1)}, u32[]{:S(2)}, u32[]{:S(2)}) %collective-permute-start.13) | collective-permute-done | bytes 147488 | tf_op jit(solution)/shard_map/ppermute | solution.py:140
  54.2 5.0 %collective-permute-done.12 = bf16[192,384]{1,0:T(8,128)(2,1)S(1)} collective-permute-done((bf16[192,384]{1,0:T(8,128)(2,1)S(1)}, bf16[192,384]{1,0:T(8,128)(2,1)S(1)}, u32[]{:S(2)}, u32[]{:S(2)}) %collective-permute-start.12) | collective-permute-done | bytes 147488 | tf_op jit(solution)/shard_map/ppermute | solution.py:140
  83.3 4.8 %fusion.98 = (f32[2,2,512]{2,1,0:T(2,128)S(1)}, f32[2,2,512,512]{2,3,1,0:T(8,128)}) fusion(pred[512,512]{0,1:T(8,128)(4,1)} %compare_and_fusion, bf16[512,2,2,96]{0,3,2,1:T(8,128)(2,1)S(1)} %pad_maximum_fusion.14, bf16[512,2,48]{0,2,1:T(8,128)(2,1)} %get-tuple-element.236, bf16[512,2,48]{0,2,1:T(8,128)(2,1)S(1)} %get-tuple-element.235), kind=kOutput, calls=%fused_computation.286 | convolution fusion | flops 205914624 | bytes 5054464 | tf_op jit(solution)/shard_map/sub | solution.py:238
  88.1 2.9 convolution_convert_fusion.6
  91.6 7.8 %collective-permute-done.21 = bf16[128,1536]{1,0:T(8,128)(2,1)S(1)} collective-permute-done((bf16[128,1536]{1,0:T(8,128)(2,1)S(1)}, bf16[128,1536]{1,0:T(8,128)(2,1)S(1)}, u32[]{:S(2)}, u32[]{:S(2)}) %collective-permute-start.21) | collective-permute-done | bytes 393248 | tf_op jit(solution)/shard_map/ppermute | solution.py:90
  105.7 8.4 %collective-permute-done.17 = bf16[128,1536]{1,0:T(8,128)(2,1)S(1)} collective-permute-done((bf16[128,1536]{1,0:T(8,128)(2,1)S(1)}, bf16[128,1536]{1,0:T(8,128)(2,1)S(1)}, u32[]{:S(2)}, u32[]{:S(2)}) %collective-permute-start.17) | collective-permute-done | bytes 393248 | tf_op jit(solution)/shard_map/ppermute | solution.py:90
  114.1 8.8 %collective-permute-done.19 = bf16[128,1536]{1,0:T(8,128)(2,1)S(1)} collective-permute-done((bf16[128,1536]{1,0:T(8,128)(2,1)S(1)}, bf16[128,1536]{1,0:T(8,128)(2,1)S(1)}, u32[]{:S(2)}, u32[]{:S(2)}) %collective-permute-start.19) | collective-permute-done | bytes 393248 | tf_op jit(solution)/shard_map/ppermute | solution.py:90
  125.5 3.1 collective-permute-start.28
  132.6 9.3 %collective-permute-done.26 = bf16[128,1536]{1,0:T(8,128)(2,1)S(1)} collective-permute-done((bf16[128,1536]{1,0:T(8,128)(2,1)S(1)}, bf16[128,1536]{1,0:T(8,128)(2,1)S(1)}, u32[]{:S(2)}, u32[]{:S(2)}) %collective-permute-start.26) | collective-permute-done | bytes 393248 | tf_op jit(solution)/shard_map/ppermute | solution.py:90
  141.9 6.2 %collective-permute-done.25 = bf16[128,1536]{1,0:T(8,128)(2,1)S(1)} collective-permute-done((bf16[128,1536]{1,0:T(8,128)(2,1)S(1)}, bf16[128,1536]{1,0:T(8,128)(2,1)S(1)}, u32[]{:S(2)}, u32[]{:S(2)}) %collective-permute-start.25) | collective-permute-done | bytes 393248 | tf_op jit(solution)/shard_map/ppermute | solution.py:90
  150.4 3.2 collective-permute-start.31
  153.6 2.7 collective-permute-done.30
  158.3 1.9 pad_maximum_fusion
  160.2 2.4 copy.75
  163.1 3.6 %fusion.100 = f32[1024,1024]{0,1:T(8,128)S(1)} fusion(bf16[1024,1536]{1,0:T(8,128)(2,1)S(1)} %copy-done.9, bf16[1536,1024]{1,0:T(8,128)(2,1)S(1)} %bitcast.335), kind=kOutput, calls=%fused_computation.288 | convolution fusion | flops 3221225472 | bytes 10485760 | tf_op jit(solution)/shard_map/dot_general | solution.py:46
  166.7 3.9 %multiply_convert_fusion.1 = (bf16[1024,512]{0,1:T(8,128)(2,1)}, bf16[1024,512]{0,1:T(8,128)(2,1)}, bf16[1024,512]{0,1:T(8,128)(2,1)S(1)}) fusion(f32[1024,1024]{0,1:T(8,128)S(1)} %fusion.100, bf16[1024,1536]{1,0:T(8,128)(2,1)S(1)} %copy-done.46, bf16[512,1536]{1,0:T(8,128)(2,1)S(1)} %bitcast.328), kind=kOutput, calls=%fused_computation.26 | convolution fusion | flops 1619001344 | bytes 12058624 | tf_op jit(solution)/shard_map/te,de->td/dot_general | solution.py:54
  171.6 3.0 convolution_convert_fusion.4
  177.1 3.1 convolution_convert_fusion.3
  180.7 3.2 collective-permute-done.32
  183.9 4.5 %convert_add_fusion.1 = f32[512,1536]{1,0:T(8,128)S(1)} fusion(bf16[512,1536]{1,0:T(8,128)(2,1)} %collective-permute-done.32, bf16[1536,1024]{1,0:T(8,128)(2,1)} %bitcast.336, bf16[1024,1024]{0,1:T(8,128)(2,1)} %copy-done.17), kind=kOutput, calls=%fused_computation.17 | convolution fusion | flops 1612185600 | bytes 8912896 | tf_op jit(solution)/shard_map/te,de->td/dot_general | solution.py:54
  192.3 3.8 %convolution_convert_fusion = bf16[1536,1024]{1,0:T(8,128)(2,1)S(1)} fusion(bf16[1024,1536]{1,0:T(8,128)(2,1)S(1)} %copy-done.10, bf16[1024,1024]{0,1:T(8,128)(2,1)S(1)} %copy-done.18), kind=kOutput, calls=%fused_computation.10 | convolution fusion | flops 3222798336 | bytes 8388608 | tf_op jit(solution)/shard_map/td,te->de/dot_general | solution.py:50
  196.1 2.0 copy.76
  198.8 2.3 convolution_convert_fusion.2
  201.1 7.5 %collective-permute-done.35 = bf16[128,1536]{1,0:T(8,128)(2,1)S(1)} collective-permute-done((bf16[128,1536]{1,0:T(8,128)(2,1)S(1)}, bf16[128,1536]{1,0:T(8,128)(2,1)S(1)}, u32[]{:S(2)}, u32[]{:S(2)}) %collective-permute-start.35) | collective-permute-done | bytes 393248 | tf_op jit(solution)/shard_map/ppermute | solution.py:90
  214.4 9.2 %collective-permute-done.38 = bf16[128,1536]{1,0:T(8,128)(2,1)} collective-permute-done((bf16[128,1536]{1,0:T(8,128)(2,1)S(1)}, bf16[128,1536]{1,0:T(8,128)(2,1)}, u32[]{:S(2)}, u32[]{:S(2)}) %collective-permute-start.38) | collective-permute-done | bytes 393248 | tf_op jit(solution)/shard_map/ppermute | solution.py:90
  223.6 5.3 %collective-permute-done.37 = bf16[128,1536]{1,0:T(8,128)(2,1)} collective-permute-done((bf16[128,1536]{1,0:T(8,128)(2,1)S(1)}, bf16[128,1536]{1,0:T(8,128)(2,1)}, u32[]{:S(2)}, u32[]{:S(2)}) %collective-permute-start.37) | collective-permute-done | bytes 393248 | tf_op jit(solution)/shard_map/ppermute | solution.py:90
  229.0 2.5 pad_maximum_fusion.7
  231.5 2.4 convert_add_fusion
  236.0 2.7 convolution_convert_fusion.7
  250.2 3.1 fusion.101
  254.8 2.1 convert.86
  260.5 8.5 %collective-permute-done.42 = bf16[128,1536]{1,0:T(8,128)(2,1)S(1)} collective-permute-done((bf16[128,1536]{1,0:T(8,128)(2,1)S(1)}, bf16[128,1536]{1,0:T(8,128)(2,1)S(1)}, u32[]{:S(2)}, u32[]{:S(2)}) %collective-permute-start.42) | collective-permute-done | bytes 393248 | tf_op jit(solution)/shard_map/ppermute | solution.py:90
  269.0 8.4 %collective-permute-done.44 = bf16[128,1536]{1,0:T(8,128)(2,1)S(1)} collective-permute-done((bf16[128,1536]{1,0:T(8,128)(2,1)S(1)}, bf16[128,1536]{1,0:T(8,128)(2,1)S(1)}, u32[]{:S(2)}, u32[]{:S(2)}) %collective-permute-start.44) | collective-permute-done | bytes 393248 | tf_op jit(solution)/shard_map/ppermute | solution.py:90
  281.9 2.0 convert_element_type.272
  288.9 4.3 %collective-permute-done.46 = bf16[2,48,1024]{2,1,0:T(8,128)(2,1)S(1)} collective-permute-done((bf16[2,48,1024]{2,1,0:T(8,128)(2,1)S(1)}, bf16[2,48,1024]{2,1,0:T(8,128)(2,1)S(1)}, u32[]{:S(2)}, u32[]{:S(2)}) %collective-permute-start.46) | collective-permute-done | bytes 196640 | tf_op jit(solution)/shard_map/ppermute | solution.py:90
  293.2 4.4 %collective-permute-done.47 = bf16[2,48,1024]{2,1,0:T(8,128)(2,1)S(1)} collective-permute-done((bf16[2,48,1024]{2,1,0:T(8,128)(2,1)S(1)}, bf16[2,48,1024]{2,1,0:T(8,128)(2,1)S(1)}, u32[]{:S(2)}, u32[]{:S(2)}) %collective-permute-start.47) | collective-permute-done | bytes 196640 | tf_op jit(solution)/shard_map/ppermute | solution.py:90
  304.4 2.0 convert_bitcast_fusion
  306.4 2.7 reshape.482
  309.1 2.7 reshape.480
  311.8 2.4 fusion.32
  314.3 5.4 %collective-permute-done.51 = bf16[128,1536]{1,0:T(8,128)(2,1)} collective-permute-done((bf16[128,1536]{1,0:T(8,128)(2,1)}, bf16[128,1536]{1,0:T(8,128)(2,1)}, u32[]{:S(2)}, u32[]{:S(2)}) %collective-permute-start.51) | collective-permute-done | bytes 393248 | tf_op jit(solution)/shard_map/ppermute | solution.py:90
  321.1 2.4 fusion.28
  (378 shorter events, 129.9 us)
Async XLA Ops:
  7.2 71.3 %all-gather.6.cloned.1.call-start = ((), (), s32[]{:S(2)}) async-start(), calls=%async_computation.7 | async-start | bytes 1720320 | tf_op jit(solution)/shard_map/all_gather | solution.py:198
  21.5 8.8 %collective-permute-start.8 = (bf16[2,48,1024]{2,1,0:T(8,128)(2,1)}, bf16[2,48,1024]{2,1,0:T(8,128)(2,1)S(1)}, u32[]{:S(2)}, u32[]{:S(2)}) collective-permute-start(bf16[2,48,1024]{2,1,0:T(8,128)(2,1)} %get-tuple-element.224), channel_id=1, source_target_pairs={{0,24},{8,16},{16,8},{24,0},{1,25},{9,17},{17,9},{25,1},{2,26},{10... | collective-permute-start | bytes 589832 | tf_op jit(solution)/shard_map/ppermute | solution.py:90
  23.0 9.4 %collective-permute-start.7 = (bf16[2,48,1024]{2,1,0:T(8,128)(2,1)S(1)}, bf16[2,48,1024]{2,1,0:T(8,128)(2,1)S(1)}, u32[]{:S(2)}, u32[]{:S(2)}) collective-permute-start(bf16[2,48,1024]{2,1,0:T(8,128)(2,1)S(1)} %get-tuple-element.225), channel_id=1, source_target_pairs={{0,16},{8,24},{16,0},{24,8},{1,17},{9,25},{17,1},{25,9},{2,18},{10... | collective-permute-start | bytes 589832 | tf_op jit(solution)/shard_map/ppermute | solution.py:90
  23.7 8.8 %collective-permute-start.6 = (bf16[2,48,1024]{2,1,0:T(8,128)(2,1)S(1)}, bf16[2,48,1024]{2,1,0:T(8,128)(2,1)S(1)}, u32[]{:S(2)}, u32[]{:S(2)}) collective-permute-start(bf16[2,48,1024]{2,1,0:T(8,128)(2,1)S(1)} %get-tuple-element.226), channel_id=1, source_target_pairs={{0,8},{8,0},{16,24},{24,16},{1,9},{9,1},{17,25},{25,17},{2,10},{10... | collective-permute-start | bytes 589832 | tf_op jit(solution)/shard_map/ppermute | solution.py:90
  25.7 11.0 %collective-permute-start.5 = (bf16[192,768]{1,0:T(8,128)(2,1)S(1)}, bf16[192,768]{1,0:T(8,128)(2,1)S(1)}, u32[]{:S(2)}, u32[]{:S(2)}) collective-permute-start(bf16[192,768]{1,0:T(8,128)(2,1)S(1)} %bitcast.375), channel_id=1, source_target_pairs={{0,3},{1,0},{2,1},{3,2},{4,7},{5,4},{6,5},{7,6},{8,11},{9,8},{10,9... | collective-permute-start | bytes 884744 | tf_op jit(solution)/shard_map/ppermute | solution.py:140
  29.3 11.6 %collective-permute-start.4 = (bf16[192,768]{1,0:T(8,128)(2,1)S(1)}, bf16[192,768]{1,0:T(8,128)(2,1)S(1)}, u32[]{:S(2)}, u32[]{:S(2)}) collective-permute-start(bf16[192,768]{1,0:T(8,128)(2,1)S(1)} %bitcast.376), channel_id=1, source_target_pairs={{0,1},{1,2},{2,3},{3,0},{4,5},{5,6},{6,7},{7,4},{8,9},{9,10},{10,1... | collective-permute-start | bytes 884744 | tf_op jit(solution)/shard_map/ppermute | solution.py:140
  41.7 118.5 %all-gather.4.cloned.1.call-start = ((), (), s32[]{:S(2)}) async-start(), calls=%async_computation.3 | async-start | bytes 3932160 | tf_op jit(solution)/shard_map/all_gather | solution.py:248
  41.8 17.4 %collective-permute-start.11 = (bf16[128,1664]{1,0:T(8,128)(2,1)S(1)}, bf16[128,1664]{1,0:T(8,128)(2,1)}, u32[]{:S(2)}, u32[]{:S(2)}) collective-permute-start(bf16[128,1664]{1,0:T(8,128)(2,1)S(1)} %slice.312), channel_id=1, source_target_pairs={{0,16},{8,24},{16,0},{24,8},{1,17},{9,25},{17,1},{25,9},{2,18},{10... | collective-permute-start | bytes 1277960 | tf_op jit(solution)/shard_map/ppermute | solution.py:90
  43.3 15.9 %collective-permute-start.10 = (bf16[128,1664]{1,0:T(8,128)(2,1)S(1)}, bf16[128,1664]{1,0:T(8,128)(2,1)}, u32[]{:S(2)}, u32[]{:S(2)}) collective-permute-start(bf16[128,1664]{1,0:T(8,128)(2,1)S(1)} %slice.312), channel_id=1, source_target_pairs={{0,8},{8,0},{16,24},{24,16},{1,9},{9,1},{17,25},{25,17},{2,10},{10... | collective-permute-start | bytes 1277960 | tf_op jit(solution)/shard_map/ppermute | solution.py:90
  44.3 22.4 %collective-permute-start.15 = (bf16[128,1664]{1,0:T(8,128)(2,1)S(1)}, bf16[128,1664]{1,0:T(8,128)(2,1)}, u32[]{:S(2)}, u32[]{:S(2)}) collective-permute-start(bf16[128,1664]{1,0:T(8,128)(2,1)S(1)} %slice.312), channel_id=1, source_target_pairs={{0,24},{8,16},{16,8},{24,0},{1,25},{9,17},{17,9},{25,1},{2,26},{10... | collective-permute-start | bytes 1277960 | tf_op jit(solution)/shard_map/ppermute | solution.py:90
  45.5 8.7 %collective-permute-start.13 = (bf16[192,384]{1,0:T(8,128)(2,1)S(1)}, bf16[192,384]{1,0:T(8,128)(2,1)S(1)}, u32[]{:S(2)}, u32[]{:S(2)}) collective-permute-start(bf16[192,384]{1,0:T(8,128)(2,1)S(1)} %slice.316), channel_id=1, source_target_pairs={{0,3},{1,0},{2,1},{3,2},{4,7},{5,4},{6,5},{7,6},{8,11},{9,8},{10,9... | collective-permute-start | bytes 442376 | tf_op jit(solution)/shard_map/ppermute | solution.py:140
  47.3 11.9 %collective-permute-start.12 = (bf16[192,384]{1,0:T(8,128)(2,1)S(1)}, bf16[192,384]{1,0:T(8,128)(2,1)S(1)}, u32[]{:S(2)}, u32[]{:S(2)}) collective-permute-start(bf16[192,384]{1,0:T(8,128)(2,1)S(1)} %slice.315), channel_id=1, source_target_pairs={{0,1},{1,2},{2,3},{3,0},{4,5},{5,6},{6,7},{7,4},{8,9},{9,10},{10,1... | collective-permute-start | bytes 442376 | tf_op jit(solution)/shard_map/ppermute | solution.py:140
  64.6 7.7 %collective-permute-start.14 = (bf16[4,4,48,768]{3,2,1,0:T(8,128)(2,1)}, bf16[4,4,48,768]{3,2,1,0:T(8,128)(2,1)}, u32[]{:S(2)}, u32[]{:S(2)}) collective-permute-start(bf16[4,4,48,768]{3,2,1,0:T(8,128)(2,1)} %constant_dynamic-update-slice_fusion.9), channel_id=1, source_target_pairs={{0,4},{4,0},{1,5},{5,1},{2,6},{6,2},{3,7},{7,3},{8,12},{12,8},{9,1... | collective-permute-start | bytes 3538952 | tf_op jit(solution)/shard_map/ppermute | solution.py:87
  69.1 166.9 %reduce-scatter.4.cloned.1.call-start = ((), (), s32[]{:S(2)}) async-start(), calls=%async_computation.4 | async-start | bytes 1966080 | tf_op jit(solution)/shard_map/reduce_scatter | solution.py:271
  78.6 13.0 %collective-permute-start.22 = (bf16[128,1536]{1,0:T(8,128)(2,1)S(1)}, bf16[128,1536]{1,0:T(8,128)(2,1)S(1)}, u32[]{:S(2)}, u32[]{:S(2)}) collective-permute-start(bf16[128,1536]{1,0:T(8,128)(2,1)S(1)} %slice.318), channel_id=1, source_target_pairs={{0,24},{8,16},{16,8},{24,0},{1,25},{9,17},{17,9},{25,1},{2,26},{10... | collective-permute-start | bytes 1179656 | tf_op jit(solution)/shard_map/ppermute | solution.py:90
  79.6 19.8 %collective-permute-start.21 = (bf16[128,1536]{1,0:T(8,128)(2,1)S(1)}, bf16[128,1536]{1,0:T(8,128)(2,1)S(1)}, u32[]{:S(2)}, u32[]{:S(2)}) collective-permute-start(bf16[128,1536]{1,0:T(8,128)(2,1)S(1)} %slice.318), channel_id=1, source_target_pairs={{0,16},{8,24},{16,0},{24,8},{1,17},{9,25},{17,1},{25,9},{2,18},{10... | collective-permute-start | bytes 1179656 | tf_op jit(solution)/shard_map/ppermute | solution.py:90
  81.4 18.0 %collective-permute-start.20 = (bf16[128,1536]{1,0:T(8,128)(2,1)S(1)}, bf16[128,1536]{1,0:T(8,128)(2,1)S(1)}, u32[]{:S(2)}, u32[]{:S(2)}) collective-permute-start(bf16[128,1536]{1,0:T(8,128)(2,1)S(1)} %slice.318), channel_id=1, source_target_pairs={{0,8},{8,0},{16,24},{24,16},{1,9},{9,1},{17,25},{25,17},{2,10},{10... | collective-permute-start | bytes 1179656 | tf_op jit(solution)/shard_map/ppermute | solution.py:90
  83.2 16.4 %collective-permute-start.16 = (bf16[192,1536]{1,0:T(8,128)(2,1)S(1)}, bf16[192,1536]{1,0:T(8,128)(2,1)}, u32[]{:S(2)}, u32[]{:S(2)}) collective-permute-start(bf16[192,1536]{1,0:T(8,128)(2,1)S(1)} %bitcast.356), channel_id=1, source_target_pairs={{0,4},{4,0},{1,5},{5,1},{2,6},{6,2},{3,7},{7,3},{8,12},{12,8},{9,1... | collective-permute-start | bytes 1769480 | tf_op jit(solution)/shard_map/ppermute | solution.py:87
  99.5 25.1 %collective-permute-start.23 = (bf16[512,1536]{1,0:T(8,128)(2,1)S(1)}, bf16[512,1536]{1,0:T(8,128)(2,1)S(1)}, u32[]{:S(2)}, u32[]{:S(2)}) collective-permute-start(bf16[512,1536]{1,0:T(8,128)(2,1)S(1)} %pad_maximum_fusion.4), channel_id=1, source_target_pairs={{0,4},{4,0},{1,5},{5,1},{2,6},{6,2},{3,7},{7,3},{8,12},{12,8},{9,1... | collective-permute-start | bytes 4718600 | tf_op jit(solution)/shard_map/ppermute | solution.py:87
  102.0 12.1 %collective-permute-start.17 = (bf16[128,1536]{1,0:T(8,128)(2,1)S(1)}, bf16[128,1536]{1,0:T(8,128)(2,1)S(1)}, u32[]{:S(2)}, u32[]{:S(2)}) collective-permute-start(bf16[128,1536]{1,0:T(8,128)(2,1)S(1)} %get-tuple-element.193), channel_id=1, source_target_pairs={{0,8},{8,0},{16,24},{24,16},{1,9},{9,1},{17,25},{25,17},{2,10},{10... | collective-permute-start | bytes 1179656 | tf_op jit(solution)/shard_map/ppermute | solution.py:90
  103.7 19.2 %collective-permute-start.19 = (bf16[128,1536]{1,0:T(8,128)(2,1)S(1)}, bf16[128,1536]{1,0:T(8,128)(2,1)S(1)}, u32[]{:S(2)}, u32[]{:S(2)}) collective-permute-start(bf16[128,1536]{1,0:T(8,128)(2,1)S(1)} %get-tuple-element.194), channel_id=1, source_target_pairs={{0,24},{8,16},{16,8},{24,0},{1,25},{9,17},{17,9},{25,1},{2,26},{10... | collective-permute-start | bytes 1179656 | tf_op jit(solution)/shard_map/ppermute | solution.py:90
  105.0 19.2 %collective-permute-start.18 = (bf16[128,1536]{1,0:T(8,128)(2,1)S(1)}, bf16[128,1536]{1,0:T(8,128)(2,1)S(1)}, u32[]{:S(2)}, u32[]{:S(2)}) collective-permute-start(bf16[128,1536]{1,0:T(8,128)(2,1)S(1)} %get-tuple-element.195), channel_id=1, source_target_pairs={{0,16},{8,24},{16,0},{24,8},{1,17},{9,25},{17,1},{25,9},{2,18},{10... | collective-permute-start | bytes 1179656 | tf_op jit(solution)/shard_map/ppermute | solution.py:90
  125.5 22.7 %collective-permute-start.28 = (bf16[64,1536]{1,0:T(8,128)(2,1)S(1)}, bf16[64,1536]{1,0:T(8,128)(2,1)S(1)}, u32[]{:S(2)}, u32[]{:S(2)}) collective-permute-start(bf16[64,1536]{1,0:T(8,128)(2,1)S(1)} %copy-done.26), channel_id=1, source_target_pairs={{0,3},{1,0},{2,1},{3,2},{4,7},{5,4},{6,5},{7,6},{8,11},{9,8},{10,9... | collective-permute-start | bytes 589832 | tf_op jit(solution)/shard_map/ppermute | solution.py:140
  128.6 20.7 %collective-permute-start.27 = (bf16[64,1536]{1,0:T(8,128)(2,1)S(1)}, bf16[64,1536]{1,0:T(8,128)(2,1)S(1)}, u32[]{:S(2)}, u32[]{:S(2)}) collective-permute-start(bf16[64,1536]{1,0:T(8,128)(2,1)S(1)} %copy-done.26), channel_id=1, source_target_pairs={{0,1},{1,2},{2,3},{3,0},{4,5},{5,6},{6,7},{7,4},{8,9},{9,10},{10,1... | collective-permute-start | bytes 589832 | tf_op jit(solution)/shard_map/ppermute | solution.py:140
  128.9 13.0 %collective-permute-start.26 = (bf16[128,1536]{1,0:T(8,128)(2,1)S(1)}, bf16[128,1536]{1,0:T(8,128)(2,1)S(1)}, u32[]{:S(2)}, u32[]{:S(2)}) collective-permute-start(bf16[128,1536]{1,0:T(8,128)(2,1)S(1)} %multiply_convert_fusion.3), channel_id=1, source_target_pairs={{0,24},{8,16},{16,8},{24,0},{1,25},{9,17},{17,9},{25,1},{2,26},{10... | collective-permute-start | bytes 1179656 | tf_op jit(solution)/shard_map/ppermute | solution.py:90
  130.7 17.4 %collective-permute-start.25 = (bf16[128,1536]{1,0:T(8,128)(2,1)S(1)}, bf16[128,1536]{1,0:T(8,128)(2,1)S(1)}, u32[]{:S(2)}, u32[]{:S(2)}) collective-permute-start(bf16[128,1536]{1,0:T(8,128)(2,1)S(1)} %multiply_convert_fusion.3), channel_id=1, source_target_pairs={{0,16},{8,24},{16,0},{24,8},{1,17},{9,25},{17,1},{25,9},{2,18},{10... | collective-permute-start | bytes 1179656 | tf_op jit(solution)/shard_map/ppermute | solution.py:90
  131.3 16.8 %collective-permute-start.24 = (bf16[128,1536]{1,0:T(8,128)(2,1)S(1)}, bf16[128,1536]{1,0:T(8,128)(2,1)S(1)}, u32[]{:S(2)}, u32[]{:S(2)}) collective-permute-start(bf16[128,1536]{1,0:T(8,128)(2,1)S(1)} %multiply_convert_fusion.3), channel_id=1, source_target_pairs={{0,8},{8,0},{16,24},{24,16},{1,9},{9,1},{17,25},{25,17},{2,10},{10... | collective-permute-start | bytes 1179656 | tf_op jit(solution)/shard_map/ppermute | solution.py:90
  149.4 7.0 %collective-permute-start.30 = (bf16[64,768]{1,0:T(8,128)(2,1)S(1)}, bf16[64,768]{1,0:T(8,128)(2,1)S(1)}, u32[]{:S(2)}, u32[]{:S(2)}) collective-permute-start(bf16[64,768]{1,0:T(8,128)(2,1)S(1)} %slice.339), channel_id=1, source_target_pairs={{0,1},{1,2},{2,3},{3,0},{4,5},{5,6},{6,7},{7,4},{8,9},{9,10},{10,1... | collective-permute-start | bytes 294920 | tf_op jit(solution)/shard_map/ppermute | solution.py:140
  150.3 8.0 %collective-permute-start.29 = (bf16[512,1536]{1,0:T(8,128)(2,1)S(1)}, bf16[512,1536]{1,0:T(8,128)(2,1)S(1)}, u32[]{:S(2)}, u32[]{:S(2)}) collective-permute-start(bf16[512,1536]{1,0:T(8,128)(2,1)S(1)} %pad_maximum_fusion.5), channel_id=1, source_target_pairs={{0,4},{4,0},{1,5},{5,1},{2,6},{6,2},{3,7},{7,3},{8,12},{12,8},{9,1... | collective-permute-start | bytes 4718600 | tf_op jit(solution)/shard_map/ppermute | solution.py:87
  150.4 6.7 %collective-permute-start.31 = (bf16[64,768]{1,0:T(8,128)(2,1)S(1)}, bf16[64,768]{1,0:T(8,128)(2,1)S(1)}, u32[]{:S(2)}, u32[]{:S(2)}) collective-permute-start(bf16[64,768]{1,0:T(8,128)(2,1)S(1)} %slice.340), channel_id=1, source_target_pairs={{0,3},{1,0},{2,1},{3,2},{4,7},{5,4},{6,5},{7,6},{8,11},{9,8},{10,9... | collective-permute-start | bytes 294920 | tf_op jit(solution)/shard_map/ppermute | solution.py:140
  180.2 99.8 %reduce-scatter.6.cloned.1.call-start = ((), (), s32[]{:S(2)}) async-start(), calls=%async_computation.5 | async-start | bytes 3932160 | tf_op jit(solution)/shard_map/reduce_scatter | solution.py:281
  188.8 12.4 %collective-permute-start.33 = (bf16[128,1536]{1,0:T(8,128)(2,1)S(1)}, bf16[128,1536]{1,0:T(8,128)(2,1)S(1)}, u32[]{:S(2)}, u32[]{:S(2)}) collective-permute-start(bf16[128,1536]{1,0:T(8,128)(2,1)S(1)} %get-tuple-element.190), channel_id=1, source_target_pairs={{0,8},{8,0},{16,24},{24,16},{1,9},{9,1},{17,25},{25,17},{2,10},{10... | collective-permute-start | bytes 1179656 | tf_op jit(solution)/shard_map/ppermute | solution.py:90
  189.7 18.9 %collective-permute-start.35 = (bf16[128,1536]{1,0:T(8,128)(2,1)S(1)}, bf16[128,1536]{1,0:T(8,128)(2,1)S(1)}, u32[]{:S(2)}, u32[]{:S(2)}) collective-permute-start(bf16[128,1536]{1,0:T(8,128)(2,1)S(1)} %get-tuple-element.191), channel_id=1, source_target_pairs={{0,24},{8,16},{16,8},{24,0},{1,25},{9,17},{17,9},{25,1},{2,26},{10... | collective-permute-start | bytes 1179656 | tf_op jit(solution)/shard_map/ppermute | solution.py:90
  190.9 19.0 %collective-permute-start.34 = (bf16[128,1536]{1,0:T(8,128)(2,1)S(1)}, bf16[128,1536]{1,0:T(8,128)(2,1)S(1)}, u32[]{:S(2)}, u32[]{:S(2)}) collective-permute-start(bf16[128,1536]{1,0:T(8,128)(2,1)S(1)} %get-tuple-element.192), channel_id=1, source_target_pairs={{0,16},{8,24},{16,0},{24,8},{1,17},{9,25},{17,1},{25,9},{2,18},{10... | collective-permute-start | bytes 1179656 | tf_op jit(solution)/shard_map/ppermute | solution.py:90
  201.1 30.3 %collective-permute-start.39 = (bf16[512,1536]{1,0:T(8,128)(2,1)}, bf16[512,1536]{1,0:T(8,128)(2,1)}, u32[]{:S(2)}, u32[]{:S(2)}) collective-permute-start(bf16[512,1536]{1,0:T(8,128)(2,1)} %convolution_convert_fusion.2), channel_id=1, source_target_pairs={{0,4},{4,0},{1,5},{5,1},{2,6},{6,2},{3,7},{7,3},{8,12},{12,8},{9,1... | collective-permute-start | bytes 4718600 | tf_op jit(solution)/shard_map/ppermute | solution.py:87
  210.6 13.1 %collective-permute-start.38 = (bf16[128,1536]{1,0:T(8,128)(2,1)S(1)}, bf16[128,1536]{1,0:T(8,128)(2,1)}, u32[]{:S(2)}, u32[]{:S(2)}) collective-permute-start(bf16[128,1536]{1,0:T(8,128)(2,1)S(1)} %fusion.86), channel_id=1, source_target_pairs={{0,24},{8,16},{16,8},{24,0},{1,25},{9,17},{17,9},{25,1},{2,26},{10... | collective-permute-start | bytes 1179656 | tf_op jit(solution)/shard_map/ppermute | solution.py:90
  212.4 16.6 %collective-permute-start.37 = (bf16[128,1536]{1,0:T(8,128)(2,1)S(1)}, bf16[128,1536]{1,0:T(8,128)(2,1)}, u32[]{:S(2)}, u32[]{:S(2)}) collective-permute-start(bf16[128,1536]{1,0:T(8,128)(2,1)S(1)} %fusion.86), channel_id=1, source_target_pairs={{0,16},{8,24},{16,0},{24,8},{1,17},{9,25},{17,1},{25,9},{2,18},{10... | collective-permute-start | bytes 1179656 | tf_op jit(solution)/shard_map/ppermute | solution.py:90
  213.7 15.2 %collective-permute-start.36 = (bf16[128,1536]{1,0:T(8,128)(2,1)S(1)}, bf16[128,1536]{1,0:T(8,128)(2,1)}, u32[]{:S(2)}, u32[]{:S(2)}) collective-permute-start(bf16[128,1536]{1,0:T(8,128)(2,1)S(1)} %fusion.86), channel_id=1, source_target_pairs={{0,8},{8,0},{16,24},{24,16},{1,9},{9,1},{17,25},{25,17},{2,10},{10... | collective-permute-start | bytes 1179656 | tf_op jit(solution)/shard_map/ppermute | solution.py:90
  214.2 111.1 %reduce-scatter.8.cloned.1.call-start = ((), (), s32[]{:S(2)}) async-start(), calls=%async_computation.6 | async-start | bytes 2211840 | tf_op jit(solution)/shard_map/reduce_scatter | solution.py:321
  257.0 12.1 %collective-permute-start.42 = (bf16[128,1536]{1,0:T(8,128)(2,1)S(1)}, bf16[128,1536]{1,0:T(8,128)(2,1)S(1)}, u32[]{:S(2)}, u32[]{:S(2)}) collective-permute-start(bf16[128,1536]{1,0:T(8,128)(2,1)S(1)} %get-tuple-element.187), channel_id=1, source_target_pairs={{0,8},{8,0},{16,24},{24,16},{1,9},{9,1},{17,25},{25,17},{2,10},{10... | collective-permute-start | bytes 1179656 | tf_op jit(solution)/shard_map/ppermute | solution.py:90
  258.7 18.7 %collective-permute-start.44 = (bf16[128,1536]{1,0:T(8,128)(2,1)S(1)}, bf16[128,1536]{1,0:T(8,128)(2,1)S(1)}, u32[]{:S(2)}, u32[]{:S(2)}) collective-permute-start(bf16[128,1536]{1,0:T(8,128)(2,1)S(1)} %get-tuple-element.188), channel_id=1, source_target_pairs={{0,24},{8,16},{16,8},{24,0},{1,25},{9,17},{17,9},{25,1},{2,26},{10... | collective-permute-start | bytes 1179656 | tf_op jit(solution)/shard_map/ppermute | solution.py:90
  259.9 18.9 %collective-permute-start.43 = (bf16[128,1536]{1,0:T(8,128)(2,1)S(1)}, bf16[128,1536]{1,0:T(8,128)(2,1)S(1)}, u32[]{:S(2)}, u32[]{:S(2)}) collective-permute-start(bf16[128,1536]{1,0:T(8,128)(2,1)S(1)} %get-tuple-element.189), channel_id=1, source_target_pairs={{0,16},{8,24},{16,0},{24,8},{1,17},{9,25},{17,1},{25,9},{2,18},{10... | collective-permute-start | bytes 1179656 | tf_op jit(solution)/shard_map/ppermute | solution.py:90
  285.3 7.8 %collective-permute-start.46 = (bf16[2,48,1024]{2,1,0:T(8,128)(2,1)S(1)}, bf16[2,48,1024]{2,1,0:T(8,128)(2,1)S(1)}, u32[]{:S(2)}, u32[]{:S(2)}) collective-permute-start(bf16[2,48,1024]{2,1,0:T(8,128)(2,1)S(1)} %get-tuple-element.220), channel_id=1, source_target_pairs={{0,8},{8,0},{16,24},{24,16},{1,9},{9,1},{17,25},{25,17},{2,10},{10... | collective-permute-start | bytes 589832 | tf_op jit(solution)/shard_map/ppermute | solution.py:90
  286.3 11.2 %collective-permute-start.47 = (bf16[2,48,1024]{2,1,0:T(8,128)(2,1)S(1)}, bf16[2,48,1024]{2,1,0:T(8,128)(2,1)S(1)}, u32[]{:S(2)}, u32[]{:S(2)}) collective-permute-start(bf16[2,48,1024]{2,1,0:T(8,128)(2,1)S(1)} %get-tuple-element.221), channel_id=1, source_target_pairs={{0,16},{8,24},{16,0},{24,8},{1,17},{9,25},{17,1},{25,9},{2,18},{10... | collective-permute-start | bytes 589832 | tf_op jit(solution)/shard_map/ppermute | solution.py:90
  287.6 9.9 %collective-permute-start.48 = (bf16[2,48,1024]{2,1,0:T(8,128)(2,1)S(1)}, bf16[2,48,1024]{2,1,0:T(8,128)(2,1)S(1)}, u32[]{:S(2)}, u32[]{:S(2)}) collective-permute-start(bf16[2,48,1024]{2,1,0:T(8,128)(2,1)S(1)} %get-tuple-element.222), channel_id=1, source_target_pairs={{0,24},{8,16},{16,8},{24,0},{1,25},{9,17},{17,9},{25,1},{2,26},{10... | collective-permute-start | bytes 589832 | tf_op jit(solution)/shard_map/ppermute | solution.py:90
  299.9 14.4 %collective-permute-start.49 = (bf16[128,1536]{1,0:T(8,128)(2,1)}, bf16[128,1536]{1,0:T(8,128)(2,1)}, u32[]{:S(2)}, u32[]{:S(2)}) collective-permute-start(bf16[128,1536]{1,0:T(8,128)(2,1)} %get-tuple-element.196), channel_id=1, source_target_pairs={{0,8},{8,0},{16,24},{24,16},{1,9},{9,1},{17,25},{25,17},{2,10},{10... | collective-permute-start | bytes 1179656 | tf_op jit(solution)/shard_map/ppermute | solution.py:90
  301.0 18.7 %collective-permute-start.51 = (bf16[128,1536]{1,0:T(8,128)(2,1)}, bf16[128,1536]{1,0:T(8,128)(2,1)}, u32[]{:S(2)}, u32[]{:S(2)}) collective-permute-start(bf16[128,1536]{1,0:T(8,128)(2,1)} %get-tuple-element.197), channel_id=1, source_target_pairs={{0,24},{8,16},{16,8},{24,0},{1,25},{9,17},{17,9},{25,1},{2,26},{10... | collective-permute-start | bytes 1179656 | tf_op jit(solution)/shard_map/ppermute | solution.py:90
  302.7 18.4 %collective-permute-start.50 = (bf16[128,1536]{1,0:T(8,128)(2,1)}, bf16[128,1536]{1,0:T(8,128)(2,1)}, u32[]{:S(2)}, u32[]{:S(2)}) collective-permute-start(bf16[128,1536]{1,0:T(8,128)(2,1)} %get-tuple-element.198), channel_id=1, source_target_pairs={{0,16},{8,24},{16,0},{24,8},{1,17},{9,25},{17,1},{25,9},{2,18},{10... | collective-permute-start | bytes 1179656 | tf_op jit(solution)/shard_map/ppermute | solution.py:90
  (66 other events, 306.9 us)
Sparse Core Ops, SparseCore 0:
  41.9 35.7 all-gather.5
  79.8 71.2 all-gather.3
  180.3 35.9 reduce-scatter.3
  218.5 59.2 reduce-scatter.5
  282.0 38.9 reduce-scatter.7
